TPU v7x, 32 devices: a whole 2x2x4 slice. The times are simulated.
32 devices in a mesh: groups: 2 (over y), cubes: 16 (over z, x, core).
Axes of the slice: x: 2, y: 2, z: 4, core: 2. Of those that a mesh axis runs over, the one named last changes fastest.
Arguments:
- query_rows: bfloat16 [4096, 2560], P(('groups', 'cubes')), parts along dimension 0, may hold values from -8 to 8
- key_rows: bfloat16 [4096, 2560], P(('groups', 'cubes')), parts along dimension 0, may hold values from -9 to 9
- value_rows: bfloat16 [4096, 2560], P(('groups', 'cubes')), parts along dimension 0, may hold values from -6 to 6
- gate_logits: bfloat16 [4096, 40], P(('groups', 'cubes')), parts along dimension 0, may hold values from -6 to 6
- selection: int32 [64, 20, 8], P('groups'), parts along dimension 0, may hold values from 0 to 31, all different within a row; in each aligned block of 40 rows (0 to 39, 40 to 79, ..., all dimensions but the last counted through in order) at most 11 rows name the same one
- cube_ids: int32 [64], P('groups'), parts along dimension 0, may hold values from 0 to 31, each once
Outputs:
- mixed: bfloat16 [4096, 2560], P(('groups', 'cubes')), parts along dimension 0
There are 2 independent parts, one for each index of `groups`. A program takes and returns all parts, laid end to end along the dimension named above; each array names one. Nothing has to cross between parts.
Inputs may be any that keep to these rules, and one draw needn't show every extreme that they name: `selection`: each row of 8 names different cubes. Among the rows of one device (its 2 stored blocks with all 20 heads) no cube is named more than 11 times, a bound that some block reaches. `cube_ids`: each cube number appears once.
All inputs are finite; a program needn't handle non-finite values.
Results may differ from a plain program's by a relative error of at most 0.0047.
Values may be sent and summed in bfloat16 or wider, within the bound.
No kernel may reach another device: no remote copies, remote signals or barrier semaphores. Data moves between devices by JAX's collectives and lax.ppermute only.
A program may use at most 128 MiB of HBM per device.

v0:
```python
import math

import jax
import jax.numpy as jnp
from jax import lax
from jax.sharding import PartitionSpec as P

CUBE = 64


NEG_START = -1e30


def block_partials(query_slots, pair_slots):
    head_size = query_slots.shape[-1]
    factor = 1.0 / math.sqrt(head_size)
    slot_keys = pair_slots[:, :, :head_size]
    slot_values = pair_slots[:, :, head_size:]
    scores = (
        jnp.einsum("sqd,skd->sqk", query_slots, slot_keys, preferred_element_type=jnp.float32)
        * factor
    )
    slot_max = jnp.max(scores, axis=2)
    weights = jnp.exp(scores - slot_max[:, :, None])
    slot_total = jnp.sum(weights, axis=2)
    numerator = jnp.einsum(
        "sqk,skd->sqd",
        weights.astype(jnp.bfloat16),
        slot_values,
        preferred_element_type=jnp.float32,
    )
    return (numerator, slot_max, slot_total)


def merge_slots(state, results, slot_group):
    numerator, running_max, totals = state
    slot_numerator, slot_max, slot_total = results
    group_count = numerator.shape[0]
    slot_count = slot_group.shape[0]
    member = slot_group[:, None] == jnp.arange(group_count, dtype=jnp.int32)[None, :]
    is_valid = slot_group >= 0
    group_max = jnp.max(jnp.where(member[:, :, None], slot_max[:, None, :], -jnp.inf), axis=0)
    new_max = jnp.maximum(running_max, group_max)
    slot_base = jnp.take(new_max, jnp.maximum(slot_group, 0), axis=0)
    slot_weight = jnp.exp(jnp.where(is_valid[:, None], slot_max - slot_base, -jnp.inf))
    onehot = member.astype(jnp.float32).T
    weighted = (slot_weight[:, :, None] * slot_numerator).reshape(slot_count, -1)
    added_numerator = jnp.dot(onehot, weighted, precision=lax.Precision.HIGHEST).reshape(
        numerator.shape
    )
    added_total = jnp.dot(onehot, slot_weight * slot_total, precision=lax.Precision.HIGHEST)
    decay_factor = jnp.exp(running_max - new_max)
    return (
        numerator * decay_factor[:, :, None] + added_numerator,
        new_max,
        totals * decay_factor + added_total,
    )


def body(query_rows, key_rows, value_rows, gate_logits, selection, cube_ids):
    device_count = lax.axis_size("cubes")
    token_count = query_rows.shape[0]
    feature_width = query_rows.shape[1]
    head_count = gate_logits.shape[1] // 2
    head_size = feature_width // head_count
    local_cubes = token_count // CUBE
    total_cubes = cube_ids.shape[0]
    picks_each = selection.shape[2]
    depth_rounds = max(2, head_count * picks_each // device_count + 1)
    request_count = local_cubes * head_count * picks_each
    factor = 1.0 / math.sqrt(head_size)
    self_index = lax.axis_index("cubes")
    pooled_keys = jnp.mean(
        key_rows.reshape(local_cubes, CUBE, feature_width), axis=1, dtype=jnp.float32
    ).astype(jnp.bfloat16)
    pooled_values = jnp.mean(
        value_rows.reshape(local_cubes, CUBE, feature_width), axis=1, dtype=jnp.float32
    ).astype(jnp.bfloat16)
    query_heads = query_rows.reshape(token_count, head_count, head_size)
    start_state = (
        jnp.zeros((head_count, token_count, head_size), jnp.float32),
        jnp.full((head_count, token_count), NEG_START, jnp.float32),
        jnp.zeros((head_count, token_count), jnp.float32),
    )
    numerator, running_max, totals = start_state
    piece_keys = lax.all_gather(pooled_keys, "cubes", axis=0, tiled=True)
    piece_values = lax.all_gather(pooled_values, "cubes", axis=0, tiled=True)
    piece_rows = piece_keys.shape[0]
    scores = (
        jnp.einsum(
            "thd,jhd->htj",
            query_heads,
            piece_keys.reshape(piece_rows, head_count, head_size),
            preferred_element_type=jnp.float32,
        )
        * factor
    )
    new_max = jnp.maximum(running_max, jnp.max(scores, axis=2))
    weights = jnp.exp(scores - new_max[:, :, None])
    added = jnp.einsum(
        "htj,jhd->htd",
        weights.astype(jnp.bfloat16),
        piece_values.reshape(piece_rows, head_count, head_size),
        preferred_element_type=jnp.float32,
    )
    numerator = added
    totals = jnp.sum(weights, axis=2)
    coarse = jnp.transpose(numerator / totals[:, :, None], (1, 0, 2))
    cube_range = jnp.arange(total_cubes, dtype=jnp.int32)
    position = jnp.sum(
        jnp.where(cube_ids[None, :] == cube_range[:, None], cube_range[None, :], 0), axis=1
    )
    targets = jnp.take(position, selection.reshape(-1)).reshape(device_count, request_count)
    request_range = jnp.arange(request_count, dtype=jnp.int32)
    request_group = request_range // picks_each
    request_head = request_group % head_count
    round_range = jnp.arange(depth_rounds, dtype=jnp.int32)
    own_targets = lax.dynamic_index_in_dim(targets, self_index, 0, keepdims=False)
    same_target = own_targets[:, None] == cube_range[None, :]
    running_count = jnp.cumsum(same_target.astype(jnp.int32), axis=0)
    own_rank = jnp.sum(jnp.where(same_target, running_count, 0), axis=1) - 1
    chosen_round = same_target[None, :, :] & (own_rank[None, :, None] == round_range[:, None, None])
    wanted_all = jnp.sum(jnp.where(chosen_round, request_group[None, :, None] + 1, 0), axis=1) - 1
    own_cubes = self_index * local_cubes + jnp.arange(local_cubes, dtype=jnp.int32)
    hit_mine = targets[:, :, None] == own_cubes[None, None, :]
    mine_rank = jnp.cumsum(hit_mine.astype(jnp.int32), axis=1) - 1
    round_hit = hit_mine[None] & (mine_rank[None] == round_range[:, None, None, None])
    incoming_all = (
        jnp.sum(jnp.where(round_hit, request_head[None, None, :, None] + 1, 0), axis=2) - 1
    )
    query_groups = (
        query_rows.reshape(local_cubes, CUBE, head_count, head_size)
        .transpose(0, 2, 1, 3)
        .reshape(local_cubes * head_count, CUBE, head_size)
    )
    pair_blocks = jnp.concatenate(
        (
            key_rows.reshape(local_cubes, CUBE, head_count, head_size),
            value_rows.reshape(local_cubes, CUBE, head_count, head_size),
        ),
        axis=3,
    )
    pair_groups = pair_blocks.transpose(0, 2, 1, 3).reshape(
        local_cubes * head_count, CUBE, 2 * head_size
    )
    base_group = head_count * jnp.arange(local_cubes, dtype=jnp.int32)

    def held_pairs(incoming):
        source = (jnp.maximum(incoming, 0) + base_group[None, :]).reshape(-1)
        picked = jnp.take(pair_groups, source, axis=0)
        return jnp.where(
            (incoming >= 0).reshape(-1)[:, None, None], picked, jnp.zeros((), jnp.bfloat16)
        )

    def asked_queries(wanted):
        picked = jnp.take(query_groups, jnp.maximum(wanted, 0), axis=0)
        return jnp.where((wanted >= 0)[:, None, None], picked, jnp.zeros((), jnp.bfloat16))

    def one_round(state, tables):
        wanted, incoming = tables
        arrived = lax.all_to_all(
            held_pairs(incoming), "cubes", split_axis=0, concat_axis=0, tiled=True
        )
        results = block_partials(asked_queries(wanted), arrived)
        return (merge_slots(state, results, wanted), None)

    group_count = local_cubes * head_count
    start_state = (
        jnp.zeros((group_count, CUBE, head_size), jnp.float32),
        jnp.full((group_count, CUBE), NEG_START, jnp.float32),
        jnp.zeros((group_count, CUBE), jnp.float32),
    )
    final_state, unused = lax.scan(one_round, start_state, (wanted_all, incoming_all))
    numerator, running_max, totals = final_state
    fine_groups = numerator / totals[:, :, None]
    fine = (
        fine_groups.reshape(local_cubes, head_count, CUBE, head_size)
        .transpose(0, 2, 1, 3)
        .reshape(token_count, head_count, head_size)
    )
    gates = jax.nn.sigmoid(gate_logits.astype(jnp.float32))
    mixed = gates[:, :head_count, None] * coarse + gates[:, head_count:, None] * fine
    return mixed.reshape(token_count, feature_width).astype(jnp.bfloat16)


def solution(mesh):
    placed = (
        P(("groups", "cubes"), None),
        P(("groups", "cubes"), None),
        P(("groups", "cubes"), None),
        P(("groups", "cubes"), None),
        P("groups", None, None),
        P("groups"),
    )
    return jax.shard_map(
        body, mesh=mesh, in_specs=placed, out_specs=P(("groups", "cubes"), None), check_vma=False
    )
```

profile of v0, /device:TPU:0, one launch (start us, length us, event | category | flops | bytes accessed | tf_op | source)
XLA Modules:
  0.0 511.7 jit_solution(15837783295440268176)
XLA Ops:
  2.8 4.5 compare_select_fusion.3
  9.5 15.6 %select_select_fusion.1 = s32[5120]{0:T(1024)S(1)} fusion(pred[5120]{0:T(1024)(128)(4,1)S(1)} %get-tuple-element.141, pred[5120]{0:T(1024)(128)(4,1)S(1)} %get-tuple-element.140, pred[5120]{0:T(1024)(128)(4,1)S(1)} %get-tuple-element.139, pred[5120]{0:T(1024)(128)(4,1)S(1)} %get-tuple-element.138, pred[5120]{0:T(1024)(128)(4,1)S(1)} %get-tuple-element.137, ...), kind=kLoop, calls=%fused_computation.125 | loop fusion | flops 128000 | bytes 169060 | tf_op jit(solution)/shard_map/jit(_take)/gather | solution.py:113
  32.9 432.1 %while.16 = (s32[]{:T(128)}, f32[40,64,128]{2,0,1:T(8,128)S(1)}, f32[40,64]{1,0:T(8,128)S(1)}, f32[40,64]{1,0:T(8,128)S(1)}, s32[11,32]{1,0:T(8,128)S(1)}, /*ind...) while((s32[]{:T(128)}, f32[40,64,128]{2,0,1:T(8,128)S(1)}, ...), condition=%wide.region_16.17_spmd.clone.clone, body=%wide.region_12.16_spmd.clone.clone.sunk | while | flops 197712672 | bytes 22294940 | solution.py:173
  33.6 1.9 gather_fusion
  36.8 7.4 %all-to-all-start = ((bf16[32,64,256]{2,1,0:T(8,128)(2,1)}), bf16[32,64,256]{2,1,0:T(8,128)(2,1)S(1)}, u32[]{:S(2)}, u32[]{:S(2)}) async-start(bf16[32,64,256]{2,1,0:T(8,128)(2,1)} %select_select_fusion.3), calls=%async_computation | async-start | bytes 2097152 | tf_op jit(solution)/shard_map/while/body/eval_jaxpr/all_to_all | solution.py:161
  45.8 21.3 %all-to-all-done = bf16[32,64,256]{2,1,0:T(8,128)(2,1)S(1)} async-done(((bf16[32,64,256]{2,1,0:T(8,128)(2,1)}), bf16[32,64,256]{2,1,0:T(8,128)(2,1)S(1)}, u32[]{:S(2)}, u32[]{:S(2)}) %all-to-all-start) | async-done | bytes 1048608 | tf_op jit(solution)/shard_map/while/body/eval_jaxpr/all_to_all | solution.py:161
  73.5 1.9 gather_fusion
  76.6 6.8 %all-to-all-start = ((bf16[32,64,256]{2,1,0:T(8,128)(2,1)}), bf16[32,64,256]{2,1,0:T(8,128)(2,1)S(1)}, u32[]{:S(2)}, u32[]{:S(2)}) async-start(bf16[32,64,256]{2,1,0:T(8,128)(2,1)} %select_select_fusion.3), calls=%async_computation | async-start | bytes 2097152 | tf_op jit(solution)/shard_map/while/body/eval_jaxpr/all_to_all | solution.py:161
  85.0 21.3 %all-to-all-done = bf16[32,64,256]{2,1,0:T(8,128)(2,1)S(1)} async-done(((bf16[32,64,256]{2,1,0:T(8,128)(2,1)}), bf16[32,64,256]{2,1,0:T(8,128)(2,1)S(1)}, u32[]{:S(2)}, u32[]{:S(2)}) %all-to-all-start) | async-done | bytes 1048608 | tf_op jit(solution)/shard_map/while/body/eval_jaxpr/all_to_all | solution.py:161
  112.7 1.9 gather_fusion
  115.8 6.8 %all-to-all-start = ((bf16[32,64,256]{2,1,0:T(8,128)(2,1)}), bf16[32,64,256]{2,1,0:T(8,128)(2,1)S(1)}, u32[]{:S(2)}, u32[]{:S(2)}) async-start(bf16[32,64,256]{2,1,0:T(8,128)(2,1)} %select_select_fusion.3), calls=%async_computation | async-start | bytes 2097152 | tf_op jit(solution)/shard_map/while/body/eval_jaxpr/all_to_all | solution.py:161
  124.2 21.3 %all-to-all-done = bf16[32,64,256]{2,1,0:T(8,128)(2,1)S(1)} async-done(((bf16[32,64,256]{2,1,0:T(8,128)(2,1)}), bf16[32,64,256]{2,1,0:T(8,128)(2,1)S(1)}, u32[]{:S(2)}, u32[]{:S(2)}) %all-to-all-start) | async-done | bytes 1048608 | tf_op jit(solution)/shard_map/while/body/eval_jaxpr/all_to_all | solution.py:161
  151.9 1.9 gather_fusion
  155.1 6.8 %all-to-all-start = ((bf16[32,64,256]{2,1,0:T(8,128)(2,1)}), bf16[32,64,256]{2,1,0:T(8,128)(2,1)S(1)}, u32[]{:S(2)}, u32[]{:S(2)}) async-start(bf16[32,64,256]{2,1,0:T(8,128)(2,1)} %select_select_fusion.3), calls=%async_computation | async-start | bytes 2097152 | tf_op jit(solution)/shard_map/while/body/eval_jaxpr/all_to_all | solution.py:161
  163.4 21.3 %all-to-all-done = bf16[32,64,256]{2,1,0:T(8,128)(2,1)S(1)} async-done(((bf16[32,64,256]{2,1,0:T(8,128)(2,1)}), bf16[32,64,256]{2,1,0:T(8,128)(2,1)S(1)}, u32[]{:S(2)}, u32[]{:S(2)}) %all-to-all-start) | async-done | bytes 1048608 | tf_op jit(solution)/shard_map/while/body/eval_jaxpr/all_to_all | solution.py:161
  194.3 6.8 %all-to-all-start = ((bf16[32,64,256]{2,1,0:T(8,128)(2,1)}), bf16[32,64,256]{2,1,0:T(8,128)(2,1)S(1)}, u32[]{:S(2)}, u32[]{:S(2)}) async-start(bf16[32,64,256]{2,1,0:T(8,128)(2,1)} %select_select_fusion.3), calls=%async_computation | async-start | bytes 2097152 | tf_op jit(solution)/shard_map/while/body/eval_jaxpr/all_to_all | solution.py:161
  202.7 21.3 %all-to-all-done = bf16[32,64,256]{2,1,0:T(8,128)(2,1)S(1)} async-done(((bf16[32,64,256]{2,1,0:T(8,128)(2,1)}), bf16[32,64,256]{2,1,0:T(8,128)(2,1)S(1)}, u32[]{:S(2)}, u32[]{:S(2)}) %all-to-all-start) | async-done | bytes 1048608 | tf_op jit(solution)/shard_map/while/body/eval_jaxpr/all_to_all | solution.py:161
  233.5 6.8 %all-to-all-start = ((bf16[32,64,256]{2,1,0:T(8,128)(2,1)}), bf16[32,64,256]{2,1,0:T(8,128)(2,1)S(1)}, u32[]{:S(2)}, u32[]{:S(2)}) async-start(bf16[32,64,256]{2,1,0:T(8,128)(2,1)} %select_select_fusion.3), calls=%async_computation | async-start | bytes 2097152 | tf_op jit(solution)/shard_map/while/body/eval_jaxpr/all_to_all | solution.py:161
  241.9 21.3 %all-to-all-done = bf16[32,64,256]{2,1,0:T(8,128)(2,1)S(1)} async-done(((bf16[32,64,256]{2,1,0:T(8,128)(2,1)}), bf16[32,64,256]{2,1,0:T(8,128)(2,1)S(1)}, u32[]{:S(2)}, u32[]{:S(2)}) %all-to-all-start) | async-done | bytes 1048608 | tf_op jit(solution)/shard_map/while/body/eval_jaxpr/all_to_all | solution.py:161
  269.6 1.9 gather_fusion
  272.7 6.8 %all-to-all-start = ((bf16[32,64,256]{2,1,0:T(8,128)(2,1)}), bf16[32,64,256]{2,1,0:T(8,128)(2,1)S(1)}, u32[]{:S(2)}, u32[]{:S(2)}) async-start(bf16[32,64,256]{2,1,0:T(8,128)(2,1)} %select_select_fusion.3), calls=%async_computation | async-start | bytes 2097152 | tf_op jit(solution)/shard_map/while/body/eval_jaxpr/all_to_all | solution.py:161
  281.1 21.3 %all-to-all-done = bf16[32,64,256]{2,1,0:T(8,128)(2,1)S(1)} async-done(((bf16[32,64,256]{2,1,0:T(8,128)(2,1)}), bf16[32,64,256]{2,1,0:T(8,128)(2,1)S(1)}, u32[]{:S(2)}, u32[]{:S(2)}) %all-to-all-start) | async-done | bytes 1048608 | tf_op jit(solution)/shard_map/while/body/eval_jaxpr/all_to_all | solution.py:161
  312.0 6.8 %all-to-all-start = ((bf16[32,64,256]{2,1,0:T(8,128)(2,1)}), bf16[32,64,256]{2,1,0:T(8,128)(2,1)S(1)}, u32[]{:S(2)}, u32[]{:S(2)}) async-start(bf16[32,64,256]{2,1,0:T(8,128)(2,1)} %select_select_fusion.3), calls=%async_computation | async-start | bytes 2097152 | tf_op jit(solution)/shard_map/while/body/eval_jaxpr/all_to_all | solution.py:161
  320.3 21.3 %all-to-all-done = bf16[32,64,256]{2,1,0:T(8,128)(2,1)S(1)} async-done(((bf16[32,64,256]{2,1,0:T(8,128)(2,1)}), bf16[32,64,256]{2,1,0:T(8,128)(2,1)S(1)}, u32[]{:S(2)}, u32[]{:S(2)}) %all-to-all-start) | async-done | bytes 1048608 | tf_op jit(solution)/shard_map/while/body/eval_jaxpr/all_to_all | solution.py:161
  351.2 6.8 %all-to-all-start = ((bf16[32,64,256]{2,1,0:T(8,128)(2,1)}), bf16[32,64,256]{2,1,0:T(8,128)(2,1)S(1)}, u32[]{:S(2)}, u32[]{:S(2)}) async-start(bf16[32,64,256]{2,1,0:T(8,128)(2,1)} %select_select_fusion.3), calls=%async_computation | async-start | bytes 2097152 | tf_op jit(solution)/shard_map/while/body/eval_jaxpr/all_to_all | solution.py:161
  359.6 21.3 %all-to-all-done = bf16[32,64,256]{2,1,0:T(8,128)(2,1)S(1)} async-done(((bf16[32,64,256]{2,1,0:T(8,128)(2,1)}), bf16[32,64,256]{2,1,0:T(8,128)(2,1)S(1)}, u32[]{:S(2)}, u32[]{:S(2)}) %all-to-all-start) | async-done | bytes 1048608 | tf_op jit(solution)/shard_map/while/body/eval_jaxpr/all_to_all | solution.py:161
  390.4 6.8 %all-to-all-start = ((bf16[32,64,256]{2,1,0:T(8,128)(2,1)}), bf16[32,64,256]{2,1,0:T(8,128)(2,1)S(1)}, u32[]{:S(2)}, u32[]{:S(2)}) async-start(bf16[32,64,256]{2,1,0:T(8,128)(2,1)} %select_select_fusion.3), calls=%async_computation | async-start | bytes 2097152 | tf_op jit(solution)/shard_map/while/body/eval_jaxpr/all_to_all | solution.py:161
  398.8 21.3 %all-to-all-done = bf16[32,64,256]{2,1,0:T(8,128)(2,1)S(1)} async-done(((bf16[32,64,256]{2,1,0:T(8,128)(2,1)}), bf16[32,64,256]{2,1,0:T(8,128)(2,1)S(1)}, u32[]{:S(2)}, u32[]{:S(2)}) %all-to-all-start) | async-done | bytes 1048608 | tf_op jit(solution)/shard_map/while/body/eval_jaxpr/all_to_all | solution.py:161
  429.6 6.8 %all-to-all-start = ((bf16[32,64,256]{2,1,0:T(8,128)(2,1)}), bf16[32,64,256]{2,1,0:T(8,128)(2,1)S(1)}, u32[]{:S(2)}, u32[]{:S(2)}) async-start(bf16[32,64,256]{2,1,0:T(8,128)(2,1)} %select_select_fusion.3), calls=%async_computation | async-start | bytes 2097152 | tf_op jit(solution)/shard_map/while/body/eval_jaxpr/all_to_all | solution.py:161
  438.0 21.3 %all-to-all-done = bf16[32,64,256]{2,1,0:T(8,128)(2,1)S(1)} async-done(((bf16[32,64,256]{2,1,0:T(8,128)(2,1)}), bf16[32,64,256]{2,1,0:T(8,128)(2,1)S(1)}, u32[]{:S(2)}, u32[]{:S(2)}) %all-to-all-start) | async-done | bytes 1048608 | tf_op jit(solution)/shard_map/while/body/eval_jaxpr/all_to_all | solution.py:161
  468.2 23.1 %all-gather = bf16[16,2,2560]{2,1,0:T(2,128)(2,1)S(1)} all-gather(bf16[1,2,2560]{2,1,0:T(2,128)(2,1)S(1)} %fusion.37), channel_id=1, replica_groups=mesh['groups'=2,'cubes'=16] {'cubes'}, dimensions={0}, use_global_device_ids=true | all-gather | bytes 174080 | tf_op jit(solution)/shard_map/all_gather | solution.py:86
  492.0 18.0 %all-gather.1 = bf16[16,2,2560]{2,1,0:T(2,128)(2,1)S(1)} all-gather(bf16[1,2,2560]{2,1,0:T(2,128)(2,1)S(1)} %fusion.38), channel_id=1, replica_groups=mesh['groups'=2,'cubes'=16] {'cubes'}, dimensions={0}, use_global_device_ids=true | all-gather | bytes 174080 | tf_op jit(solution)/shard_map/all_gather | solution.py:87
  (557 shorter events, 128.1 us)
Async XLA Ops:
  2.6 27.3 %copy-start.4 = (bf16[128,2560]{1,0:T(8,128)(2,1)S(1)}, bf16[128,2560]{1,0:T(8,128)(2,1)}, u32[]{:S(2)}) copy-start(bf16[128,2560]{1,0:T(8,128)(2,1)} %param.9) | copy-start | bytes 1966084
  32.9 11.3 %copy-start = (bf16[40,64,128]{2,1,0:T(8,128)(2,1)}, bf16[40,64,128]{2,1,0:T(8,128)(2,1)S(1)}, u32[]{:S(2)}) copy-start(bf16[40,64,128]{2,1,0:T(8,128)(2,1)S(1)} %get-tuple-element.288) | copy-start | bytes 1966084 | tf_op jit(solution)/shard_map/while
  33.0 12.7 %copy-start.11 = (s32[11,32]{1,0:T(8,128)}, s32[11,32]{1,0:T(8,128)S(1)}, u32[]{:S(2)}) copy-start(s32[11,32]{1,0:T(8,128)S(1)} %get-tuple-element.287) | copy-start | bytes 4228 | tf_op jit(solution)/shard_map/while
  36.8 30.3 %all-to-all-start = ((bf16[32,64,256]{2,1,0:T(8,128)(2,1)}), bf16[32,64,256]{2,1,0:T(8,128)(2,1)S(1)}, u32[]{:S(2)}, u32[]{:S(2)}) async-start(bf16[32,64,256]{2,1,0:T(8,128)(2,1)} %select_select_fusion.3), calls=%async_computation | async-start | bytes 2097152 | tf_op jit(solution)/shard_map/while/body/eval_jaxpr/all_to_all | solution.py:161
  72.8 10.7 %copy-start = (bf16[40,64,128]{2,1,0:T(8,128)(2,1)}, bf16[40,64,128]{2,1,0:T(8,128)(2,1)S(1)}, u32[]{:S(2)}) copy-start(bf16[40,64,128]{2,1,0:T(8,128)(2,1)S(1)} %get-tuple-element.288) | copy-start | bytes 1966084 | tf_op jit(solution)/shard_map/while
  72.8 12.1 %copy-start.11 = (s32[11,32]{1,0:T(8,128)}, s32[11,32]{1,0:T(8,128)S(1)}, u32[]{:S(2)}) copy-start(s32[11,32]{1,0:T(8,128)S(1)} %get-tuple-element.287) | copy-start | bytes 4228 | tf_op jit(solution)/shard_map/while
  76.6 29.7 %all-to-all-start = ((bf16[32,64,256]{2,1,0:T(8,128)(2,1)}), bf16[32,64,256]{2,1,0:T(8,128)(2,1)S(1)}, u32[]{:S(2)}, u32[]{:S(2)}) async-start(bf16[32,64,256]{2,1,0:T(8,128)(2,1)} %select_select_fusion.3), calls=%async_computation | async-start | bytes 2097152 | tf_op jit(solution)/shard_map/while/body/eval_jaxpr/all_to_all | solution.py:161
  112.0 10.7 %copy-start = (bf16[40,64,128]{2,1,0:T(8,128)(2,1)}, bf16[40,64,128]{2,1,0:T(8,128)(2,1)S(1)}, u32[]{:S(2)}) copy-start(bf16[40,64,128]{2,1,0:T(8,128)(2,1)S(1)} %get-tuple-element.288) | copy-start | bytes 1966084 | tf_op jit(solution)/shard_map/while
  112.0 12.1 %copy-start.11 = (s32[11,32]{1,0:T(8,128)}, s32[11,32]{1,0:T(8,128)S(1)}, u32[]{:S(2)}) copy-start(s32[11,32]{1,0:T(8,128)S(1)} %get-tuple-element.287) | copy-start | bytes 4228 | tf_op jit(solution)/shard_map/while
  115.8 29.7 %all-to-all-start = ((bf16[32,64,256]{2,1,0:T(8,128)(2,1)}), bf16[32,64,256]{2,1,0:T(8,128)(2,1)S(1)}, u32[]{:S(2)}, u32[]{:S(2)}) async-start(bf16[32,64,256]{2,1,0:T(8,128)(2,1)} %select_select_fusion.3), calls=%async_computation | async-start | bytes 2097152 | tf_op jit(solution)/shard_map/while/body/eval_jaxpr/all_to_all | solution.py:161
  151.2 12.1 %copy-start.11 = (s32[11,32]{1,0:T(8,128)}, s32[11,32]{1,0:T(8,128)S(1)}, u32[]{:S(2)}) copy-start(s32[11,32]{1,0:T(8,128)S(1)} %get-tuple-element.287) | copy-start | bytes 4228 | tf_op jit(solution)/shard_map/while
  155.1 29.7 %all-to-all-start = ((bf16[32,64,256]{2,1,0:T(8,128)(2,1)}), bf16[32,64,256]{2,1,0:T(8,128)(2,1)S(1)}, u32[]{:S(2)}, u32[]{:S(2)}) async-start(bf16[32,64,256]{2,1,0:T(8,128)(2,1)} %select_select_fusion.3), calls=%async_computation | async-start | bytes 2097152 | tf_op jit(solution)/shard_map/while/body/eval_jaxpr/all_to_all | solution.py:161
  190.4 10.7 %copy-start = (bf16[40,64,128]{2,1,0:T(8,128)(2,1)}, bf16[40,64,128]{2,1,0:T(8,128)(2,1)S(1)}, u32[]{:S(2)}) copy-start(bf16[40,64,128]{2,1,0:T(8,128)(2,1)S(1)} %get-tuple-element.288) | copy-start | bytes 1966084 | tf_op jit(solution)/shard_map/while
  190.5 12.1 %copy-start.11 = (s32[11,32]{1,0:T(8,128)}, s32[11,32]{1,0:T(8,128)S(1)}, u32[]{:S(2)}) copy-start(s32[11,32]{1,0:T(8,128)S(1)} %get-tuple-element.287) | copy-start | bytes 4228 | tf_op jit(solution)/shard_map/while
  194.3 29.7 %all-to-all-start = ((bf16[32,64,256]{2,1,0:T(8,128)(2,1)}), bf16[32,64,256]{2,1,0:T(8,128)(2,1)S(1)}, u32[]{:S(2)}, u32[]{:S(2)}) async-start(bf16[32,64,256]{2,1,0:T(8,128)(2,1)} %select_select_fusion.3), calls=%async_computation | async-start | bytes 2097152 | tf_op jit(solution)/shard_map/while/body/eval_jaxpr/all_to_all | solution.py:161
  229.7 12.1 %copy-start.11 = (s32[11,32]{1,0:T(8,128)}, s32[11,32]{1,0:T(8,128)S(1)}, u32[]{:S(2)}) copy-start(s32[11,32]{1,0:T(8,128)S(1)} %get-tuple-element.287) | copy-start | bytes 4228 | tf_op jit(solution)/shard_map/while
  233.5 29.7 %all-to-all-start = ((bf16[32,64,256]{2,1,0:T(8,128)(2,1)}), bf16[32,64,256]{2,1,0:T(8,128)(2,1)S(1)}, u32[]{:S(2)}, u32[]{:S(2)}) async-start(bf16[32,64,256]{2,1,0:T(8,128)(2,1)} %select_select_fusion.3), calls=%async_computation | async-start | bytes 2097152 | tf_op jit(solution)/shard_map/while/body/eval_jaxpr/all_to_all | solution.py:161
  268.9 12.1 %copy-start.11 = (s32[11,32]{1,0:T(8,128)}, s32[11,32]{1,0:T(8,128)S(1)}, u32[]{:S(2)}) copy-start(s32[11,32]{1,0:T(8,128)S(1)} %get-tuple-element.287) | copy-start | bytes 4228 | tf_op jit(solution)/shard_map/while
  272.7 29.7 %all-to-all-start = ((bf16[32,64,256]{2,1,0:T(8,128)(2,1)}), bf16[32,64,256]{2,1,0:T(8,128)(2,1)S(1)}, u32[]{:S(2)}, u32[]{:S(2)}) async-start(bf16[32,64,256]{2,1,0:T(8,128)(2,1)} %select_select_fusion.3), calls=%async_computation | async-start | bytes 2097152 | tf_op jit(solution)/shard_map/while/body/eval_jaxpr/all_to_all | solution.py:161
  308.1 12.1 %copy-start.11 = (s32[11,32]{1,0:T(8,128)}, s32[11,32]{1,0:T(8,128)S(1)}, u32[]{:S(2)}) copy-start(s32[11,32]{1,0:T(8,128)S(1)} %get-tuple-element.287) | copy-start | bytes 4228 | tf_op jit(solution)/shard_map/while
  312.0 29.7 %all-to-all-start = ((bf16[32,64,256]{2,1,0:T(8,128)(2,1)}), bf16[32,64,256]{2,1,0:T(8,128)(2,1)S(1)}, u32[]{:S(2)}, u32[]{:S(2)}) async-start(bf16[32,64,256]{2,1,0:T(8,128)(2,1)} %select_select_fusion.3), calls=%async_computation | async-start | bytes 2097152 | tf_op jit(solution)/shard_map/while/body/eval_jaxpr/all_to_all | solution.py:161
  347.3 10.7 %copy-start = (bf16[40,64,128]{2,1,0:T(8,128)(2,1)}, bf16[40,64,128]{2,1,0:T(8,128)(2,1)S(1)}, u32[]{:S(2)}) copy-start(bf16[40,64,128]{2,1,0:T(8,128)(2,1)S(1)} %get-tuple-element.288) | copy-start | bytes 1966084 | tf_op jit(solution)/shard_map/while
  347.3 12.1 %copy-start.11 = (s32[11,32]{1,0:T(8,128)}, s32[11,32]{1,0:T(8,128)S(1)}, u32[]{:S(2)}) copy-start(s32[11,32]{1,0:T(8,128)S(1)} %get-tuple-element.287) | copy-start | bytes 4228 | tf_op jit(solution)/shard_map/while
  351.2 29.7 %all-to-all-start = ((bf16[32,64,256]{2,1,0:T(8,128)(2,1)}), bf16[32,64,256]{2,1,0:T(8,128)(2,1)S(1)}, u32[]{:S(2)}, u32[]{:S(2)}) async-start(bf16[32,64,256]{2,1,0:T(8,128)(2,1)} %select_select_fusion.3), calls=%async_computation | async-start | bytes 2097152 | tf_op jit(solution)/shard_map/while/body/eval_jaxpr/all_to_all | solution.py:161
  386.6 10.7 %copy-start = (bf16[40,64,128]{2,1,0:T(8,128)(2,1)}, bf16[40,64,128]{2,1,0:T(8,128)(2,1)S(1)}, u32[]{:S(2)}) copy-start(bf16[40,64,128]{2,1,0:T(8,128)(2,1)S(1)} %get-tuple-element.288) | copy-start | bytes 1966084 | tf_op jit(solution)/shard_map/while
  386.6 12.1 %copy-start.11 = (s32[11,32]{1,0:T(8,128)}, s32[11,32]{1,0:T(8,128)S(1)}, u32[]{:S(2)}) copy-start(s32[11,32]{1,0:T(8,128)S(1)} %get-tuple-element.287) | copy-start | bytes 4228 | tf_op jit(solution)/shard_map/while
  390.4 29.7 %all-to-all-start = ((bf16[32,64,256]{2,1,0:T(8,128)(2,1)}), bf16[32,64,256]{2,1,0:T(8,128)(2,1)S(1)}, u32[]{:S(2)}, u32[]{:S(2)}) async-start(bf16[32,64,256]{2,1,0:T(8,128)(2,1)} %select_select_fusion.3), calls=%async_computation | async-start | bytes 2097152 | tf_op jit(solution)/shard_map/while/body/eval_jaxpr/all_to_all | solution.py:161
  425.8 12.1 %copy-start.11 = (s32[11,32]{1,0:T(8,128)}, s32[11,32]{1,0:T(8,128)S(1)}, u32[]{:S(2)}) copy-start(s32[11,32]{1,0:T(8,128)S(1)} %get-tuple-element.287) | copy-start | bytes 4228 | tf_op jit(solution)/shard_map/while
  429.6 29.7 %all-to-all-start = ((bf16[32,64,256]{2,1,0:T(8,128)(2,1)}), bf16[32,64,256]{2,1,0:T(8,128)(2,1)S(1)}, u32[]{:S(2)}, u32[]{:S(2)}) async-start(bf16[32,64,256]{2,1,0:T(8,128)(2,1)} %select_select_fusion.3), calls=%async_computation | async-start | bytes 2097152 | tf_op jit(solution)/shard_map/while/body/eval_jaxpr/all_to_all | solution.py:161
  468.1 23.7 %copy-start.13 = (bf16[128,40]{0,1:T(8,128)(2,1)S(1)}, bf16[128,40]{0,1:T(8,128)(2,1)}, u32[]{:S(2)}) copy-start(bf16[128,40]{0,1:T(8,128)(2,1)} %param.11) | copy-start | bytes 30724
  468.1 23.8 %copy-start.7 = (bf16[128,2560]{1,0:T(8,128)(2,1)S(1)}, bf16[128,2560]{1,0:T(8,128)(2,1)}, u32[]{:S(2)}) copy-start(bf16[128,2560]{1,0:T(8,128)(2,1)} %param.10) | copy-start | bytes 1966084
  491.7 18.4 %copy-start.8 = (f32[128,20,128]{0,2,1:T(8,128)S(1)}, f32[128,20,128]{0,2,1:T(8,128)}, u32[]{:S(2)}) copy-start(f32[128,20,128]{0,2,1:T(8,128)} %copy.95) | copy-start | bytes 3932164
  (53 other events, 130.9 us)
where the time goes:
time: 514 us; the launch traced here: 512 us
  waiting for transfers between devices  235 us (46%)
  starting transfers between devices  75.3 us (15%)
  local copies, waits for them, and re-layouts  61.1 us (12%)
  matrix products  48.6 us (9%)
  other arithmetic  48.2 us (9%)
  blocking collectives  41.1 us (8%)
    all_to_all x11, waiting for transfers between devices, one_round(): lax.all_to_all(held_pairs(incoming), 'cubes', split_axis=0, concat_axis=0...  235 us
    all_to_all x11, starting transfers between devices, one_round(): lax.all_to_all(held_pairs(incoming), 'cubes', split_axis=0, concat_axis=0...  75.3 us
    all_gather x1, blocking collectives, body(): piece_keys = lax.all_gather(pooled_keys, 'cubes', axis=0, tiled=True)  23.1 us
    gather x3, other arithmetic, body(): jnp.take(position, selection.reshape(-1))  21.6 us
    gather x11, local copies, waits for them, and re-layouts, held_pairs(): picked = jnp.take(pair_groups, source, axis=0)  21.3 us
    dot_general x11, matrix products, merge_slots(): jnp.dot(onehot, weighted, precision=lax.Precision.HIGHEST)  20.3 us
    all_gather x1, blocking collectives, body(): piece_values = lax.all_gather(pooled_values, 'cubes', axis=0, tiled=True)  18 us
    dot_general x11, matrix products, block_partials(): jnp.einsum('sqd,skd->sqk', query_slots, slot_keys, preferred_element_type...  16.8 us
  transfers between devices with their start and end apart: 11, of which 11 were waited for; matrix products, arithmetic and copies ran while one was open for 3% of the time, Pallas kernels for 0%

commit v1 on v0

v1 whole, which is shorter than its diff:
```python
import functools
import math

import jax
import jax.numpy as jnp
from jax import lax
from jax.experimental import pallas as pl
from jax.experimental.pallas import tpu as pltpu
from jax.sharding import PartitionSpec as P

CUBE = 64
GATE_ROWS = 8
CHUNKS = (3, 2)
LOG2E = 1.4426950408889634

VMEM = pl.BlockSpec(memory_space=pltpu.VMEM)
SMEM = pl.BlockSpec(memory_space=pltpu.SMEM)
ANY = pl.BlockSpec(memory_space=pl.ANY)


def pack_kernel(spans, width, index_ref, *refs):
    sources = refs[: len(refs) - len(spans)]
    outputs = refs[len(sources) :]
    for (relative, (begin, size)), out in zip(spans, outputs):
        head_group = index_ref[0] ^ relative
        columns = pl.ds(pl.multiple_of(head_group * width + begin, 128), size)
        row = 0
        for source in sources:
            rows = source.shape[0]
            out[row : row + rows, :] = source[:, columns]
            row += rows


def pack(index, sources, spans, width):
    rows = sum(source.shape[0] for source in sources)
    return pl.pallas_call(
        functools.partial(pack_kernel, spans, width),
        out_shape=[jax.ShapeDtypeStruct((rows, size), jnp.bfloat16) for _, (_, size) in spans],
        in_specs=[SMEM] + [VMEM] * len(sources),
        out_specs=[VMEM] * len(spans),
        name="pack",
    )(index, *sources)


def unpack_kernel(spans, width, index_ref, *refs):
    pieces, out = refs[:-1], refs[-1]
    for (relative, (begin, size)), piece in zip(spans, pieces):
        head_group = index_ref[0] ^ relative
        out[:, pl.ds(pl.multiple_of(head_group * width + begin, 128), size)] = piece[...]


def unpack(index, pieces, spans, width, columns):
    return pl.pallas_call(
        functools.partial(unpack_kernel, spans, width),
        out_shape=jax.ShapeDtypeStruct((pieces[0].shape[0], columns), jnp.bfloat16),
        in_specs=[SMEM] + [VMEM] * len(pieces),
        out_specs=VMEM,
        name="unpack",
    )(index, *pieces)


def attend_kernel(shape, tables_ref, *refs):
    groups, local, cubes, heads, first, count, picks, head_size, halves = shape
    queries = refs[:groups]
    stores = refs[groups : groups + halves]
    outs = refs[groups + halves : 2 * groups + halves]
    held, pooled_keys, pooled_values, sems = refs[2 * groups + halves :]
    tokens = local * CUBE
    half_rows = stores[0].shape[0]
    factor = 1.0 / math.sqrt(head_size)

    def copies(head):
        slot = head % 2
        columns = pl.ds(head * head_size, head_size)
        return [
            pltpu.make_async_copy(
                stores[i].at[:, columns],
                held.at[slot, pl.ds(i * half_rows, half_rows), :],
                sems.at[slot, i],
            )
            for i in range(halves)
        ]

    for copy in copies(0):
        copy.start()
    home = tables_ref[cubes + groups * local * heads * picks]
    for head in range(count):
        slot = head % 2
        if head + 1 < count:
            for copy in copies(head + 1):
                copy.start()
        for copy in copies(head):
            copy.wait()
        columns = pl.ds(head * head_size, head_size)

        def pool(piece, carry):
            base = pl.multiple_of(piece * 2 * tokens, 2 * tokens)
            rows = held[slot, pl.ds(base, 2 * tokens), :].astype(jnp.float32)
            means = jnp.sum(rows.reshape(2 * local, CUBE, head_size), axis=1) * (1.0 / CUBE)
            pooled_keys[pl.ds(piece * local, local), :] = means[:local]
            pooled_values[pl.ds(piece * local, local), :] = means[local:]
            return carry

        lax.fori_loop(0, cubes // local, pool, 0)
        coarse_keys = pooled_keys[...].astype(jnp.bfloat16)
        coarse_values = pooled_values[...].astype(jnp.bfloat16)
        for group in range(groups):
            gate_rows = queries[group][tokens : tokens + GATE_ROWS, columns].astype(jnp.float32)
            gates = jnp.transpose(jax.nn.sigmoid(gate_rows))
            for block in range(local):
                rows = slice(block * CUBE, (block + 1) * CUBE)
                query = queries[group][rows, columns]
                base = cubes + (((home ^ group) * local + block) * heads + first + head) * picks
                starts = [
                    pl.multiple_of(tables_ref[tables_ref[base + pick]], CUBE)
                    for pick in range(picks)
                ]
                keys = jnp.concatenate(
                    [held[slot, pl.ds(start, CUBE), :] for start in starts], axis=0
                )
                values = jnp.concatenate(
                    [held[slot, pl.ds(start + tokens, CUBE), :] for start in starts], axis=0
                )

                def part(keys, values):
                    scores = lax.dot_general(
                        query, keys, (((1,), (1,)), ((), ())), preferred_element_type=jnp.float32
                    )
                    top = jnp.max(scores, axis=1, keepdims=True)
                    weights = jnp.exp2((scores - top) * (factor * LOG2E))
                    total = jnp.sum(weights, axis=1, keepdims=True)
                    sums = jnp.dot(
                        weights.astype(jnp.bfloat16), values, preferred_element_type=jnp.float32
                    )
                    return sums, total

                coarse, coarse_total = part(coarse_keys, coarse_values)
                fine, fine_total = part(keys, values)
                mixed = coarse * (gates[rows, 0:1] / coarse_total)
                mixed += fine * (gates[rows, 1:2] / fine_total)
                outs[group][rows, columns] = mixed.astype(jnp.bfloat16)


def attend(tables, queries, stores, local, cubes, heads, first, count, picks, head_size):
    groups, halves = len(queries), len(stores)
    shape = (groups, local, cubes, heads, first, count, picks, head_size, halves)
    tokens = local * CUBE
    out = jax.ShapeDtypeStruct((tokens, count * head_size), jnp.bfloat16)
    units = groups * local * count
    flops = 4 * units * CUBE * CUBE * picks * head_size
    return pl.pallas_call(
        functools.partial(attend_kernel, shape),
        out_shape=[out] * groups,
        in_specs=[SMEM] + [VMEM] * groups + [ANY] * halves,
        out_specs=[VMEM] * groups,
        scratch_shapes=[
            pltpu.VMEM((2, 2 * cubes * CUBE, head_size), jnp.bfloat16),
            pltpu.VMEM((cubes, head_size), jnp.float32),
            pltpu.VMEM((cubes, head_size), jnp.float32),
            pltpu.SemaphoreType.DMA((2, halves)),
        ],
        cost_estimate=pl.CostEstimate(
            flops=flops,
            bytes_accessed=4 * cubes * CUBE * count * head_size,
            transcendentals=units * CUBE * CUBE * picks,
        ),
        name="attend",
    )(tables, *queries, *stores)


def body(query_rows, key_rows, value_rows, gate_logits, selection, cube_ids):
    devices = lax.axis_size("cubes")
    tokens, width = query_rows.shape
    heads_all = gate_logits.shape[1] // 2
    head_size = width // heads_all
    local = tokens // CUBE
    cubes = cube_ids.shape[0]
    picks = selection.shape[2]
    common = math.gcd(heads_all, devices)
    groups = common & -common
    ring = devices // groups
    heads = heads_all // groups
    group_width = heads * head_size
    self_index = lax.axis_index("cubes")
    home = self_index // ring
    place = self_index % ring

    sizes = CHUNKS if sum(CHUNKS) == heads else (heads,)
    firsts = [sum(sizes[:i]) for i in range(len(sizes))]
    spans = [(first * head_size, size * head_size) for first, size in zip(firsts, sizes)]

    def over_groups(value, relative):
        pairs = [(i, i ^ (relative * ring)) for i in range(devices)]
        return lax.ppermute(value, "cubes", pairs)

    def over_ring(value, step):
        return lax.ppermute(value, "cubes", [(i, i ^ step) for i in range(devices)])

    index = home.astype(jnp.int32).reshape(1)
    order = [r for r in range(groups - 1, 1, -1)] + ([1] if groups > 1 else [])
    kv_spans = [(r, span) for span in spans for r in range(groups)]
    kv_sent = pack(index, (key_rows, value_rows), kv_spans, group_width)
    gate_rows = jnp.transpose(gate_logits).reshape(2, heads_all * tokens)
    if tokens != head_size:
        raise ValueError("gate rows")
    gate_rows = jnp.pad(gate_rows, ((0, GATE_ROWS - 2), (0, 0)))
    q_spans = [(r, span) for span in spans for r in range(groups)]
    q_sent = pack(index, (query_rows, gate_rows), q_spans, group_width)

    cube_range = jnp.arange(cubes, dtype=jnp.int32)
    device_of = cube_range // local
    offset = jnp.bitwise_xor(device_of % ring, place)
    steps = [1 << bit for bit in range(ring.bit_length() - 2, -1, -1)]
    slot = jnp.zeros_like(offset)
    for number, step in enumerate(steps):
        slot = slot + jnp.where(jnp.bitwise_and(offset, step) > 0, 1 << number, 0)
    slot = slot * groups + jnp.bitwise_xor(device_of // ring, home)
    start = slot * (2 * tokens) + (cube_range % local) * CUBE
    row_of_cube = jnp.sum(
        jnp.where(cube_ids[None, :] == cube_range[:, None], start[None, :], 0), axis=1
    )
    chosen = selection.reshape(groups, ring, local, heads_all, picks)
    chosen = lax.dynamic_slice(
        chosen, (0, place, 0, home * heads, 0), (groups, 1, local, heads, picks)
    )
    tables = jnp.concatenate((row_of_cube, chosen.reshape(-1), index)).astype(jnp.int32)

    kv_pieces, q_pieces = [], []
    for c in range(len(sizes)):
        kv = list(kv_sent[c * groups : (c + 1) * groups])
        q = list(q_sent[c * groups : (c + 1) * groups])
        for r in order:
            kv[r] = over_groups(kv[r], r)
        for r in order:
            q[r] = over_groups(q[r], r)
        kv_pieces.append(kv)
        q_pieces.append(q)

    out_pieces = []
    for c, (first, size) in enumerate(zip(firsts, sizes)):
        stores = [jnp.concatenate(kv_pieces[c], axis=0)]
        for step in steps:
            gathered = stores[0] if len(stores) == 1 else jnp.concatenate(stores, axis=0)
            stores = [gathered, over_ring(gathered, step)]
        outs = attend(
            tables, q_pieces[c], stores, local, cubes, heads, first, size, picks, head_size
        )
        outs = list(outs)
        for r in order:
            outs[r] = over_groups(outs[r], r)
        out_pieces += outs
    return unpack(index, out_pieces, kv_spans, group_width, width)


def solution(mesh):
    placed = (
        P(("groups", "cubes"), None),
        P(("groups", "cubes"), None),
        P(("groups", "cubes"), None),
        P(("groups", "cubes"), None),
        P("groups", None, None),
        P("groups"),
    )
    return jax.shard_map(
        body, mesh=mesh, in_specs=placed, out_specs=P(("groups", "cubes"), None), check_vma=False
    )
```

time: 514 us -> 122 us (0.24)
  waiting for transfers between devices: 235 us -> 43.9 us
  local copies, waits for them, and re-layouts: 61.1 us -> 7.38 us
  matrix products: 48.6 us -> 0 us
  other arithmetic: 48.2 us -> 1.83 us
  starting transfers between devices: 75.3 us -> 33.9 us
  blocking collectives: 41.1 us -> 0 us
  Pallas kernels: 0 us -> 34.2 us
    all_to_all x11 -> x0, waiting for transfers between devices: 235 us -> none  [one_round(): lax.all_to_all(held_pairs(incoming), 'cubes', split_axis=0, concat_axis=0...]
    all_to_all x11 -> x0, starting transfers between devices: 75.3 us -> none  [one_round(): lax.all_to_all(held_pairs(incoming), 'cubes', split_axis=0, concat_axis=0...]
    dot_general x46 -> x0, matrix products: 48.6 us -> none  [the longest x11 20.3 us: merge_slots(): jnp.dot(onehot, weighted, precision=lax.Precision.HIGHEST)]
    gather x36 -> x0, local copies, waits for them, and re-layouts: 44.7 us -> none  [the longest x11 21.3 us: held_pairs(): picked = jnp.take(pair_groups, source, axis=0)]
    ppermute x0 -> x22, waiting for transfers between devices: none -> 43.9 us  [the longest x18 35.9 us: over_groups(): return lax.ppermute(value, 'cubes', pairs)]
    all_gather x2 -> x0, blocking collectives: 41.1 us -> none  [the longest x1 23.1 us: body(): piece_keys = lax.all_gather(pooled_keys, 'cubes', axis=0, tiled=True)]
    pallas_call x0 -> x5, Pallas kernels: none -> 34.2 us  [the longest x2 27.8 us: attend(): pl.pallas_call(functools.partial(attend_kernel, shape), out_shape=[out] *...]
    ppermute x0 -> x22, starting transfers between devices: none -> 33.9 us  [the longest x18 31.7 us: over_groups(): return lax.ppermute(value, 'cubes', pairs)]
  transfers between devices with their start and end apart: 11 -> 22, of which waited for: 11 -> 8; matrix products, arithmetic and copies ran while one was open for 3% -> 5% of each run, Pallas kernels for 0% -> 24%
where the time goes in v1:
time: 122 us; the launch traced here: 121 us
  waiting for transfers between devices  43.9 us (36%)
  Pallas kernels  34.2 us (28%)
  starting transfers between devices  33.9 us (28%)
  local copies, waits for them, and re-layouts  7.38 us (6%)
  other arithmetic  1.83 us (2%)
    ppermute x18, waiting for transfers between devices, over_groups(): return lax.ppermute(value, 'cubes', pairs)  35.9 us
    ppermute x18, starting transfers between devices, over_groups(): return lax.ppermute(value, 'cubes', pairs)  31.7 us
    pallas_call x2, Pallas kernels, attend(): pl.pallas_call(functools.partial(attend_kernel, shape), out_shape=[out] *...  27.8 us
    ppermute x4, waiting for transfers between devices, over_ring(): return lax.ppermute(value, 'cubes', [(i, i ^ step) for i in range(devices)])  7.99 us
    unnamed x55, local copies, waits for them, and re-layouts  5.48 us
    pallas_call x2, Pallas kernels, pack(): pl.pallas_call(functools.partial(pack_kernel, spans, width), out_shape=[j...  4.4 us
  transfers between devices with their start and end apart: 22, of which 8 were waited for; matrix products, arithmetic and copies ran while one was open for 5% of the time, Pallas kernels for 24%

profile of v1, /device:TPU:0, one launch (start us, length us, event | category | flops | bytes accessed | tf_op | source)
XLA Modules:
  0.0 121.4 jit_solution(5069797270598171262)
XLA Ops:
  0.0 2.4 %pack.3 = (bf16[256,384]{1,0:T(8,128)(2,1)}, bf16[256,384]{1,0:T(8,128)(2,1)}, bf16[256,384]{1,0:T(8,128)(2,1)}, bf16[256,384]{1,0:T(8,128)(2,1)}, bf16[256,256]...) custom-call(s32[1]{0:T(128)} %bitcast.index_ref, ...), custom_call_target="tpu_custom_call" | custom-call | tf_op jit(solution)/shard_map/pack/pallas_call | solution.py:36
  2.5 3.1 %collective-permute-start.3 = (bf16[256,384]{1,0:T(8,128)(2,1)}, bf16[256,384]{1,0:T(8,128)(2,1)S(1)}, u32[]{:S(2)}, u32[]{:S(2)}) collective-permute-start(bf16[256,384]{1,0:T(8,128)(2,1)} %get-tuple-element.34), channel_id=1, source_target_pairs={{0,4},{1,5},{2,6},{3,7},{4,0},{5,1},{6,2},{7,3},{8,12},{9,13},{10,... | collective-permute-start | bytes 589832 | tf_op jit(solution)/shard_map/ppermute | solution.py:194
  5.6 2.6 %collective-permute-start.4 = (bf16[256,384]{1,0:T(8,128)(2,1)}, bf16[256,384]{1,0:T(8,128)(2,1)S(1)}, u32[]{:S(2)}, u32[]{:S(2)}) collective-permute-start(bf16[256,384]{1,0:T(8,128)(2,1)} %get-tuple-element.35), channel_id=1, source_target_pairs={{0,8},{1,9},{2,10},{3,11},{4,12},{5,13},{6,14},{7,15},{8,0},{9,1},... | collective-permute-start | bytes 589832 | tf_op jit(solution)/shard_map/ppermute | solution.py:194
  8.2 6.0 %collective-permute-done.3 = bf16[256,384]{1,0:T(8,128)(2,1)S(1)} collective-permute-done((bf16[256,384]{1,0:T(8,128)(2,1)}, bf16[256,384]{1,0:T(8,128)(2,1)S(1)}, u32[]{:S(2)}, u32[]{:S(2)}) %collective-permute-start.3) | collective-permute-done | bytes 196640 | tf_op jit(solution)/shard_map/ppermute | solution.py:194
  14.2 8.7 %collective-permute-done.4 = bf16[256,384]{1,0:T(8,128)(2,1)S(1)} collective-permute-done((bf16[256,384]{1,0:T(8,128)(2,1)}, bf16[256,384]{1,0:T(8,128)(2,1)S(1)}, u32[]{:S(2)}, u32[]{:S(2)}) %collective-permute-start.4) | collective-permute-done | bytes 196640 | tf_op jit(solution)/shard_map/ppermute | solution.py:194
  22.9 1.0 pad_maximum_fusion
  23.9 1.6 %collective-permute-start.6 = (bf16[1024,384]{1,0:T(8,128)(2,1)S(1)}, bf16[1024,384]{1,0:T(8,128)(2,1)S(1)}, u32[]{:S(2)}, u32[]{:S(2)}) collective-permute-start(bf16[1024,384]{1,0:T(8,128)(2,1)S(1)} %pad_maximum_fusion), channel_id=1, source_target_pairs={{0,2},{1,3},{2,0},{3,1},{4,6},{5,7},{6,4},{7,5},{8,10},{9,11},{10,... | collective-permute-start | bytes 2359304 | tf_op jit(solution)/shard_map/ppermute | solution.py:197
  25.5 3.4 %collective-permute-start.14 = (bf16[256,256]{1,0:T(8,128)(2,1)S(1)}, bf16[256,256]{1,0:T(8,128)(2,1)S(1)}, u32[]{:S(2)}, u32[]{:S(2)}) collective-permute-start(bf16[256,256]{1,0:T(8,128)(2,1)S(1)} %copy-done.19), channel_id=1, source_target_pairs={{0,4},{1,5},{2,6},{3,7},{4,0},{5,1},{6,2},{7,3},{8,12},{9,13},{10,... | collective-permute-start | bytes 393224 | tf_op jit(solution)/shard_map/ppermute | solution.py:194
  28.9 1.1 collective-permute-start.15
  30.0 1.5 %collective-permute-start.16 = (bf16[256,256]{1,0:T(8,128)(2,1)S(1)}, bf16[256,256]{1,0:T(8,128)(2,1)S(1)}, u32[]{:S(2)}, u32[]{:S(2)}) collective-permute-start(bf16[256,256]{1,0:T(8,128)(2,1)S(1)} %copy-done.17), channel_id=1, source_target_pairs={{0,12},{1,13},{2,14},{3,15},{4,8},{5,9},{6,10},{7,11},{8,4},{9,5},... | collective-permute-start | bytes 393224 | tf_op jit(solution)/shard_map/ppermute | solution.py:194
  31.4 1.8 %collective-permute-done.14 = bf16[256,256]{1,0:T(8,128)(2,1)S(1)} collective-permute-done((bf16[256,256]{1,0:T(8,128)(2,1)S(1)}, bf16[256,256]{1,0:T(8,128)(2,1)S(1)}, u32[]{:S(2)}, u32[]{:S(2)}) %collective-permute-start.14) | collective-permute-done | bytes 131104 | tf_op jit(solution)/shard_map/ppermute | solution.py:194
  33.2 7.2 %collective-permute-done.15 = bf16[256,256]{1,0:T(8,128)(2,1)S(1)} collective-permute-done((bf16[256,256]{1,0:T(8,128)(2,1)S(1)}, bf16[256,256]{1,0:T(8,128)(2,1)S(1)}, u32[]{:S(2)}, u32[]{:S(2)}) %collective-permute-start.15) | collective-permute-done | bytes 131104 | tf_op jit(solution)/shard_map/ppermute | solution.py:194
  41.2 1.6 %collective-permute-done.6 = bf16[1024,384]{1,0:T(8,128)(2,1)S(1)} collective-permute-done((bf16[1024,384]{1,0:T(8,128)(2,1)S(1)}, bf16[1024,384]{1,0:T(8,128)(2,1)S(1)}, u32[]{:S(2)}, u32[]{:S(2)}) %collective-permute-start.6) | collective-permute-done | bytes 786464 | tf_op jit(solution)/shard_map/ppermute | solution.py:197
  43.1 0.7 constant_dynamic-update-slice_fusion.9
  45.7 6.4 %collective-permute-done.17 = bf16[1024,256]{1,0:T(8,128)(2,1)S(1)} collective-permute-done((bf16[1024,256]{1,0:T(8,128)(2,1)S(1)}, bf16[1024,256]{1,0:T(8,128)(2,1)S(1)}, u32[]{:S(2)}, u32[]{:S(2)}) %collective-permute-start.17) | collective-permute-done | bytes 524320 | tf_op jit(solution)/shard_map/ppermute | solution.py:197
  52.1 0.8 constant_dynamic-update-slice_fusion.5.refs_4_
  53.6 2.0 %pack.2 = (bf16[136,384]{1,0:T(8,128)(2,1)}, bf16[136,384]{1,0:T(8,128)(2,1)}, bf16[136,384]{1,0:T(8,128)(2,1)}, bf16[136,384]{1,0:T(8,128)(2,1)}, bf16[136,256]...) custom-call(s32[1]{0:T(128)} %bitcast.index_ref, ...), custom_call_target="tpu_custom_call" | custom-call | tf_op jit(solution)/shard_map/pack/pallas_call | solution.py:36
  55.5 4.7 %collective-permute-start.11 = (bf16[136,256]{1,0:T(8,128)(2,1)}, bf16[136,256]{1,0:T(8,128)(2,1)S(1)}, u32[]{:S(2)}, u32[]{:S(2)}) collective-permute-start(bf16[136,256]{1,0:T(8,128)(2,1)} %get-tuple-element.42), channel_id=1, source_target_pairs={{0,4},{1,5},{2,6},{3,7},{4,0},{5,1},{6,2},{7,3},{8,12},{9,13},{10,... | collective-permute-start | bytes 208904 | tf_op jit(solution)/shard_map/ppermute | solution.py:194
  60.2 1.1 collective-permute-start.12
  61.3 1.4 %collective-permute-start.13 = (bf16[136,256]{1,0:T(8,128)(2,1)}, bf16[136,256]{1,0:T(8,128)(2,1)}, u32[]{:S(2)}, u32[]{:S(2)}) collective-permute-start(bf16[136,256]{1,0:T(8,128)(2,1)} %get-tuple-element.44), channel_id=1, source_target_pairs={{0,12},{1,13},{2,14},{3,15},{4,8},{5,9},{6,10},{7,11},{8,4},{9,5},... | collective-permute-start | bytes 208904 | tf_op jit(solution)/shard_map/ppermute | solution.py:194
  63.3 2.1 %collective-permute-start = (bf16[136,384]{1,0:T(8,128)(2,1)}, bf16[136,384]{1,0:T(8,128)(2,1)S(1)}, u32[]{:S(2)}, u32[]{:S(2)}) collective-permute-start(bf16[136,384]{1,0:T(8,128)(2,1)} %get-tuple-element.30), channel_id=1, source_target_pairs={{0,4},{1,5},{2,6},{3,7},{4,0},{5,1},{6,2},{7,3},{8,12},{9,13},{10,... | collective-permute-start | bytes 313352 | tf_op jit(solution)/shard_map/ppermute | solution.py:194
  65.5 3.6 %collective-permute-done.12.refs_2_ = bf16[136,256]{1,0:T(8,128)(2,1)S(1)} collective-permute-done((bf16[136,256]{1,0:T(8,128)(2,1)}, bf16[136,256]{1,0:T(8,128)(2,1)S(1)}, u32[]{:S(2)}, u32[]{:S(2)}) %collective-permute-start.12) | collective-permute-done | bytes 69664 | tf_op jit(solution)/shard_map/ppermute | solution.py:194
  69.7 2.4 %collective-permute-start.2 = (bf16[136,384]{1,0:T(8,128)(2,1)}, bf16[136,384]{1,0:T(8,128)(2,1)S(1)}, u32[]{:S(2)}, u32[]{:S(2)}) collective-permute-start(bf16[136,384]{1,0:T(8,128)(2,1)} %get-tuple-element.32), channel_id=1, source_target_pairs={{0,12},{1,13},{2,14},{3,15},{4,8},{5,9},{6,10},{7,11},{8,4},{9,5},... | collective-permute-start | bytes 313352 | tf_op jit(solution)/shard_map/ppermute | solution.py:194
  72.1 0.7 pad_add_fusion.tables_ref
  72.8 11.6 %attend.3 = (bf16[128,256]{1,0:T(8,128)(2,1)}, bf16[128,256]{1,0:T(8,128)(2,1)}, bf16[128,256]{1,0:T(8,128)(2,1)}, bf16[128,256]{1,0:T(8,128)(2,1)}) custom-call(s32[353]{0:T(512)} %pad_add_fusion.tables_ref, bf16[136,256]{1,0:T(8,128)(2,1)} %get-tuple-element.41.refs_0_, bf16[136,256]{1,0:T(8,128)(2,1)} %copy-done.11, bf16[136,256]{1,0:T(8,128)(2,1)} %copy-done.12, ...), custom_call_target="tpu_custom_call" | custom-call | flops 268435456 | bytes 2097152 | tf_op jit(solution)/shard_map/attend/pallas_call | solution.py:151
  84.4 1.4 %collective-permute-start.19 = (bf16[128,256]{1,0:T(8,128)(2,1)}, bf16[128,256]{1,0:T(8,128)(2,1)S(1)}, u32[]{:S(2)}, u32[]{:S(2)}) collective-permute-start(bf16[128,256]{1,0:T(8,128)(2,1)} %get-tuple-element.50), channel_id=1, source_target_pairs={{0,4},{1,5},{2,6},{3,7},{4,0},{5,1},{6,2},{7,3},{8,12},{9,13},{10,... | collective-permute-start | bytes 196616 | tf_op jit(solution)/shard_map/ppermute | solution.py:194
  87.1 16.1 %attend.2 = (bf16[128,384]{1,0:T(8,128)(2,1)}, bf16[128,384]{1,0:T(8,128)(2,1)}, bf16[128,384]{1,0:T(8,128)(2,1)}, bf16[128,384]{1,0:T(8,128)(2,1)}) custom-call(s32[353]{0:T(512)} %pad_add_fusion.tables_ref, bf16[136,384]{1,0:T(8,128)(2,1)} %get-tuple-element.29.refs_0_, bf16[136,384]{1,0:T(8,128)(2,1)} %copy-done.4, bf16[136,384]{1,0:T(8,128)(2,1)} %copy-done.5, ...), custom_call_target="tpu_custom_call" | custom-call | flops 402653184 | bytes 3145728 | tf_op jit(solution)/shard_map/attend/pallas_call | solution.py:151
  103.2 1.6 %collective-permute-start.10 = (bf16[128,384]{1,0:T(8,128)(2,1)}, bf16[128,384]{1,0:T(8,128)(2,1)S(1)}, u32[]{:S(2)}, u32[]{:S(2)}) collective-permute-start(bf16[128,384]{1,0:T(8,128)(2,1)} %get-tuple-element.40), channel_id=1, source_target_pairs={{0,12},{1,13},{2,14},{3,15},{4,8},{5,9},{6,10},{7,11},{8,4},{9,5},... | collective-permute-start | bytes 294920 | tf_op jit(solution)/shard_map/ppermute | solution.py:194
  104.8 2.9 %collective-permute-start.9 = (bf16[128,384]{1,0:T(8,128)(2,1)}, bf16[128,384]{1,0:T(8,128)(2,1)S(1)}, u32[]{:S(2)}, u32[]{:S(2)}) collective-permute-start(bf16[128,384]{1,0:T(8,128)(2,1)} %get-tuple-element.39), channel_id=1, source_target_pairs={{0,8},{1,9},{2,10},{3,11},{4,12},{5,13},{6,14},{7,15},{8,0},{9,1},... | collective-permute-start | bytes 294920 | tf_op jit(solution)/shard_map/ppermute | solution.py:194
  107.7 2.4 %collective-permute-start.21 = (bf16[128,256]{1,0:T(8,128)(2,1)S(1)}, bf16[128,256]{1,0:T(8,128)(2,1)S(1)}, u32[]{:S(2)}, u32[]{:S(2)}) collective-permute-start(bf16[128,256]{1,0:T(8,128)(2,1)S(1)} %copy-done.20), channel_id=1, source_target_pairs={{0,12},{1,13},{2,14},{3,15},{4,8},{5,9},{6,10},{7,11},{8,4},{9,5},... | collective-permute-start | bytes 196616 | tf_op jit(solution)/shard_map/ppermute | solution.py:194
  110.1 8.5 %collective-permute-done.20.refs_6_ = bf16[128,256]{1,0:T(8,128)(2,1)S(1)} collective-permute-done((bf16[128,256]{1,0:T(8,128)(2,1)S(1)}, bf16[128,256]{1,0:T(8,128)(2,1)S(1)}, u32[]{:S(2)}, u32[]{:S(2)}) %collective-permute-start.20) | collective-permute-done | bytes 65568 | tf_op jit(solution)/shard_map/ppermute | solution.py:194
  119.4 2.0 %unpack.1 = bf16[128,2560]{1,0:T(8,128)(2,1)} custom-call(s32[1]{0:T(128)} %bitcast.index_ref, bf16[128,384]{1,0:T(8,128)(2,1)} %get-tuple-element.37.refs_0_, bf16[128,384]{1,0:T(8,128)(2,1)} %copy-done.8, bf16[128,384]{1,0:T(8,128)(2,1)} %copy-done.9, bf16[128,384]{1,0:T(8,128)(2,1)} %copy-done.7, bf16[128,256]{1,0:T(8,128)(2,1)} %get-tuple-element.49.refs_4_, ...), custom_call_target="tpu_custom_call" | custom-call | tf_op jit(solution)/shard_map/unpack/pallas_call | solution.py:53
  (84 shorter events, 6.8 us)
Async XLA Ops:
  2.4 23.0 %copy-start.19 = (bf16[256,256]{1,0:T(8,128)(2,1)S(1)}, bf16[256,256]{1,0:T(8,128)(2,1)}, u32[]{:S(2)}) copy-start(bf16[256,256]{1,0:T(8,128)(2,1)} %get-tuple-element.46) | copy-start | bytes 393220
  2.4 26.4 %copy-start.18 = (bf16[256,256]{1,0:T(8,128)(2,1)S(1)}, bf16[256,256]{1,0:T(8,128)(2,1)}, u32[]{:S(2)}) copy-start(bf16[256,256]{1,0:T(8,128)(2,1)} %get-tuple-element.47) | copy-start | bytes 393220
  2.4 27.5 %copy-start.17 = (bf16[256,256]{1,0:T(8,128)(2,1)S(1)}, bf16[256,256]{1,0:T(8,128)(2,1)}, u32[]{:S(2)}) copy-start(bf16[256,256]{1,0:T(8,128)(2,1)} %get-tuple-element.48) | copy-start | bytes 393220
  2.4 29.0 %copy-start.2 = (bf16[256,384]{1,0:T(8,128)(2,1)S(1)}, bf16[256,384]{1,0:T(8,128)(2,1)}, u32[]{:S(2)}) copy-start(bf16[256,384]{1,0:T(8,128)(2,1)} %get-tuple-element.33) | copy-start | bytes 589828
  2.5 38.0 %copy-start.3 = (bf16[256,256]{1,0:T(8,128)(2,1)S(1)}, bf16[256,256]{1,0:T(8,128)(2,1)}, u32[]{:S(2)}) copy-start(bf16[256,256]{1,0:T(8,128)(2,1)} %get-tuple-element.45) | copy-start | bytes 393220
  2.5 11.7 %collective-permute-start.3 = (bf16[256,384]{1,0:T(8,128)(2,1)}, bf16[256,384]{1,0:T(8,128)(2,1)S(1)}, u32[]{:S(2)}, u32[]{:S(2)}) collective-permute-start(bf16[256,384]{1,0:T(8,128)(2,1)} %get-tuple-element.34), channel_id=1, source_target_pairs={{0,4},{1,5},{2,6},{3,7},{4,0},{5,1},{6,2},{7,3},{8,12},{9,13},{10,... | collective-permute-start | bytes 589832 | tf_op jit(solution)/shard_map/ppermute | solution.py:194
  5.6 17.3 %collective-permute-start.4 = (bf16[256,384]{1,0:T(8,128)(2,1)}, bf16[256,384]{1,0:T(8,128)(2,1)S(1)}, u32[]{:S(2)}, u32[]{:S(2)}) collective-permute-start(bf16[256,384]{1,0:T(8,128)(2,1)} %get-tuple-element.35), channel_id=1, source_target_pairs={{0,8},{1,9},{2,10},{3,11},{4,12},{5,13},{6,14},{7,15},{8,0},{9,1},... | collective-permute-start | bytes 589832 | tf_op jit(solution)/shard_map/ppermute | solution.py:194
  8.2 14.7 %collective-permute-start.5 = (bf16[256,384]{1,0:T(8,128)(2,1)}, bf16[256,384]{1,0:T(8,128)(2,1)S(1)}, u32[]{:S(2)}, u32[]{:S(2)}) collective-permute-start(bf16[256,384]{1,0:T(8,128)(2,1)} %get-tuple-element.36), channel_id=1, source_target_pairs={{0,12},{1,13},{2,14},{3,15},{4,8},{5,9},{6,10},{7,11},{8,4},{9,5},... | collective-permute-start | bytes 589832 | tf_op jit(solution)/shard_map/ppermute | solution.py:194
  23.9 18.9 %collective-permute-start.6 = (bf16[1024,384]{1,0:T(8,128)(2,1)S(1)}, bf16[1024,384]{1,0:T(8,128)(2,1)S(1)}, u32[]{:S(2)}, u32[]{:S(2)}) collective-permute-start(bf16[1024,384]{1,0:T(8,128)(2,1)S(1)} %pad_maximum_fusion), channel_id=1, source_target_pairs={{0,2},{1,3},{2,0},{3,1},{4,6},{5,7},{6,4},{7,5},{8,10},{9,11},{10,... | collective-permute-start | bytes 2359304 | tf_op jit(solution)/shard_map/ppermute | solution.py:197
  25.5 7.7 %collective-permute-start.14 = (bf16[256,256]{1,0:T(8,128)(2,1)S(1)}, bf16[256,256]{1,0:T(8,128)(2,1)S(1)}, u32[]{:S(2)}, u32[]{:S(2)}) collective-permute-start(bf16[256,256]{1,0:T(8,128)(2,1)S(1)} %copy-done.19), channel_id=1, source_target_pairs={{0,4},{1,5},{2,6},{3,7},{4,0},{5,1},{6,2},{7,3},{8,12},{9,13},{10,... | collective-permute-start | bytes 393224 | tf_op jit(solution)/shard_map/ppermute | solution.py:194
  28.9 11.6 %collective-permute-start.15 = (bf16[256,256]{1,0:T(8,128)(2,1)S(1)}, bf16[256,256]{1,0:T(8,128)(2,1)S(1)}, u32[]{:S(2)}, u32[]{:S(2)}) collective-permute-start(bf16[256,256]{1,0:T(8,128)(2,1)S(1)} %copy-done.18), channel_id=1, source_target_pairs={{0,8},{1,9},{2,10},{3,11},{4,12},{5,13},{6,14},{7,15},{8,0},{9,1},... | collective-permute-start | bytes 393224 | tf_op jit(solution)/shard_map/ppermute | solution.py:194
  30.0 10.5 %collective-permute-start.16 = (bf16[256,256]{1,0:T(8,128)(2,1)S(1)}, bf16[256,256]{1,0:T(8,128)(2,1)S(1)}, u32[]{:S(2)}, u32[]{:S(2)}) collective-permute-start(bf16[256,256]{1,0:T(8,128)(2,1)S(1)} %copy-done.17), channel_id=1, source_target_pairs={{0,12},{1,13},{2,14},{3,15},{4,8},{5,9},{6,10},{7,11},{8,4},{9,5},... | collective-permute-start | bytes 393224 | tf_op jit(solution)/shard_map/ppermute | solution.py:194
  40.5 11.6 %collective-permute-start.17 = (bf16[1024,256]{1,0:T(8,128)(2,1)S(1)}, bf16[1024,256]{1,0:T(8,128)(2,1)S(1)}, u32[]{:S(2)}, u32[]{:S(2)}) collective-permute-start(bf16[1024,256]{1,0:T(8,128)(2,1)S(1)} %pad_maximum_fusion.1), channel_id=1, source_target_pairs={{0,2},{1,3},{2,0},{3,1},{4,6},{5,7},{6,4},{7,5},{8,10},{9,11},{10,... | collective-permute-start | bytes 1572872 | tf_op jit(solution)/shard_map/ppermute | solution.py:197
  43.0 20.0 %copy-start = (bf16[2048,384]{1,0:T(8,128)(2,1)}, bf16[2048,384]{1,0:T(8,128)(2,1)S(1)}, u32[]{:S(2)}) copy-start(bf16[2048,384]{1,0:T(8,128)(2,1)S(1)} %constant_dynamic-update-slice_fusion.refs_4_) | copy-start | bytes 4718596
  43.0 19.7 %copy-start.10 = (s32[32,20,8]{0,2,1:T(8,128)S(1)}, s32[32,20,8]{0,2,1:T(8,128)}, u32[]{:S(2)}) copy-start(s32[32,20,8]{0,2,1:T(8,128)} %param.10) | copy-start | bytes 61444
  43.0 42.9 %collective-permute-start.7 = (bf16[2048,384]{1,0:T(8,128)(2,1)S(1)}, bf16[2048,384]{1,0:T(8,128)(2,1)S(1)}, u32[]{:S(2)}, u32[]{:S(2)}) collective-permute-start(bf16[2048,384]{1,0:T(8,128)(2,1)S(1)} %constant_dynamic-update-slice_fusion.refs_4_), channel_id=1, source_target_pairs={{0,1},{1,0},{2,3},{3,2},{4,5},{5,4},{6,7},{7,6},{8,9},{9,8},{10,11... | collective-permute-start | bytes 4718600 | tf_op jit(solution)/shard_map/ppermute | solution.py:197
  43.7 19.5 %copy-start.22 = (s32[32]{0:T(128)S(1)}, s32[32]{0:T(128)}, u32[]{:S(2)}) copy-start(s32[32]{0:T(128)} %param.11) | copy-start | bytes 388
  52.9 19.8 %collective-permute-start.18 = (bf16[2048,256]{1,0:T(8,128)(2,1)}, bf16[2048,256]{1,0:T(8,128)(2,1)}, u32[]{:S(2)}, u32[]{:S(2)}) collective-permute-start(bf16[2048,256]{1,0:T(8,128)(2,1)} %constant_dynamic-update-slice_fusion.5.refs_4_), channel_id=1, source_target_pairs={{0,1},{1,0},{2,3},{3,2},{4,5},{5,4},{6,7},{7,6},{8,9},{9,8},{10,11... | collective-permute-start | bytes 3145736 | tf_op jit(solution)/shard_map/ppermute | solution.py:197
  55.5 7.8 %collective-permute-start.11 = (bf16[136,256]{1,0:T(8,128)(2,1)}, bf16[136,256]{1,0:T(8,128)(2,1)S(1)}, u32[]{:S(2)}, u32[]{:S(2)}) collective-permute-start(bf16[136,256]{1,0:T(8,128)(2,1)} %get-tuple-element.42), channel_id=1, source_target_pairs={{0,4},{1,5},{2,6},{3,7},{4,0},{5,1},{6,2},{7,3},{8,12},{9,13},{10,... | collective-permute-start | bytes 208904 | tf_op jit(solution)/shard_map/ppermute | solution.py:194
  60.2 8.8 %collective-permute-start.12 = (bf16[136,256]{1,0:T(8,128)(2,1)}, bf16[136,256]{1,0:T(8,128)(2,1)S(1)}, u32[]{:S(2)}, u32[]{:S(2)}) collective-permute-start(bf16[136,256]{1,0:T(8,128)(2,1)} %get-tuple-element.43), channel_id=1, source_target_pairs={{0,8},{1,9},{2,10},{3,11},{4,12},{5,13},{6,14},{7,15},{8,0},{9,1},... | collective-permute-start | bytes 208904 | tf_op jit(solution)/shard_map/ppermute | solution.py:194
  61.3 7.8 %collective-permute-start.13 = (bf16[136,256]{1,0:T(8,128)(2,1)}, bf16[136,256]{1,0:T(8,128)(2,1)}, u32[]{:S(2)}, u32[]{:S(2)}) collective-permute-start(bf16[136,256]{1,0:T(8,128)(2,1)} %get-tuple-element.44), channel_id=1, source_target_pairs={{0,12},{1,13},{2,14},{3,15},{4,8},{5,9},{6,10},{7,11},{8,4},{9,5},... | collective-permute-start | bytes 208904 | tf_op jit(solution)/shard_map/ppermute | solution.py:194
  63.3 22.5 %collective-permute-start = (bf16[136,384]{1,0:T(8,128)(2,1)}, bf16[136,384]{1,0:T(8,128)(2,1)S(1)}, u32[]{:S(2)}, u32[]{:S(2)}) collective-permute-start(bf16[136,384]{1,0:T(8,128)(2,1)} %get-tuple-element.30), channel_id=1, source_target_pairs={{0,4},{1,5},{2,6},{3,7},{4,0},{5,1},{6,2},{7,3},{8,12},{9,13},{10,... | collective-permute-start | bytes 313352 | tf_op jit(solution)/shard_map/ppermute | solution.py:194
  69.1 16.7 %collective-permute-start.1 = (bf16[136,384]{1,0:T(8,128)(2,1)}, bf16[136,384]{1,0:T(8,128)(2,1)S(1)}, u32[]{:S(2)}, u32[]{:S(2)}) collective-permute-start(bf16[136,384]{1,0:T(8,128)(2,1)} %get-tuple-element.31), channel_id=1, source_target_pairs={{0,8},{1,9},{2,10},{3,11},{4,12},{5,13},{6,14},{7,15},{8,0},{9,1},... | collective-permute-start | bytes 313352 | tf_op jit(solution)/shard_map/ppermute | solution.py:194
  69.7 16.1 %collective-permute-start.2 = (bf16[136,384]{1,0:T(8,128)(2,1)}, bf16[136,384]{1,0:T(8,128)(2,1)S(1)}, u32[]{:S(2)}, u32[]{:S(2)}) collective-permute-start(bf16[136,384]{1,0:T(8,128)(2,1)} %get-tuple-element.32), channel_id=1, source_target_pairs={{0,12},{1,13},{2,14},{3,15},{4,8},{5,9},{6,10},{7,11},{8,4},{9,5},... | collective-permute-start | bytes 313352 | tf_op jit(solution)/shard_map/ppermute | solution.py:194
  84.4 23.3 %collective-permute-start.19 = (bf16[128,256]{1,0:T(8,128)(2,1)}, bf16[128,256]{1,0:T(8,128)(2,1)S(1)}, u32[]{:S(2)}, u32[]{:S(2)}) collective-permute-start(bf16[128,256]{1,0:T(8,128)(2,1)} %get-tuple-element.50), channel_id=1, source_target_pairs={{0,4},{1,5},{2,6},{3,7},{4,0},{5,1},{6,2},{7,3},{8,12},{9,13},{10,... | collective-permute-start | bytes 196616 | tf_op jit(solution)/shard_map/ppermute | solution.py:194
  87.1 20.6 %copy-start.21 = (bf16[128,256]{1,0:T(8,128)(2,1)S(1)}, bf16[128,256]{1,0:T(8,128)(2,1)}, u32[]{:S(2)}) copy-start(bf16[128,256]{1,0:T(8,128)(2,1)} %get-tuple-element.51) | copy-start | bytes 196612
  87.1 20.7 %copy-start.20 = (bf16[128,256]{1,0:T(8,128)(2,1)S(1)}, bf16[128,256]{1,0:T(8,128)(2,1)}, u32[]{:S(2)}) copy-start(bf16[128,256]{1,0:T(8,128)(2,1)} %get-tuple-element.52) | copy-start | bytes 196612
  103.2 15.4 %collective-permute-start.10 = (bf16[128,384]{1,0:T(8,128)(2,1)}, bf16[128,384]{1,0:T(8,128)(2,1)S(1)}, u32[]{:S(2)}, u32[]{:S(2)}) collective-permute-start(bf16[128,384]{1,0:T(8,128)(2,1)} %get-tuple-element.40), channel_id=1, source_target_pairs={{0,12},{1,13},{2,14},{3,15},{4,8},{5,9},{6,10},{7,11},{8,4},{9,5},... | collective-permute-start | bytes 294920 | tf_op jit(solution)/shard_map/ppermute | solution.py:194
  104.8 13.9 %collective-permute-start.8 = (bf16[128,384]{1,0:T(8,128)(2,1)}, bf16[128,384]{1,0:T(8,128)(2,1)S(1)}, u32[]{:S(2)}, u32[]{:S(2)}) collective-permute-start(bf16[128,384]{1,0:T(8,128)(2,1)} %get-tuple-element.38), channel_id=1, source_target_pairs={{0,4},{1,5},{2,6},{3,7},{4,0},{5,1},{6,2},{7,3},{8,12},{9,13},{10,... | collective-permute-start | bytes 294920 | tf_op jit(solution)/shard_map/ppermute | solution.py:194
  104.8 13.9 %collective-permute-start.9 = (bf16[128,384]{1,0:T(8,128)(2,1)}, bf16[128,384]{1,0:T(8,128)(2,1)S(1)}, u32[]{:S(2)}, u32[]{:S(2)}) collective-permute-start(bf16[128,384]{1,0:T(8,128)(2,1)} %get-tuple-element.39), channel_id=1, source_target_pairs={{0,8},{1,9},{2,10},{3,11},{4,12},{5,13},{6,14},{7,15},{8,0},{9,1},... | collective-permute-start | bytes 294920 | tf_op jit(solution)/shard_map/ppermute | solution.py:194
  107.7 11.0 %collective-permute-start.20 = (bf16[128,256]{1,0:T(8,128)(2,1)S(1)}, bf16[128,256]{1,0:T(8,128)(2,1)S(1)}, u32[]{:S(2)}, u32[]{:S(2)}) collective-permute-start(bf16[128,256]{1,0:T(8,128)(2,1)S(1)} %copy-done.21), channel_id=1, source_target_pairs={{0,8},{1,9},{2,10},{3,11},{4,12},{5,13},{6,14},{7,15},{8,0},{9,1},... | collective-permute-start | bytes 196616 | tf_op jit(solution)/shard_map/ppermute | solution.py:194
  107.7 10.9 %collective-permute-start.21 = (bf16[128,256]{1,0:T(8,128)(2,1)S(1)}, bf16[128,256]{1,0:T(8,128)(2,1)S(1)}, u32[]{:S(2)}, u32[]{:S(2)}) collective-permute-start(bf16[128,256]{1,0:T(8,128)(2,1)S(1)} %copy-done.20), channel_id=1, source_target_pairs={{0,12},{1,13},{2,14},{3,15},{4,8},{5,9},{6,10},{7,11},{8,4},{9,5},... | collective-permute-start | bytes 196616 | tf_op jit(solution)/shard_map/ppermute | solution.py:194
  (13 other events, 39.3 us)

commit v2 on v1

v2 whole, which is shorter than its diff:
```python
import functools
import math

import jax
import jax.numpy as jnp
from jax import lax
from jax.experimental import pallas as pl
from jax.experimental.pallas import tpu as pltpu
from jax.sharding import PartitionSpec as P


CUBE = 64
GATE_ROWS = 8
CHUNKS = (3, 2)
POOL_ROWS = 1024
HELD_BYTES = 8 << 20
LOG2E = 1.4426950408889634

VMEM = pl.BlockSpec(memory_space=pltpu.VMEM)
SMEM = pl.BlockSpec(memory_space=pltpu.SMEM)
ANY = pl.BlockSpec(memory_space=pl.ANY)
TRANSPOSED = (((1,), (1,)), ((), ()))


def pack_kernel(jobs, width, index_ref, *refs):
    sources = refs[: 1 + max(max(rows) for rows, _ in jobs)]
    outputs = iter(refs[len(sources) :])
    for numbers, spans in jobs:
        for relative, begin, size in spans:
            head_group = index_ref[0] ^ relative
            columns = pl.ds(pl.multiple_of(head_group * width + begin, 128), size)
            out, row = next(outputs), 0
            for number in numbers:
                rows = sources[number].shape[0]
                out[row : row + rows, :] = sources[number][:, columns]
                row += rows


def pack(index, jobs, width):
    operands, numbered, shapes = [], [], []
    for sources, spans in jobs:
        numbers = []
        for source in sources:
            known = [i for i, operand in enumerate(operands) if operand is source]
            numbers.append(known[0] if known else len(operands))
            if not known:
                operands.append(source)
        numbered.append((tuple(numbers), tuple(spans)))
        rows = sum(source.shape[0] for source in sources)
        shapes += [jax.ShapeDtypeStruct((rows, size), jnp.bfloat16) for _, _, size in spans]
    return pl.pallas_call(
        functools.partial(pack_kernel, tuple(numbered), width),
        out_shape=shapes,
        in_specs=[SMEM] + [VMEM] * len(operands),
        out_specs=[VMEM] * len(shapes),
        name="pack",
    )(index, *operands)


def unpack_kernel(spans, width, index_ref, *refs):
    pieces, out = refs[:-1], refs[-1]
    for (relative, begin, size), piece in zip(spans, pieces):
        head_group = index_ref[0] ^ relative
        out[:, pl.ds(pl.multiple_of(head_group * width + begin, 128), size)] = piece[...]


def unpack(index, pieces, spans, width, columns):
    return pl.pallas_call(
        functools.partial(unpack_kernel, spans, width),
        out_shape=jax.ShapeDtypeStruct((pieces[0].shape[0], columns), jnp.bfloat16),
        in_specs=[SMEM] + [VMEM] * len(pieces),
        out_specs=VMEM,
        name="unpack",
    )(index, *pieces)


def attend_kernel(shape, tables_ref, *refs):
    groups, local, cubes, heads, first, count, picks, head_size, query_bases, store_bases = shape
    queries = refs[:groups]
    stores = refs[groups : groups + len(store_bases)]
    outs = refs[groups + len(store_bases) : 2 * groups + len(store_bases)]
    (
        held,
        pool_mask,
        pooled_keys,
        pooled_values,
        query_all,
        gate_columns,
        coarse_part,
        scores_buffer,
        weights_buffer,
        mixed_all,
        sems,
    ) = refs[2 * groups + len(store_bases) :]
    tokens = local * CUBE
    units = groups * local
    slots = held.shape[0]
    scale = LOG2E / math.sqrt(head_size)
    tile_rows = pool_mask.shape[1]
    tile_blocks = pool_mask.shape[0] // 2
    tiles = held.shape[1] // tile_rows

    def copies(head):
        slot = head % slots
        row, result = 0, []
        for i, (store, base) in enumerate(zip(stores, store_bases)):
            rows = store.shape[0]
            source = store.at[:, pl.ds(base + head * head_size, head_size)]
            target = held.at[slot, pl.ds(row, rows), :]
            result.append(pltpu.make_async_copy(source, target, sems.at[slot, i]))
            row += rows
        return result

    for head in range(min(slots, count)):
        for copy in copies(head):
            copy.start()
    home = tables_ref[cubes + units * heads * picks]
    mask_block = lax.broadcasted_iota(jnp.int32, pool_mask.shape, 0)
    is_value = mask_block >= tile_blocks
    mask_block = jnp.where(is_value, mask_block - tile_blocks, mask_block)
    mask_start = (mask_block + lax.div(mask_block, local) * local) * CUBE
    mask_start = jnp.where(is_value, mask_start + tokens, mask_start)
    mask_row = lax.broadcasted_iota(jnp.int32, pool_mask.shape, 1)
    inside = jnp.logical_and(mask_row >= mask_start, mask_row < mask_start + CUBE)
    pool_mask[...] = jnp.where(inside, 1.0, 0.0).astype(jnp.bfloat16)
    for group in range(groups):
        base = query_bases[group]
        rows = slice(group * tokens, (group + 1) * tokens)
        query_all[rows, :] = queries[group][:tokens, base : base + count * head_size]
    ones = jnp.ones((picks * CUBE, head_size), jnp.bfloat16)

    for head in range(count):
        slot = head % slots
        columns = slice(head * head_size, (head + 1) * head_size)
        for group in range(groups):
            base = query_bases[group] + head * head_size
            gate_rows = queries[group][tokens : tokens + GATE_ROWS, base : base + head_size]
            gate_rows = jax.nn.sigmoid(gate_rows.astype(jnp.float32))
            gate_columns[group * tokens : (group + 1) * tokens, :] = jnp.transpose(gate_rows)
        for copy in copies(head):
            copy.wait()
        for tile in range(0, tiles, 2):
            pair = [held[slot, t * tile_rows : (t + 1) * tile_rows, :] for t in (tile, tile + 1)]
            sums = jnp.dot(
                pool_mask[...], jnp.concatenate(pair, axis=1), preferred_element_type=jnp.float32
            )
            means = (sums * (1.0 / CUBE)).astype(jnp.bfloat16)
            for t in (0, 1):
                rows = slice((tile + t) * tile_blocks, (tile + t + 1) * tile_blocks)
                part = means[:, t * head_size : (t + 1) * head_size]
                pooled_keys[rows, :] = part[:tile_blocks]
                pooled_values[rows, :head_size] = part[tile_blocks:]
        pooled_values[:, head_size:] = ones[:cubes] if cubes <= picks * CUBE else jnp.ones(
            (cubes, head_size), jnp.bfloat16
        )
        for group in range(groups):
            rows = slice(group * tokens, (group + 1) * tokens)
            scores = lax.dot_general(
                query_all[rows, columns],
                pooled_keys[...],
                TRANSPOSED,
                preferred_element_type=jnp.float32,
            )
            top = jnp.max(scores, axis=1, keepdims=True)
            weights = jnp.exp2((scores - top) * scale).astype(jnp.bfloat16)
            sums = jnp.dot(weights, pooled_values[...], preferred_element_type=jnp.float32)
            gate = gate_columns[rows, 0:1]
            coarse_part[rows, :] = sums[:, :head_size] * (gate / sums[:, head_size:])

        def unit_starts(unit):
            block = ((home ^ (unit // local)) * local + unit % local) * heads
            base = cubes + (block + first + head) * picks
            return [
                pl.multiple_of(tables_ref[tables_ref[base + pick]], CUBE) for pick in range(picks)
            ]

        def score_stage(unit):
            keys = [held[slot, pl.ds(start, CUBE), :] for start in unit_starts(unit)]
            scores_buffer[unit % 2] = lax.dot_general(
                query_all[unit * CUBE : (unit + 1) * CUBE, columns],
                jnp.concatenate(keys, axis=0),
                TRANSPOSED,
                preferred_element_type=jnp.float32,
            )

        def weight_stage(unit):
            scores = scores_buffer[unit % 2]
            top = jnp.max(scores, axis=1, keepdims=True)
            weights_buffer[unit % 2] = jnp.exp2((scores - top) * scale).astype(jnp.bfloat16)

        def value_stage(unit):
            values = [held[slot, pl.ds(start + tokens, CUBE), :] for start in unit_starts(unit)]
            values = jnp.concatenate((jnp.concatenate(values, axis=0), ones), axis=1)
            sums = jnp.dot(weights_buffer[unit % 2], values, preferred_element_type=jnp.float32)
            rows = slice(unit * CUBE, (unit + 1) * CUBE)
            gate = gate_columns[rows, 1:2]
            fine = sums[:, :head_size] * (gate / sums[:, head_size:])
            mixed_all[rows, columns] = (coarse_part[rows, :] + fine).astype(jnp.bfloat16)

        for unit in range(units + 2):
            if unit >= 2:
                value_stage(unit - 2)
            if 1 <= unit <= units:
                weight_stage(unit - 1)
            if unit < units:
                score_stage(unit)
        for group in range(groups):
            rows = slice(group * tokens, (group + 1) * tokens)
            outs[group][:, columns] = mixed_all[rows, columns]
        if head + slots < count:
            for copy in copies(head + slots):
                copy.start()


def attend(tables, queries, query_bases, stores, store_bases, sizes):
    local, cubes, heads, first, count, picks, head_size = sizes
    groups = len(queries)
    tokens = local * CUBE
    rows_all = 2 * cubes * CUBE
    tile_rows = min(POOL_ROWS, rows_all // 2)
    slots = max(2, min(count, HELD_BYTES // (2 * rows_all * head_size)))
    shape = (
        groups,
        local,
        cubes,
        heads,
        first,
        count,
        picks,
        head_size,
        tuple(query_bases),
        tuple(store_bases),
    )
    out = jax.ShapeDtypeStruct((tokens, count * head_size), jnp.bfloat16)
    units = groups * local
    return pl.pallas_call(
        functools.partial(attend_kernel, shape),
        out_shape=[out] * groups,
        in_specs=[SMEM] + [VMEM] * groups + [ANY] * len(stores),
        out_specs=[VMEM] * groups,
        scratch_shapes=[
            pltpu.VMEM((slots, rows_all, head_size), jnp.bfloat16),
            pltpu.VMEM((tile_rows // CUBE, tile_rows), jnp.bfloat16),
            pltpu.VMEM((cubes, head_size), jnp.bfloat16),
            pltpu.VMEM((cubes, 2 * head_size), jnp.bfloat16),
            pltpu.VMEM((groups * tokens, count * head_size), jnp.bfloat16),
            pltpu.VMEM((groups * tokens, GATE_ROWS), jnp.float32),
            pltpu.VMEM((groups * tokens, head_size), jnp.float32),
            pltpu.VMEM((2, CUBE, picks * CUBE), jnp.float32),
            pltpu.VMEM((2, CUBE, picks * CUBE), jnp.bfloat16),
            pltpu.VMEM((groups * tokens, count * head_size), jnp.bfloat16),
            pltpu.SemaphoreType.DMA((slots, len(stores))),
        ],
        cost_estimate=pl.CostEstimate(
            flops=4 * units * count * CUBE * CUBE * picks * head_size,
            bytes_accessed=2 * rows_all * count * head_size,
            transcendentals=units * count * CUBE * CUBE * picks,
        ),
        compiler_params=pltpu.CompilerParams(
            vmem_limit_bytes=2 * slots * rows_all * head_size + (10 << 20)
        ),
        name="attend",
    )(tables, *queries, *stores)


def body(query_rows, key_rows, value_rows, gate_logits, selection, cube_ids):
    devices = lax.axis_size("cubes")
    tokens, width = query_rows.shape
    heads_all = gate_logits.shape[1] // 2
    head_size = width // heads_all
    if tokens != head_size:
        raise ValueError("gate rows")
    local = tokens // CUBE
    cubes = cube_ids.shape[0]
    picks = selection.shape[2]
    common = math.gcd(heads_all, devices)
    groups = common & -common
    ring = devices // groups
    heads = heads_all // groups
    group_width = heads * head_size
    self_index = lax.axis_index("cubes")
    home = self_index // ring
    place = self_index % ring

    counts = CHUNKS if sum(CHUNKS) == heads else (heads,)
    firsts = [sum(counts[:i]) for i in range(len(counts))]
    spans = [(first * head_size, count * head_size) for first, count in zip(firsts, counts)]

    def over_groups(value, relative):
        pairs = [(i, i ^ (relative * ring)) for i in range(devices)]
        return lax.ppermute(value, "cubes", pairs)

    def over_ring(value, step):
        return lax.ppermute(value, "cubes", [(i, i ^ step) for i in range(devices)])

    steps = [1 << bit for bit in range(ring.bit_length() - 2, -1, -1)]

    def gather(value):
        stores = [value]
        for number, step in enumerate(steps):
            stores = stores + [over_ring(store, step) for store in stores]
            if number + 2 < len(steps):
                stores = [jnp.concatenate(stores, axis=0)]
        return stores

    index = home.astype(jnp.int32).reshape(1)
    order = [*range(groups - 1, 1, -1), 1]
    whole = (0, group_width)
    gate_rows = jnp.transpose(gate_logits).reshape(2, heads_all * tokens)
    gate_rows = jnp.pad(gate_rows, ((0, GATE_ROWS - 2), (0, 0)))

    sent = [(r, *whole) for r in order + [0]]
    keys_sent = pack(index, [((key_rows, value_rows), sent)], group_width)
    queries_sent = pack(index, [((query_rows, gate_rows), sent)], group_width)

    cube_range = jnp.arange(cubes, dtype=jnp.int32)
    device_of = cube_range // local
    offset = jnp.bitwise_xor(device_of % ring, place)
    relative = jnp.bitwise_xor(device_of // ring, home)
    slot = jnp.zeros_like(offset)
    for number, step in enumerate(steps):
        slot = slot + jnp.where(jnp.bitwise_and(offset, step) > 0, 1 << number, 0)
    piece = relative * ring + slot
    start = piece * (2 * tokens) + (cube_range % local) * CUBE
    row_of_cube = jnp.sum(
        jnp.where(cube_ids[None, :] == cube_range[:, None], start[None, :], 0), axis=1
    )
    chosen = selection.reshape(groups, ring, local, heads_all, picks)
    chosen = lax.dynamic_slice(
        chosen, (0, place, 0, home * heads, 0), (groups, 1, local, heads, picks)
    )
    tables = jnp.concatenate((row_of_cube, chosen.reshape(-1), index)).astype(jnp.int32)

    arrived = {}
    for r, value in zip(order, keys_sent):
        arrived[r] = over_groups(value, r)
    arrived[0] = keys_sent[-1]
    queries = {0: queries_sent[-1]}
    for r, value in zip(order, queries_sent):
        queries[r] = over_groups(value, r)
    stores = {}
    for r in [0] + order:
        stores[r] = gather(arrived[r])
    stores = [store for r in range(groups) for store in stores[r]]

    pieces, placed = [], []
    for number, (begin, size) in enumerate(spans):
        outs = attend(
            tables,
            [queries[r] for r in range(groups)],
            [begin] * groups,
            stores,
            [begin] * len(stores),
            (local, cubes, heads, firsts[number], counts[number], picks, head_size),
        )
        pieces.append(outs[0])
        for r in order:
            pieces.append(over_groups(outs[r], r))
        placed += [(r, begin, size) for r in [0] + order]
    return unpack(index, pieces, placed, group_width, width)


def solution(mesh):
    placed = (
        P(("groups", "cubes"), None),
        P(("groups", "cubes"), None),
        P(("groups", "cubes"), None),
        P(("groups", "cubes"), None),
        P("groups", None, None),
        P("groups"),
    )

    return jax.shard_map(
        body, mesh=mesh, in_specs=placed, out_specs=P(("groups", "cubes"), None), check_vma=False
    )
```

time: 122 us -> 106 us (0.87)
  Pallas kernels: 34.2 us -> 19 us
  starting transfers between devices: 33.9 us -> 25 us
  waiting for transfers between devices: 43.9 us -> 51.8 us
  local copies, waits for them, and re-layouts: 7.38 us -> 9.28 us
  other arithmetic: 1.83 us -> 0.2 us
    pallas_call x2, Pallas kernels: 27.8 us -> 12.5 us  [attend(): pl.pallas_call(functools.partial(attend_kernel, shape), out_shape=[out] *...]
    ppermute x18 -> x12, starting transfers between devices: 31.7 us -> 18.9 us  [over_groups(): return lax.ppermute(value, 'cubes', pairs)]
    ppermute x4 -> x12, waiting for transfers between devices: 7.99 us -> 16.9 us  [over_ring(): return lax.ppermute(value, 'cubes', [(i, i ^ step) for i in range(devices)])]
    ppermute x4 -> x12, starting transfers between devices: 2.23 us -> 6.11 us  [over_ring(): return lax.ppermute(value, 'cubes', [(i, i ^ step) for i in range(devices)])]
    unnamed x55 -> x45, local copies, waits for them, and re-layouts: 5.48 us -> 7.59 us
    ppermute x18 -> x12, waiting for transfers between devices: 35.9 us -> 34.8 us  [over_groups(): return lax.ppermute(value, 'cubes', pairs)]
  transfers between devices with their start and end apart: 22 -> 24, of which waited for: 8 -> 9; matrix products, arithmetic and copies ran while one was open for 5% -> 2% of each run, Pallas kernels for 24% -> 9%
where the time goes in v2:
time: 106 us; the launch traced here: 105 us
  waiting for transfers between devices  51.8 us (49%)
  starting transfers between devices  25 us (24%)
  Pallas kernels  19 us (18%)
  local copies, waits for them, and re-layouts  9.28 us (9%)
    ppermute x12, waiting for transfers between devices, over_groups(): return lax.ppermute(value, 'cubes', pairs)  34.8 us
    ppermute x12, starting transfers between devices, over_groups(): return lax.ppermute(value, 'cubes', pairs)  18.9 us
    ppermute x12, waiting for transfers between devices, over_ring(): return lax.ppermute(value, 'cubes', [(i, i ^ step) for i in range(devices)])  16.9 us
    pallas_call x2, Pallas kernels, attend(): pl.pallas_call(functools.partial(attend_kernel, shape), out_shape=[out] *...  12.5 us
    unnamed x45, local copies, waits for them, and re-layouts  7.59 us
    ppermute x12, starting transfers between devices, over_ring(): return lax.ppermute(value, 'cubes', [(i, i ^ step) for i in range(devices)])  6.11 us
    pallas_call x2, Pallas kernels, pack(): pl.pallas_call(functools.partial(pack_kernel, tuple(numbered), width), ou...  4.46 us
  transfers between devices with their start and end apart: 24, of which 9 were waited for; matrix products, arithmetic and copies ran while one was open for 2% of the time, Pallas kernels for 9%

profile of v2, /device:TPU:0, one launch (start us, length us, event | category | flops | bytes accessed | tf_op | source)
XLA Modules:
  0.0 105.3 jit_solution(2531323443167649294)
XLA Ops:
  0.0 0.7 copy-done.20
  1.3 2.0 %pack.2 = (bf16[136,640]{1,0:T(8,128)(2,1)}, bf16[136,640]{1,0:T(8,128)(2,1)}, bf16[136,640]{1,0:T(8,128)(2,1)}, bf16[136,640]{1,0:T(8,128)(2,1)}) custom-call(s32[1]{0:T(128)} %bitcast.index_ref, bf16[128,2560]{1,0:T(8,128)(2,1)} %refs_0_.2, bf16[8,2560]{1,0:T(8,128)(2,1)} %pad.4.refs_1_), custom_call_target="tpu_custom_call" | custom-call | tf_op jit(solution)/shard_map/pack/pallas_call | solution.py:51
  3.3 3.1 %collective-permute-start = (bf16[136,640]{1,0:T(8,128)(2,1)}, bf16[136,640]{1,0:T(8,128)(2,1)S(1)}, u32[]{:S(2)}, u32[]{:S(2)}) collective-permute-start(bf16[136,640]{1,0:T(8,128)(2,1)} %get-tuple-element.22), channel_id=1, source_target_pairs={{0,4},{1,5},{2,6},{3,7},{4,0},{5,1},{6,2},{7,3},{8,12},{9,13},{10,... | collective-permute-start | bytes 522248 | tf_op jit(solution)/shard_map/ppermute | solution.py:291
  6.4 2.6 %collective-permute-start.1 = (bf16[136,640]{1,0:T(8,128)(2,1)}, bf16[136,640]{1,0:T(8,128)(2,1)S(1)}, u32[]{:S(2)}, u32[]{:S(2)}) collective-permute-start(bf16[136,640]{1,0:T(8,128)(2,1)} %get-tuple-element.23), channel_id=1, source_target_pairs={{0,8},{1,9},{2,10},{3,11},{4,12},{5,13},{6,14},{7,15},{8,0},{9,1},... | collective-permute-start | bytes 522248 | tf_op jit(solution)/shard_map/ppermute | solution.py:291
  9.0 2.5 %pack.3 = (bf16[256,640]{1,0:T(8,128)(2,1)}, bf16[256,640]{1,0:T(8,128)(2,1)}, bf16[256,640]{1,0:T(8,128)(2,1)}, bf16[256,640]{1,0:T(8,128)(2,1)}) custom-call(s32[1]{0:T(128)} %bitcast.index_ref, bf16[128,2560]{1,0:T(8,128)(2,1)} %refs_0_.3, bf16[128,2560]{1,0:T(8,128)(2,1)} %refs_1_.1), custom_call_target="tpu_custom_call" | custom-call | tf_op jit(solution)/shard_map/pack/pallas_call | solution.py:51
  11.5 1.9 %collective-permute-start.10 = (bf16[256,640]{1,0:T(8,128)(2,1)}, bf16[256,640]{1,0:T(8,128)(2,1)S(1)}, u32[]{:S(2)}, u32[]{:S(2)}) collective-permute-start(bf16[256,640]{1,0:T(8,128)(2,1)} %get-tuple-element.27), channel_id=1, source_target_pairs={{0,8},{1,9},{2,10},{3,11},{4,12},{5,13},{6,14},{7,15},{8,0},{9,1},... | collective-permute-start | bytes 983048 | tf_op jit(solution)/shard_map/ppermute | solution.py:291
  13.4 2.0 %collective-permute-start.14 = (bf16[256,640]{1,0:T(8,128)(2,1)}, bf16[256,640]{1,0:T(8,128)(2,1)S(1)}, u32[]{:S(2)}, u32[]{:S(2)}) collective-permute-start(bf16[256,640]{1,0:T(8,128)(2,1)} %get-tuple-element.28), channel_id=1, source_target_pairs={{0,12},{1,13},{2,14},{3,15},{4,8},{5,9},{6,10},{7,11},{8,4},{9,5},... | collective-permute-start | bytes 983048 | tf_op jit(solution)/shard_map/ppermute | solution.py:291
  15.3 0.7 copy-done.2
  16.5 19.8 %collective-permute-done.1.refs_2_ = bf16[136,640]{1,0:T(8,128)(2,1)S(1)} collective-permute-done((bf16[136,640]{1,0:T(8,128)(2,1)}, bf16[136,640]{1,0:T(8,128)(2,1)S(1)}, u32[]{:S(2)}, u32[]{:S(2)}) %collective-permute-start.1) | collective-permute-done | bytes 174112 | tf_op jit(solution)/shard_map/ppermute | solution.py:291
  36.3 0.7 copy-done.5
  37.0 1.5 %collective-permute-start.3 = (bf16[256,640]{1,0:T(8,128)(2,1)}, bf16[256,640]{1,0:T(8,128)(2,1)S(1)}, u32[]{:S(2)}, u32[]{:S(2)}) collective-permute-start(bf16[256,640]{1,0:T(8,128)(2,1)} %get-tuple-element.25.refs_4_), channel_id=1, source_target_pairs={{0,2},{1,3},{2,0},{3,1},{4,6},{5,7},{6,4},{7,5},{8,10},{9,11},{10,... | collective-permute-start | bytes 983048 | tf_op jit(solution)/shard_map/ppermute | solution.py:294
  38.5 0.7 copy-done.8
  39.2 7.9 %collective-permute-done.10.refs_12_ = bf16[256,640]{1,0:T(8,128)(2,1)S(1)} collective-permute-done((bf16[256,640]{1,0:T(8,128)(2,1)}, bf16[256,640]{1,0:T(8,128)(2,1)S(1)}, u32[]{:S(2)}, u32[]{:S(2)}) %collective-permute-start.10) | collective-permute-done | bytes 327712 | tf_op jit(solution)/shard_map/ppermute | solution.py:291
  47.1 1.5 %collective-permute-start.11 = (bf16[256,640]{1,0:T(8,128)(2,1)S(1)}, bf16[256,640]{1,0:T(8,128)(2,1)S(1)}, u32[]{:S(2)}, u32[]{:S(2)}) collective-permute-start(bf16[256,640]{1,0:T(8,128)(2,1)S(1)} %collective-permute-done.10.refs_12_), channel_id=1, source_target_pairs={{0,2},{1,3},{2,0},{3,1},{4,6},{5,7},{6,4},{7,5},{8,10},{9,11},{10,... | collective-permute-start | bytes 983048 | tf_op jit(solution)/shard_map/ppermute | solution.py:294
  49.1 1.5 %collective-permute-start.7 = (bf16[256,640]{1,0:T(8,128)(2,1)S(1)}, bf16[256,640]{1,0:T(8,128)(2,1)S(1)}, u32[]{:S(2)}, u32[]{:S(2)}) collective-permute-start(bf16[256,640]{1,0:T(8,128)(2,1)S(1)} %collective-permute-done.6.refs_8_), channel_id=1, source_target_pairs={{0,2},{1,3},{2,0},{3,1},{4,6},{5,7},{6,4},{7,5},{8,10},{9,11},{10,... | collective-permute-start | bytes 983048 | tf_op jit(solution)/shard_map/ppermute | solution.py:294
  51.1 0.8 copy.9
  51.9 0.8 constant_dynamic-slice_fusion
  53.0 4.7 %collective-permute-done.11.refs_13_ = bf16[256,640]{1,0:T(8,128)(2,1)S(1)} collective-permute-done((bf16[256,640]{1,0:T(8,128)(2,1)S(1)}, bf16[256,640]{1,0:T(8,128)(2,1)S(1)}, u32[]{:S(2)}, u32[]{:S(2)}) %collective-permute-start.11) | collective-permute-done | bytes 327712 | tf_op jit(solution)/shard_map/ppermute | solution.py:294
  57.7 6.9 %collective-permute-done.15.refs_17_ = bf16[256,640]{1,0:T(8,128)(2,1)S(1)} collective-permute-done((bf16[256,640]{1,0:T(8,128)(2,1)S(1)}, bf16[256,640]{1,0:T(8,128)(2,1)S(1)}, u32[]{:S(2)}, u32[]{:S(2)}) %collective-permute-start.15) | collective-permute-done | bytes 327712 | tf_op jit(solution)/shard_map/ppermute | solution.py:294
  64.6 3.5 %collective-permute-done.7.refs_9_ = bf16[256,640]{1,0:T(8,128)(2,1)S(1)} collective-permute-done((bf16[256,640]{1,0:T(8,128)(2,1)S(1)}, bf16[256,640]{1,0:T(8,128)(2,1)S(1)}, u32[]{:S(2)}, u32[]{:S(2)}) %collective-permute-start.7) | collective-permute-done | bytes 327712 | tf_op jit(solution)/shard_map/ppermute | solution.py:294
  68.9 0.8 collective-permute-done.13.refs_15_
  70.7 0.9 copy-done.3
  71.6 0.9 copy-done.6
  72.5 0.9 copy-done.9
  73.5 5.3 %attend.3 = (bf16[128,256]{1,0:T(8,128)(2,1)S(1)}, bf16[128,256]{1,0:T(8,128)(2,1)S(1)}, bf16[128,256]{1,0:T(8,128)(2,1)S(1)}, bf16[128,256]{1,0:T(8,128)(2,1)S(1)}) custom-call(s32[353]{0:T(512)S(1)} %pad_add_fusion.tables_ref, bf16[136,640]{1,0:T(8,128)(2,1)S(1)} %copy-done.1, bf16[136,640]{1,0:T(8,128)(2,1)S(1)} %copy-done.3, ...), custom_call_target="tpu_custom_call" | custom-call | flops 268435456 | bytes 2097152 | tf_op jit(solution)/shard_map/attend/pallas_call | solution.py:236
  78.8 2.6 %collective-permute-start.21 = (bf16[128,256]{1,0:T(8,128)(2,1)S(1)}, bf16[128,256]{1,0:T(8,128)(2,1)S(1)}, u32[]{:S(2)}, u32[]{:S(2)}) collective-permute-start(bf16[128,256]{1,0:T(8,128)(2,1)S(1)} %get-tuple-element.34), channel_id=1, source_target_pairs={{0,12},{1,13},{2,14},{3,15},{4,8},{5,9},{6,10},{7,11},{8,4},{9,5},... | collective-permute-start | bytes 196616 | tf_op jit(solution)/shard_map/ppermute | solution.py:291
  81.4 7.2 %attend.2 = (bf16[128,384]{1,0:T(8,128)(2,1)S(1)}, bf16[128,384]{1,0:T(8,128)(2,1)S(1)}, bf16[128,384]{1,0:T(8,128)(2,1)S(1)}, bf16[128,384]{1,0:T(8,128)(2,1)S(1)}) custom-call(s32[353]{0:T(512)S(1)} %pad_add_fusion.tables_ref, bf16[136,640]{1,0:T(8,128)(2,1)S(1)} %copy-done.1, bf16[136,640]{1,0:T(8,128)(2,1)S(1)} %copy-done.4, ...), custom_call_target="tpu_custom_call" | custom-call | flops 402653184 | bytes 3145728 | tf_op jit(solution)/shard_map/attend/pallas_call | solution.py:236
  89.2 1.3 %collective-permute-start.18 = (bf16[128,384]{1,0:T(8,128)(2,1)S(1)}, bf16[128,384]{1,0:T(8,128)(2,1)S(1)}, u32[]{:S(2)}, u32[]{:S(2)}) collective-permute-start(bf16[128,384]{1,0:T(8,128)(2,1)S(1)} %get-tuple-element.30), channel_id=1, source_target_pairs={{0,12},{1,13},{2,14},{3,15},{4,8},{5,9},{6,10},{7,11},{8,4},{9,5},... | collective-permute-start | bytes 294920 | tf_op jit(solution)/shard_map/ppermute | solution.py:291
  90.5 3.1 %collective-permute-start.20 = (bf16[128,384]{1,0:T(8,128)(2,1)S(1)}, bf16[128,384]{1,0:T(8,128)(2,1)S(1)}, u32[]{:S(2)}, u32[]{:S(2)}) collective-permute-start(bf16[128,384]{1,0:T(8,128)(2,1)S(1)} %get-tuple-element.32), channel_id=1, source_target_pairs={{0,4},{1,5},{2,6},{3,7},{4,0},{5,1},{6,2},{7,3},{8,12},{9,13},{10,... | collective-permute-start | bytes 294920 | tf_op jit(solution)/shard_map/ppermute | solution.py:291
  93.6 1.9 %collective-permute-start.23 = (bf16[128,256]{1,0:T(8,128)(2,1)S(1)}, bf16[128,256]{1,0:T(8,128)(2,1)S(1)}, u32[]{:S(2)}, u32[]{:S(2)}) collective-permute-start(bf16[128,256]{1,0:T(8,128)(2,1)S(1)} %get-tuple-element.36), channel_id=1, source_target_pairs={{0,4},{1,5},{2,6},{3,7},{4,0},{5,1},{6,2},{7,3},{8,12},{9,13},{10,... | collective-permute-start | bytes 196616 | tf_op jit(solution)/shard_map/ppermute | solution.py:291
  95.5 7.1 %collective-permute-done.22.refs_6_ = bf16[128,256]{1,0:T(8,128)(2,1)S(1)} collective-permute-done((bf16[128,256]{1,0:T(8,128)(2,1)S(1)}, bf16[128,256]{1,0:T(8,128)(2,1)S(1)}, u32[]{:S(2)}, u32[]{:S(2)}) %collective-permute-start.22) | collective-permute-done | bytes 65568 | tf_op jit(solution)/shard_map/ppermute | solution.py:291
  103.3 2.0 %unpack.1 = bf16[128,2560]{1,0:T(8,128)(2,1)} custom-call(s32[1]{0:T(128)} %bitcast.index_ref, bf16[128,384]{1,0:T(8,128)(2,1)} %copy-done.11, bf16[128,384]{1,0:T(8,128)(2,1)} %copy-done.13, bf16[128,384]{1,0:T(8,128)(2,1)} %copy-done.14, bf16[128,384]{1,0:T(8,128)(2,1)} %copy-done.15, bf16[128,256]{1,0:T(8,128)(2,1)} %copy-done.12, ...), custom_call_target="tpu_custom_call" | custom-call | tf_op jit(solution)/shard_map/unpack/pallas_call | solution.py:68
  (74 shorter events, 5.5 us)
Async XLA Ops:
  3.3 12.0 %collective-permute-start = (bf16[136,640]{1,0:T(8,128)(2,1)}, bf16[136,640]{1,0:T(8,128)(2,1)S(1)}, u32[]{:S(2)}, u32[]{:S(2)}) collective-permute-start(bf16[136,640]{1,0:T(8,128)(2,1)} %get-tuple-element.22), channel_id=1, source_target_pairs={{0,4},{1,5},{2,6},{3,7},{4,0},{5,1},{6,2},{7,3},{8,12},{9,13},{10,... | collective-permute-start | bytes 522248 | tf_op jit(solution)/shard_map/ppermute | solution.py:291
  6.4 29.9 %collective-permute-start.1 = (bf16[136,640]{1,0:T(8,128)(2,1)}, bf16[136,640]{1,0:T(8,128)(2,1)S(1)}, u32[]{:S(2)}, u32[]{:S(2)}) collective-permute-start(bf16[136,640]{1,0:T(8,128)(2,1)} %get-tuple-element.23), channel_id=1, source_target_pairs={{0,8},{1,9},{2,10},{3,11},{4,12},{5,13},{6,14},{7,15},{8,0},{9,1},... | collective-permute-start | bytes 522248 | tf_op jit(solution)/shard_map/ppermute | solution.py:291
  9.0 42.2 %copy-start.16 = (s32[32,20,8]{0,2,1:T(8,128)S(1)}, s32[32,20,8]{0,2,1:T(8,128)}, u32[]{:S(2)}) copy-start(s32[32,20,8]{0,2,1:T(8,128)} %param.10) | copy-start | bytes 61444
  9.0 29.5 %collective-permute-start.2 = (bf16[136,640]{1,0:T(8,128)(2,1)}, bf16[136,640]{1,0:T(8,128)(2,1)S(1)}, u32[]{:S(2)}, u32[]{:S(2)}) collective-permute-start(bf16[136,640]{1,0:T(8,128)(2,1)} %get-tuple-element.24), channel_id=1, source_target_pairs={{0,12},{1,13},{2,14},{3,15},{4,8},{5,9},{6,10},{7,11},{8,4},{9,5},... | collective-permute-start | bytes 522248 | tf_op jit(solution)/shard_map/ppermute | solution.py:291
  9.0 61.7 %copy-start.1 = (bf16[136,640]{1,0:T(8,128)(2,1)S(1)}, bf16[136,640]{1,0:T(8,128)(2,1)}, u32[]{:S(2)}) copy-start(bf16[136,640]{1,0:T(8,128)(2,1)} %get-tuple-element.21.refs_0_) | copy-start | bytes 522244
  11.5 59.2 %copy-start = (bf16[256,640]{1,0:T(8,128)(2,1)S(1)}, bf16[256,640]{1,0:T(8,128)(2,1)}, u32[]{:S(2)}) copy-start(bf16[256,640]{1,0:T(8,128)(2,1)} %get-tuple-element.25.refs_4_) | copy-start | bytes 983044
  11.5 35.6 %collective-permute-start.10 = (bf16[256,640]{1,0:T(8,128)(2,1)}, bf16[256,640]{1,0:T(8,128)(2,1)S(1)}, u32[]{:S(2)}, u32[]{:S(2)}) collective-permute-start(bf16[256,640]{1,0:T(8,128)(2,1)} %get-tuple-element.27), channel_id=1, source_target_pairs={{0,8},{1,9},{2,10},{3,11},{4,12},{5,13},{6,14},{7,15},{8,0},{9,1},... | collective-permute-start | bytes 983048 | tf_op jit(solution)/shard_map/ppermute | solution.py:291
  13.4 35.2 %collective-permute-start.14 = (bf16[256,640]{1,0:T(8,128)(2,1)}, bf16[256,640]{1,0:T(8,128)(2,1)S(1)}, u32[]{:S(2)}, u32[]{:S(2)}) collective-permute-start(bf16[256,640]{1,0:T(8,128)(2,1)} %get-tuple-element.28), channel_id=1, source_target_pairs={{0,12},{1,13},{2,14},{3,15},{4,8},{5,9},{6,10},{7,11},{8,4},{9,5},... | collective-permute-start | bytes 983048 | tf_op jit(solution)/shard_map/ppermute | solution.py:291
  16.0 33.1 %collective-permute-start.6 = (bf16[256,640]{1,0:T(8,128)(2,1)}, bf16[256,640]{1,0:T(8,128)(2,1)S(1)}, u32[]{:S(2)}, u32[]{:S(2)}) collective-permute-start(bf16[256,640]{1,0:T(8,128)(2,1)} %get-tuple-element.26), channel_id=1, source_target_pairs={{0,4},{1,5},{2,6},{3,7},{4,0},{5,1},{6,2},{7,3},{8,12},{9,13},{10,... | collective-permute-start | bytes 983048 | tf_op jit(solution)/shard_map/ppermute | solution.py:291
  37.0 13.6 %collective-permute-start.3 = (bf16[256,640]{1,0:T(8,128)(2,1)}, bf16[256,640]{1,0:T(8,128)(2,1)S(1)}, u32[]{:S(2)}, u32[]{:S(2)}) collective-permute-start(bf16[256,640]{1,0:T(8,128)(2,1)} %get-tuple-element.25.refs_4_), channel_id=1, source_target_pairs={{0,2},{1,3},{2,0},{3,1},{4,6},{5,7},{6,4},{7,5},{8,10},{9,11},{10,... | collective-permute-start | bytes 983048 | tf_op jit(solution)/shard_map/ppermute | solution.py:294
  39.2 11.5 %collective-permute-start.4 = (bf16[256,640]{1,0:T(8,128)(2,1)}, bf16[256,640]{1,0:T(8,128)(2,1)S(1)}, u32[]{:S(2)}, u32[]{:S(2)}) collective-permute-start(bf16[256,640]{1,0:T(8,128)(2,1)} %get-tuple-element.25.refs_4_), channel_id=1, source_target_pairs={{0,1},{1,0},{2,3},{3,2},{4,5},{5,4},{6,7},{7,6},{8,9},{9,8},{10,11... | collective-permute-start | bytes 983048 | tf_op jit(solution)/shard_map/ppermute | solution.py:294
  47.1 10.6 %collective-permute-start.11 = (bf16[256,640]{1,0:T(8,128)(2,1)S(1)}, bf16[256,640]{1,0:T(8,128)(2,1)S(1)}, u32[]{:S(2)}, u32[]{:S(2)}) collective-permute-start(bf16[256,640]{1,0:T(8,128)(2,1)S(1)} %collective-permute-done.10.refs_12_), channel_id=1, source_target_pairs={{0,2},{1,3},{2,0},{3,1},{4,6},{5,7},{6,4},{7,5},{8,10},{9,11},{10,... | collective-permute-start | bytes 983048 | tf_op jit(solution)/shard_map/ppermute | solution.py:294
  48.6 16.0 %collective-permute-start.15 = (bf16[256,640]{1,0:T(8,128)(2,1)S(1)}, bf16[256,640]{1,0:T(8,128)(2,1)S(1)}, u32[]{:S(2)}, u32[]{:S(2)}) collective-permute-start(bf16[256,640]{1,0:T(8,128)(2,1)S(1)} %collective-permute-done.14.refs_16_), channel_id=1, source_target_pairs={{0,2},{1,3},{2,0},{3,1},{4,6},{5,7},{6,4},{7,5},{8,10},{9,11},{10,... | collective-permute-start | bytes 983048 | tf_op jit(solution)/shard_map/ppermute | solution.py:294
  49.1 19.0 %collective-permute-start.7 = (bf16[256,640]{1,0:T(8,128)(2,1)S(1)}, bf16[256,640]{1,0:T(8,128)(2,1)S(1)}, u32[]{:S(2)}, u32[]{:S(2)}) collective-permute-start(bf16[256,640]{1,0:T(8,128)(2,1)S(1)} %collective-permute-done.6.refs_8_), channel_id=1, source_target_pairs={{0,2},{1,3},{2,0},{3,1},{4,6},{5,7},{6,4},{7,5},{8,10},{9,11},{10,... | collective-permute-start | bytes 983048 | tf_op jit(solution)/shard_map/ppermute | solution.py:294
  50.6 17.5 %collective-permute-start.5 = (bf16[256,640]{1,0:T(8,128)(2,1)S(1)}, bf16[256,640]{1,0:T(8,128)(2,1)S(1)}, u32[]{:S(2)}, u32[]{:S(2)}) collective-permute-start(bf16[256,640]{1,0:T(8,128)(2,1)S(1)} %collective-permute-done.3.refs_5_), channel_id=1, source_target_pairs={{0,1},{1,0},{2,3},{3,2},{4,5},{5,4},{6,7},{7,6},{8,9},{9,8},{10,11... | collective-permute-start | bytes 983048 | tf_op jit(solution)/shard_map/ppermute | solution.py:294
  50.6 18.0 %collective-permute-start.12 = (bf16[256,640]{1,0:T(8,128)(2,1)S(1)}, bf16[256,640]{1,0:T(8,128)(2,1)}, u32[]{:S(2)}, u32[]{:S(2)}) collective-permute-start(bf16[256,640]{1,0:T(8,128)(2,1)S(1)} %collective-permute-done.10.refs_12_), channel_id=1, source_target_pairs={{0,1},{1,0},{2,3},{3,2},{4,5},{5,4},{6,7},{7,6},{8,9},{9,8},{10,11... | collective-permute-start | bytes 983048 | tf_op jit(solution)/shard_map/ppermute | solution.py:294
  53.0 15.8 %copy-start.21 = (s32[32]{0:T(128)S(1)}, s32[32]{0:T(128)}, u32[]{:S(2)}) copy-start(s32[32]{0:T(128)} %param.11) | copy-start | bytes 388
  57.7 11.3 %collective-permute-start.16 = (bf16[256,640]{1,0:T(8,128)(2,1)S(1)}, bf16[256,640]{1,0:T(8,128)(2,1)S(1)}, u32[]{:S(2)}, u32[]{:S(2)}) collective-permute-start(bf16[256,640]{1,0:T(8,128)(2,1)S(1)} %collective-permute-done.14.refs_16_), channel_id=1, source_target_pairs={{0,1},{1,0},{2,3},{3,2},{4,5},{5,4},{6,7},{7,6},{8,9},{9,8},{10,11... | collective-permute-start | bytes 983048 | tf_op jit(solution)/shard_map/ppermute | solution.py:294
  64.6 4.3 %collective-permute-start.8 = (bf16[256,640]{1,0:T(8,128)(2,1)S(1)}, bf16[256,640]{1,0:T(8,128)(2,1)S(1)}, u32[]{:S(2)}, u32[]{:S(2)}) collective-permute-start(bf16[256,640]{1,0:T(8,128)(2,1)S(1)} %collective-permute-done.6.refs_8_), channel_id=1, source_target_pairs={{0,1},{1,0},{2,3},{3,2},{4,5},{5,4},{6,7},{7,6},{8,9},{9,8},{10,11... | collective-permute-start | bytes 983048 | tf_op jit(solution)/shard_map/ppermute | solution.py:294
  68.1 1.6 %collective-permute-start.13 = (bf16[256,640]{1,0:T(8,128)(2,1)S(1)}, bf16[256,640]{1,0:T(8,128)(2,1)S(1)}, u32[]{:S(2)}, u32[]{:S(2)}) collective-permute-start(bf16[256,640]{1,0:T(8,128)(2,1)S(1)} %collective-permute-done.11.refs_13_), channel_id=1, source_target_pairs={{0,1},{1,0},{2,3},{3,2},{4,5},{5,4},{6,7},{7,6},{8,9},{9,8},{10,11... | collective-permute-start | bytes 983048 | tf_op jit(solution)/shard_map/ppermute | solution.py:294
  68.1 2.1 %collective-permute-start.17 = (bf16[256,640]{1,0:T(8,128)(2,1)S(1)}, bf16[256,640]{1,0:T(8,128)(2,1)S(1)}, u32[]{:S(2)}, u32[]{:S(2)}) collective-permute-start(bf16[256,640]{1,0:T(8,128)(2,1)S(1)} %collective-permute-done.15.refs_17_), channel_id=1, source_target_pairs={{0,1},{1,0},{2,3},{3,2},{4,5},{5,4},{6,7},{7,6},{8,9},{9,8},{10,11... | collective-permute-start | bytes 983048 | tf_op jit(solution)/shard_map/ppermute | solution.py:294
  68.6 2.0 %collective-permute-start.9 = (bf16[256,640]{1,0:T(8,128)(2,1)S(1)}, bf16[256,640]{1,0:T(8,128)(2,1)S(1)}, u32[]{:S(2)}, u32[]{:S(2)}) collective-permute-start(bf16[256,640]{1,0:T(8,128)(2,1)S(1)} %collective-permute-done.7.refs_9_), channel_id=1, source_target_pairs={{0,1},{1,0},{2,3},{3,2},{4,5},{5,4},{6,7},{7,6},{8,9},{9,8},{10,11... | collective-permute-start | bytes 983048 | tf_op jit(solution)/shard_map/ppermute | solution.py:294
  73.5 7.9 %copy-start.7 = (bf16[136,640]{1,0:T(8,128)(2,1)S(1)}, bf16[136,640]{1,0:T(8,128)(2,1)}, u32[]{:S(2)}) copy-start(bf16[136,640]{1,0:T(8,128)(2,1)} %copy-done.5) | copy-start | bytes 522244
  73.5 7.9 %copy-start.10 = (bf16[136,640]{1,0:T(8,128)(2,1)S(1)}, bf16[136,640]{1,0:T(8,128)(2,1)}, u32[]{:S(2)}) copy-start(bf16[136,640]{1,0:T(8,128)(2,1)} %copy-done.8) | copy-start | bytes 522244
  78.8 9.8 %copy-start.12 = (bf16[128,256]{1,0:T(8,128)(2,1)}, bf16[128,256]{1,0:T(8,128)(2,1)S(1)}, u32[]{:S(2)}) copy-start(bf16[128,256]{1,0:T(8,128)(2,1)S(1)} %get-tuple-element.33.refs_4_) | copy-start | bytes 196612
  78.8 14.8 %collective-permute-start.21 = (bf16[128,256]{1,0:T(8,128)(2,1)S(1)}, bf16[128,256]{1,0:T(8,128)(2,1)S(1)}, u32[]{:S(2)}, u32[]{:S(2)}) collective-permute-start(bf16[128,256]{1,0:T(8,128)(2,1)S(1)} %get-tuple-element.34), channel_id=1, source_target_pairs={{0,12},{1,13},{2,14},{3,15},{4,8},{5,9},{6,10},{7,11},{8,4},{9,5},... | collective-permute-start | bytes 196616 | tf_op jit(solution)/shard_map/ppermute | solution.py:291
  89.2 13.4 %collective-permute-start.18 = (bf16[128,384]{1,0:T(8,128)(2,1)S(1)}, bf16[128,384]{1,0:T(8,128)(2,1)S(1)}, u32[]{:S(2)}, u32[]{:S(2)}) collective-permute-start(bf16[128,384]{1,0:T(8,128)(2,1)S(1)} %get-tuple-element.30), channel_id=1, source_target_pairs={{0,12},{1,13},{2,14},{3,15},{4,8},{5,9},{6,10},{7,11},{8,4},{9,5},... | collective-permute-start | bytes 294920 | tf_op jit(solution)/shard_map/ppermute | solution.py:291
  90.5 12.1 %collective-permute-start.19 = (bf16[128,384]{1,0:T(8,128)(2,1)S(1)}, bf16[128,384]{1,0:T(8,128)(2,1)S(1)}, u32[]{:S(2)}, u32[]{:S(2)}) collective-permute-start(bf16[128,384]{1,0:T(8,128)(2,1)S(1)} %get-tuple-element.31), channel_id=1, source_target_pairs={{0,8},{1,9},{2,10},{3,11},{4,12},{5,13},{6,14},{7,15},{8,0},{9,1},... | collective-permute-start | bytes 294920 | tf_op jit(solution)/shard_map/ppermute | solution.py:291
  90.5 12.1 %collective-permute-start.20 = (bf16[128,384]{1,0:T(8,128)(2,1)S(1)}, bf16[128,384]{1,0:T(8,128)(2,1)S(1)}, u32[]{:S(2)}, u32[]{:S(2)}) collective-permute-start(bf16[128,384]{1,0:T(8,128)(2,1)S(1)} %get-tuple-element.32), channel_id=1, source_target_pairs={{0,4},{1,5},{2,6},{3,7},{4,0},{5,1},{6,2},{7,3},{8,12},{9,13},{10,... | collective-permute-start | bytes 294920 | tf_op jit(solution)/shard_map/ppermute | solution.py:291
  93.6 9.0 %collective-permute-start.22 = (bf16[128,256]{1,0:T(8,128)(2,1)S(1)}, bf16[128,256]{1,0:T(8,128)(2,1)S(1)}, u32[]{:S(2)}, u32[]{:S(2)}) collective-permute-start(bf16[128,256]{1,0:T(8,128)(2,1)S(1)} %get-tuple-element.35), channel_id=1, source_target_pairs={{0,8},{1,9},{2,10},{3,11},{4,12},{5,13},{6,14},{7,15},{8,0},{9,1},... | collective-permute-start | bytes 196616 | tf_op jit(solution)/shard_map/ppermute | solution.py:291
  93.6 9.1 %copy-start.17 = (bf16[128,256]{1,0:T(8,128)(2,1)}, bf16[128,256]{1,0:T(8,128)(2,1)S(1)}, u32[]{:S(2)}) copy-start(bf16[128,256]{1,0:T(8,128)(2,1)S(1)} %collective-permute-done.21.refs_5_) | copy-start | bytes 196612
  93.6 9.0 %collective-permute-start.23 = (bf16[128,256]{1,0:T(8,128)(2,1)S(1)}, bf16[128,256]{1,0:T(8,128)(2,1)S(1)}, u32[]{:S(2)}, u32[]{:S(2)}) collective-permute-start(bf16[128,256]{1,0:T(8,128)(2,1)S(1)} %get-tuple-element.36), channel_id=1, source_target_pairs={{0,4},{1,5},{2,6},{3,7},{4,0},{5,1},{6,2},{7,3},{8,12},{9,13},{10,... | collective-permute-start | bytes 196616 | tf_op jit(solution)/shard_map/ppermute | solution.py:291
  (14 other events, 17.3 us)

commit v3 on v2

--- a/solution.py
+++ b/solution.py
@@ -14,6 +14,7 @@
 CHUNKS = (3, 2)
 POOL_ROWS = 1024
 HELD_BYTES = 8 << 20
+SMALL_VMEM = 12 << 20
 LOG2E = 1.4426950408889634
 
 VMEM = pl.BlockSpec(memory_space=pltpu.VMEM)
@@ -53,6 +54,7 @@
         out_shape=shapes,
         in_specs=[SMEM] + [VMEM] * len(operands),
         out_specs=[VMEM] * len(shapes),
+        compiler_params=pltpu.CompilerParams(vmem_limit_bytes=SMALL_VMEM),
         name="pack",
     )(index, *operands)
 
@@ -70,6 +72,7 @@
         out_shape=jax.ShapeDtypeStruct((pieces[0].shape[0], columns), jnp.bfloat16),
         in_specs=[SMEM] + [VMEM] * len(pieces),
         out_specs=VMEM,
+        compiler_params=pltpu.CompilerParams(vmem_limit_bytes=SMALL_VMEM),
         name="unpack",
     )(index, *pieces)
 
@@ -114,7 +117,9 @@
     for head in range(min(slots, count)):
         for copy in copies(head):
             copy.start()
-    home = tables_ref[cubes + units * heads * picks]
+    home = tables_ref[cubes + heads * picks * cubes]
+    place = tables_ref[cubes + heads * picks * cubes + 1]
+    ring = cubes // units
     mask_block = lax.broadcasted_iota(jnp.int32, pool_mask.shape, 0)
     is_value = mask_block >= tile_blocks
     mask_block = jnp.where(is_value, mask_block - tile_blocks, mask_block)
@@ -168,10 +173,11 @@
             coarse_part[rows, :] = sums[:, :head_size] * (gate / sums[:, head_size:])
 
         def unit_starts(unit):
-            block = ((home ^ (unit // local)) * local + unit % local) * heads
-            base = cubes + (block + first + head) * picks
+            block = ((home ^ (unit // local)) * ring + place) * local + unit % local
+            base = cubes + (first + head) * picks * cubes + block
             return [
-                pl.multiple_of(tables_ref[tables_ref[base + pick]], CUBE) for pick in range(picks)
+                pl.multiple_of(tables_ref[tables_ref[base + pick * cubes]], CUBE)
+                for pick in range(picks)
             ]
 
         def score_stage(unit):
@@ -295,9 +301,10 @@
 
     steps = [1 << bit for bit in range(ring.bit_length() - 2, -1, -1)]
 
-    def gather(value):
-        stores = [value]
+    def gather(stores, skipped):
         for number, step in enumerate(steps):
+            if number < skipped:
+                continue
             stores = stores + [over_ring(store, step) for store in stores]
             if number + 2 < len(steps):
                 stores = [jnp.concatenate(stores, axis=0)]
@@ -309,7 +316,7 @@
     gate_rows = jnp.transpose(gate_logits).reshape(2, heads_all * tokens)
     gate_rows = jnp.pad(gate_rows, ((0, GATE_ROWS - 2), (0, 0)))
 
-    sent = [(r, *whole) for r in order + [0]]
+    sent = [(0, *whole)] + [(r, *span) for span in spans for r in order]
     keys_sent = pack(index, [((key_rows, value_rows), sent)], group_width)
     queries_sent = pack(index, [((query_rows, gate_rows), sent)], group_width)
 
@@ -320,38 +327,40 @@
     slot = jnp.zeros_like(offset)
     for number, step in enumerate(steps):
         slot = slot + jnp.where(jnp.bitwise_and(offset, step) > 0, 1 << number, 0)
-    piece = relative * ring + slot
+    piece = jnp.where(relative == 0, slot, ring + slot * (groups - 1) + relative - 1)
     start = piece * (2 * tokens) + (cube_range % local) * CUBE
     row_of_cube = jnp.sum(
         jnp.where(cube_ids[None, :] == cube_range[:, None], start[None, :], 0), axis=1
     )
-    chosen = selection.reshape(groups, ring, local, heads_all, picks)
-    chosen = lax.dynamic_slice(
-        chosen, (0, place, 0, home * heads, 0), (groups, 1, local, heads, picks)
-    )
-    tables = jnp.concatenate((row_of_cube, chosen.reshape(-1), index)).astype(jnp.int32)
-
-    arrived = {}
-    for r, value in zip(order, keys_sent):
-        arrived[r] = over_groups(value, r)
-    arrived[0] = keys_sent[-1]
-    queries = {0: queries_sent[-1]}
-    for r, value in zip(order, queries_sent):
-        queries[r] = over_groups(value, r)
-    stores = {}
-    for r in [0] + order:
-        stores[r] = gather(arrived[r])
-    stores = [store for r in range(groups) for store in stores[r]]
-
+    chosen = jnp.transpose(selection, (1, 2, 0))
+    chosen = lax.dynamic_slice(chosen, (home * heads, 0, 0), (heads, picks, cubes))
+    tables = jnp.concatenate((row_of_cube, chosen.reshape(-1), index, place.reshape(1)))
+    tables = tables.astype(jnp.int32)
+
+    own_stores = gather([keys_sent[0]], 0)
     pieces, placed = [], []
-    for number, (begin, size) in enumerate(spans):
+    for c, (begin, size) in enumerate(spans):
+        keys, queries, beside = {}, {}, {}
+        for number, r in enumerate(order):
+            keys[r] = over_groups(keys_sent[1 + c * len(order) + number], r)
+            queries[r] = over_groups(queries_sent[1 + c * len(order) + number], r)
+        for r in order if steps else []:
+            beside[r] = over_ring(keys[r], steps[0])
+        stores = [
+            jnp.concatenate([part[r] for r in range(1, groups)], axis=0)
+            for part in (keys, beside)
+            if part
+        ]
+        if len(steps) > 2:
+            stores = [jnp.concatenate(stores, axis=0)]
+        stores = gather(stores, 1)
         outs = attend(
             tables,
-            [queries[r] for r in range(groups)],
-            [begin] * groups,
-            stores,
-            [begin] * len(stores),
-            (local, cubes, heads, firsts[number], counts[number], picks, head_size),
+            [queries_sent[0]] + [queries[r] for r in range(1, groups)],
+            [begin] + [0] * (groups - 1),
+            own_stores + stores,
+            [begin] * len(own_stores) + [0] * len(stores),
+            (local, cubes, heads, firsts[c], counts[c], picks, head_size),
         )
         pieces.append(outs[0])
         for r in order:

time: 106 us -> 101 us (0.953)
  starting transfers between devices: 25 us -> 43 us
  waiting for transfers between devices: 51.8 us -> 36.1 us
  Pallas kernels: 19 us -> 14.1 us
  local copies, waits for them, and re-layouts: 9.28 us -> 6.61 us
    ppermute x12 -> x18, starting transfers between devices: 18.9 us -> 33.3 us  [over_groups(): return lax.ppermute(value, 'cubes', pairs)]
    ppermute x12 -> x18, waiting for transfers between devices: 34.8 us -> 25.4 us  [over_groups(): return lax.ppermute(value, 'cubes', pairs)]
    ppermute x12 -> x13, waiting for transfers between devices: 16.9 us -> 10.7 us  [over_ring(): return lax.ppermute(value, 'cubes', [(i, i ^ step) for i in range(devices)])]
    pallas_call x2, Pallas kernels: 4.46 us -> 0.17 us  [pack(): pl.pallas_call(functools.partial(pack_kernel, tuple(numbered), width), ou...]
    ppermute x12 -> x13, starting transfers between devices: 6.11 us -> 9.71 us  [over_ring(): return lax.ppermute(value, 'cubes', [(i, i ^ step) for i in range(devices)])]
    unnamed x45 -> x40, local copies, waits for them, and re-layouts: 7.59 us -> 5.75 us
    pallas_call x1, Pallas kernels: 2 us -> 0.9 us  [unpack(): pl.pallas_call(functools.partial(unpack_kernel, spans, width), out_shape=...]
  transfers between devices with their start and end apart: 24 -> 31, of which waited for: 9 -> 12; matrix products, arithmetic and copies ran while one was open for 2% -> 1% of each run, Pallas kernels for 9% -> 13%
where the time goes in v3:
time: 101 us; the launch traced here: 100 us
  starting transfers between devices  43 us (43%)
  waiting for transfers between devices  36.1 us (36%)
  Pallas kernels  14.1 us (14%)
  local copies, waits for them, and re-layouts  6.61 us (7%)
    ppermute x18, starting transfers between devices, over_groups(): return lax.ppermute(value, 'cubes', pairs)  33.3 us
    ppermute x18, waiting for transfers between devices, over_groups(): return lax.ppermute(value, 'cubes', pairs)  25.4 us
    pallas_call x2, Pallas kernels, attend(): pl.pallas_call(functools.partial(attend_kernel, shape), out_shape=[out] *...  13.1 us
    ppermute x13, waiting for transfers between devices, over_ring(): return lax.ppermute(value, 'cubes', [(i, i ^ step) for i in range(devices)])  10.7 us
    ppermute x13, starting transfers between devices, over_ring(): return lax.ppermute(value, 'cubes', [(i, i ^ step) for i in range(devices)])  9.71 us
    unnamed x40, local copies, waits for them, and re-layouts  5.75 us
  transfers between devices with their start and end apart: 31, of which 12 were waited for; matrix products, arithmetic and copies ran while one was open for 1% of the time, Pallas kernels for 13%

profile of v3, /device:TPU:0, one launch (start us, length us, event | category | flops | bytes accessed | tf_op | source)
XLA Modules:
  0.0 100.2 jit_solution(5336556079348284222)
XLA Ops:
  0.0 1.1 %copy-done.1 = bf16[128,2560]{1,0:T(8,128)(2,1)S(1)} copy-done((bf16[128,2560]{1,0:T(8,128)(2,1)S(1)}, bf16[128,2560]{1,0:T(8,128)(2,1)}, u32[]{:S(2)}) %copy-start.1) | copy-done | bytes 655384
  1.1 1.1 %copy-done.2 = bf16[128,2560]{1,0:T(8,128)(2,1)S(1)} copy-done((bf16[128,2560]{1,0:T(8,128)(2,1)S(1)}, bf16[128,2560]{1,0:T(8,128)(2,1)}, u32[]{:S(2)}) %copy-start.2) | copy-done | bytes 655384
  2.3 3.1 %collective-permute-start.20 = (bf16[256,256]{1,0:T(8,128)(2,1)S(1)}, bf16[256,256]{1,0:T(8,128)(2,1)S(1)}, u32[]{:S(2)}, u32[]{:S(2)}) collective-permute-start(bf16[256,256]{1,0:T(8,128)(2,1)S(1)} %get-tuple-element.42), channel_id=1, source_target_pairs={{0,4},{1,5},{2,6},{3,7},{4,0},{5,1},{6,2},{7,3},{8,12},{9,13},{10,... | collective-permute-start | bytes 393224 | tf_op jit(solution)/shard_map/ppermute | solution.py:297
  5.4 2.6 %collective-permute-start.21 = (bf16[256,256]{1,0:T(8,128)(2,1)S(1)}, bf16[256,256]{1,0:T(8,128)(2,1)S(1)}, u32[]{:S(2)}, u32[]{:S(2)}) collective-permute-start(bf16[256,256]{1,0:T(8,128)(2,1)S(1)} %get-tuple-element.43), channel_id=1, source_target_pairs={{0,8},{1,9},{2,10},{3,11},{4,12},{5,13},{6,14},{7,15},{8,0},{9,1},... | collective-permute-start | bytes 393224 | tf_op jit(solution)/shard_map/ppermute | solution.py:297
  8.0 1.5 %collective-permute-start.3 = (bf16[256,640]{1,0:T(8,128)(2,1)S(1)}, bf16[256,640]{1,0:T(8,128)(2,1)S(1)}, u32[]{:S(2)}, u32[]{:S(2)}) collective-permute-start(bf16[256,640]{1,0:T(8,128)(2,1)S(1)} %get-tuple-element.31.refs_4_), channel_id=1, source_target_pairs={{0,2},{1,3},{2,0},{3,1},{4,6},{5,7},{6,4},{7,5},{8,10},{9,11},{10,... | collective-permute-start | bytes 983048 | tf_op jit(solution)/shard_map/ppermute | solution.py:300
  11.2 3.0 %collective-permute-done.21 = bf16[256,256]{1,0:T(8,128)(2,1)S(1)} collective-permute-done((bf16[256,256]{1,0:T(8,128)(2,1)S(1)}, bf16[256,256]{1,0:T(8,128)(2,1)S(1)}, u32[]{:S(2)}, u32[]{:S(2)}) %collective-permute-start.21) | collective-permute-done | bytes 131104 | tf_op jit(solution)/shard_map/ppermute | solution.py:297
  14.3 3.5 %collective-permute-start.6 = (bf16[256,384]{1,0:T(8,128)(2,1)S(1)}, bf16[256,384]{1,0:T(8,128)(2,1)S(1)}, u32[]{:S(2)}, u32[]{:S(2)}) collective-permute-start(bf16[256,384]{1,0:T(8,128)(2,1)S(1)} %get-tuple-element.32), channel_id=1, source_target_pairs={{0,4},{1,5},{2,6},{3,7},{4,0},{5,1},{6,2},{7,3},{8,12},{9,13},{10,... | collective-permute-start | bytes 589832 | tf_op jit(solution)/shard_map/ppermute | solution.py:297
  17.8 3.5 %collective-permute-start.7 = (bf16[256,384]{1,0:T(8,128)(2,1)S(1)}, bf16[256,384]{1,0:T(8,128)(2,1)S(1)}, u32[]{:S(2)}, u32[]{:S(2)}) collective-permute-start(bf16[256,384]{1,0:T(8,128)(2,1)S(1)} %get-tuple-element.33), channel_id=1, source_target_pairs={{0,8},{1,9},{2,10},{3,11},{4,12},{5,13},{6,14},{7,15},{8,0},{9,1},... | collective-permute-start | bytes 589832 | tf_op jit(solution)/shard_map/ppermute | solution.py:297
  21.4 3.4 %collective-permute-done.6 = bf16[256,384]{1,0:T(8,128)(2,1)S(1)} collective-permute-done((bf16[256,384]{1,0:T(8,128)(2,1)S(1)}, bf16[256,384]{1,0:T(8,128)(2,1)S(1)}, u32[]{:S(2)}, u32[]{:S(2)}) %collective-permute-start.6) | collective-permute-done | bytes 196640 | tf_op jit(solution)/shard_map/ppermute | solution.py:297
  24.8 2.7 %collective-permute-start.8 = (bf16[256,384]{1,0:T(8,128)(2,1)S(1)}, bf16[256,384]{1,0:T(8,128)(2,1)S(1)}, u32[]{:S(2)}, u32[]{:S(2)}) collective-permute-start(bf16[256,384]{1,0:T(8,128)(2,1)S(1)} %get-tuple-element.34), channel_id=1, source_target_pairs={{0,12},{1,13},{2,14},{3,15},{4,8},{5,9},{6,10},{7,11},{8,4},{9,5},... | collective-permute-start | bytes 589832 | tf_op jit(solution)/shard_map/ppermute | solution.py:297
  27.5 8.0 %collective-permute-done.7 = bf16[256,384]{1,0:T(8,128)(2,1)S(1)} collective-permute-done((bf16[256,384]{1,0:T(8,128)(2,1)S(1)}, bf16[256,384]{1,0:T(8,128)(2,1)S(1)}, u32[]{:S(2)}, u32[]{:S(2)}) %collective-permute-start.7) | collective-permute-done | bytes 196640 | tf_op jit(solution)/shard_map/ppermute | solution.py:297
  35.5 1.5 %collective-permute-start.23 = (bf16[256,256]{1,0:T(8,128)(2,1)S(1)}, bf16[256,256]{1,0:T(8,128)(2,1)S(1)}, u32[]{:S(2)}, u32[]{:S(2)}) collective-permute-start(bf16[256,256]{1,0:T(8,128)(2,1)S(1)} %collective-permute-done.20), channel_id=1, source_target_pairs={{0,2},{1,3},{2,0},{3,1},{4,6},{5,7},{6,4},{7,5},{8,10},{9,11},{10,... | collective-permute-start | bytes 393224 | tf_op jit(solution)/shard_map/ppermute | solution.py:300
  37.7 4.2 %collective-permute-done.23 = bf16[256,256]{1,0:T(8,128)(2,1)S(1)} collective-permute-done((bf16[256,256]{1,0:T(8,128)(2,1)S(1)}, bf16[256,256]{1,0:T(8,128)(2,1)S(1)}, u32[]{:S(2)}, u32[]{:S(2)}) %collective-permute-start.23) | collective-permute-done | bytes 131104 | tf_op jit(solution)/shard_map/ppermute | solution.py:300
  41.9 1.5 %collective-permute-start.9 = (bf16[256,384]{1,0:T(8,128)(2,1)S(1)}, bf16[256,384]{1,0:T(8,128)(2,1)S(1)}, u32[]{:S(2)}, u32[]{:S(2)}) collective-permute-start(bf16[256,384]{1,0:T(8,128)(2,1)S(1)} %collective-permute-done.6), channel_id=1, source_target_pairs={{0,2},{1,3},{2,0},{3,1},{4,6},{5,7},{6,4},{7,5},{8,10},{9,11},{10,... | collective-permute-start | bytes 589832 | tf_op jit(solution)/shard_map/ppermute | solution.py:300
  43.4 1.3 %collective-permute-done.24 = bf16[256,256]{1,0:T(8,128)(2,1)S(1)} collective-permute-done((bf16[256,256]{1,0:T(8,128)(2,1)S(1)}, bf16[256,256]{1,0:T(8,128)(2,1)S(1)}, u32[]{:S(2)}, u32[]{:S(2)}) %collective-permute-start.24) | collective-permute-done | bytes 131104 | tf_op jit(solution)/shard_map/ppermute | solution.py:300
  44.7 1.5 %collective-permute-start.10 = (bf16[256,384]{1,0:T(8,128)(2,1)S(1)}, bf16[256,384]{1,0:T(8,128)(2,1)S(1)}, u32[]{:S(2)}, u32[]{:S(2)}) collective-permute-start(bf16[256,384]{1,0:T(8,128)(2,1)S(1)} %collective-permute-done.7), channel_id=1, source_target_pairs={{0,2},{1,3},{2,0},{3,1},{4,6},{5,7},{6,4},{7,5},{8,10},{9,11},{10,... | collective-permute-start | bytes 589832 | tf_op jit(solution)/shard_map/ppermute | solution.py:300
  46.2 2.2 %collective-permute-done.9 = bf16[256,384]{1,0:T(8,128)(2,1)S(1)} collective-permute-done((bf16[256,384]{1,0:T(8,128)(2,1)S(1)}, bf16[256,384]{1,0:T(8,128)(2,1)S(1)}, u32[]{:S(2)}, u32[]{:S(2)}) %collective-permute-start.9) | collective-permute-done | bytes 196640 | tf_op jit(solution)/shard_map/ppermute | solution.py:300
  49.3 1.3 %collective-permute-done.10 = bf16[256,384]{1,0:T(8,128)(2,1)S(1)} collective-permute-done((bf16[256,384]{1,0:T(8,128)(2,1)S(1)}, bf16[256,384]{1,0:T(8,128)(2,1)S(1)}, u32[]{:S(2)}, u32[]{:S(2)}) %collective-permute-start.10) | collective-permute-done | bytes 196640 | tf_op jit(solution)/shard_map/ppermute | solution.py:300
  50.6 1.3 %collective-permute-start.25 = (bf16[256,256]{1,0:T(8,128)(2,1)S(1)}, bf16[256,256]{1,0:T(8,128)(2,1)S(1)}, u32[]{:S(2)}, u32[]{:S(2)}) collective-permute-start(bf16[256,256]{1,0:T(8,128)(2,1)S(1)} %collective-permute-done.22), channel_id=1, source_target_pairs={{0,2},{1,3},{2,0},{3,1},{4,6},{5,7},{6,4},{7,5},{8,10},{9,11},{10,... | collective-permute-start | bytes 393224 | tf_op jit(solution)/shard_map/ppermute | solution.py:300
  51.9 3.6 %collective-permute-start.18 = (bf16[136,256]{1,0:T(8,128)(2,1)S(1)}, bf16[136,256]{1,0:T(8,128)(2,1)S(1)}, u32[]{:S(2)}, u32[]{:S(2)}) collective-permute-start(bf16[136,256]{1,0:T(8,128)(2,1)S(1)} %get-tuple-element.40), channel_id=1, source_target_pairs={{0,8},{1,9},{2,10},{3,11},{4,12},{5,13},{6,14},{7,15},{8,0},{9,1},... | collective-permute-start | bytes 208904 | tf_op jit(solution)/shard_map/ppermute | solution.py:297
  55.5 1.9 %collective-permute-start.19 = (bf16[136,256]{1,0:T(8,128)(2,1)S(1)}, bf16[136,256]{1,0:T(8,128)(2,1)S(1)}, u32[]{:S(2)}, u32[]{:S(2)}) collective-permute-start(bf16[136,256]{1,0:T(8,128)(2,1)S(1)} %get-tuple-element.41), channel_id=1, source_target_pairs={{0,12},{1,13},{2,14},{3,15},{4,8},{5,9},{6,10},{7,11},{8,4},{9,5},... | collective-permute-start | bytes 208904 | tf_op jit(solution)/shard_map/ppermute | solution.py:297
  57.8 3.8 %collective-permute-done.19.refs_3_ = bf16[136,256]{1,0:T(8,128)(2,1)S(1)} collective-permute-done((bf16[136,256]{1,0:T(8,128)(2,1)S(1)}, bf16[136,256]{1,0:T(8,128)(2,1)S(1)}, u32[]{:S(2)}, u32[]{:S(2)}) %collective-permute-start.19) | collective-permute-done | bytes 69664 | tf_op jit(solution)/shard_map/ppermute | solution.py:297
  63.5 1.6 %collective-permute-done.27.refs_11_ = bf16[768,256]{1,0:T(8,128)(2,1)} collective-permute-done((bf16[768,256]{1,0:T(8,128)(2,1)S(1)}, bf16[768,256]{1,0:T(8,128)(2,1)}, u32[]{:S(2)}, u32[]{:S(2)}) %collective-permute-start.27) | collective-permute-done | bytes 393248 | tf_op jit(solution)/shard_map/ppermute | solution.py:300
  65.2 1.1 %collective-permute-start.1 = (bf16[136,384]{1,0:T(8,128)(2,1)}, bf16[136,384]{1,0:T(8,128)(2,1)}, u32[]{:S(2)}, u32[]{:S(2)}) collective-permute-start(bf16[136,384]{1,0:T(8,128)(2,1)} %copy-done.11), channel_id=1, source_target_pairs={{0,8},{1,9},{2,10},{3,11},{4,12},{5,13},{6,14},{7,15},{8,0},{9,1},... | collective-permute-start | bytes 313352 | tf_op jit(solution)/shard_map/ppermute | solution.py:297
  66.3 1.6 %collective-permute-start.2 = (bf16[136,384]{1,0:T(8,128)(2,1)}, bf16[136,384]{1,0:T(8,128)(2,1)}, u32[]{:S(2)}, u32[]{:S(2)}) collective-permute-start(bf16[136,384]{1,0:T(8,128)(2,1)} %copy-done.10), channel_id=1, source_target_pairs={{0,12},{1,13},{2,14},{3,15},{4,8},{5,9},{6,10},{7,11},{8,4},{9,5},... | collective-permute-start | bytes 313352 | tf_op jit(solution)/shard_map/ppermute | solution.py:297
  70.8 5.5 %attend.3 = (bf16[128,256]{1,0:T(8,128)(2,1)S(1)}, bf16[128,256]{1,0:T(8,128)(2,1)S(1)}, bf16[128,256]{1,0:T(8,128)(2,1)S(1)}, bf16[128,256]{1,0:T(8,128)(2,1)S(1)}) custom-call(s32[1314]{0:T(1024)S(1)} %concatenate.15.tables_ref, bf16[136,640]{1,0:T(8,128)(2,1)S(1)} %get-tuple-element.27.refs_0_, bf16[136,256]{1,0:T(8,128)(2,1)S(1)} %copy-done.5, ...), custom_call_target="tpu_custom_call" | custom-call | flops 268435456 | bytes 2097152 | tf_op jit(solution)/shard_map/attend/pallas_call | solution.py:242
  76.2 2.3 %collective-permute-start.28 = (bf16[128,256]{1,0:T(8,128)(2,1)S(1)}, bf16[128,256]{1,0:T(8,128)(2,1)S(1)}, u32[]{:S(2)}, u32[]{:S(2)}) collective-permute-start(bf16[128,256]{1,0:T(8,128)(2,1)S(1)} %get-tuple-element.46), channel_id=1, source_target_pairs={{0,12},{1,13},{2,14},{3,15},{4,8},{5,9},{6,10},{7,11},{8,4},{9,5},... | collective-permute-start | bytes 196616 | tf_op jit(solution)/shard_map/ppermute | solution.py:297
  78.5 7.6 %attend.2 = (bf16[128,384]{1,0:T(8,128)(2,1)S(1)}, bf16[128,384]{1,0:T(8,128)(2,1)S(1)}, bf16[128,384]{1,0:T(8,128)(2,1)S(1)}, bf16[128,384]{1,0:T(8,128)(2,1)S(1)}) custom-call(s32[1314]{0:T(1024)S(1)} %concatenate.15.tables_ref, bf16[136,640]{1,0:T(8,128)(2,1)S(1)} %get-tuple-element.27.refs_0_, bf16[136,384]{1,0:T(8,128)(2,1)} %collective-permute-done.refs_1_, ...), custom_call_target="tpu_custom_call" | custom-call | flops 402653184 | bytes 3145728 | tf_op jit(solution)/shard_map/attend/pallas_call | solution.py:242
  86.2 1.7 %collective-permute-start.14 = (bf16[128,384]{1,0:T(8,128)(2,1)S(1)}, bf16[128,384]{1,0:T(8,128)(2,1)S(1)}, u32[]{:S(2)}, u32[]{:S(2)}) collective-permute-start(bf16[128,384]{1,0:T(8,128)(2,1)S(1)} %get-tuple-element.36), channel_id=1, source_target_pairs={{0,12},{1,13},{2,14},{3,15},{4,8},{5,9},{6,10},{7,11},{8,4},{9,5},... | collective-permute-start | bytes 294920 | tf_op jit(solution)/shard_map/ppermute | solution.py:297
  87.8 2.8 %collective-permute-start.16 = (bf16[128,384]{1,0:T(8,128)(2,1)S(1)}, bf16[128,384]{1,0:T(8,128)(2,1)S(1)}, u32[]{:S(2)}, u32[]{:S(2)}) collective-permute-start(bf16[128,384]{1,0:T(8,128)(2,1)S(1)} %get-tuple-element.38), channel_id=1, source_target_pairs={{0,4},{1,5},{2,6},{3,7},{4,0},{5,1},{6,2},{7,3},{8,12},{9,13},{10,... | collective-permute-start | bytes 294920 | tf_op jit(solution)/shard_map/ppermute | solution.py:297
  90.8 2.0 %collective-permute-start.30 = (bf16[128,256]{1,0:T(8,128)(2,1)S(1)}, bf16[128,256]{1,0:T(8,128)(2,1)S(1)}, u32[]{:S(2)}, u32[]{:S(2)}) collective-permute-start(bf16[128,256]{1,0:T(8,128)(2,1)S(1)} %get-tuple-element.48), channel_id=1, source_target_pairs={{0,4},{1,5},{2,6},{3,7},{4,0},{5,1},{6,2},{7,3},{8,12},{9,13},{10,... | collective-permute-start | bytes 196616 | tf_op jit(solution)/shard_map/ppermute | solution.py:297
  92.8 6.5 %collective-permute-done.29.refs_6_ = bf16[128,256]{1,0:T(8,128)(2,1)S(1)} collective-permute-done((bf16[128,256]{1,0:T(8,128)(2,1)S(1)}, bf16[128,256]{1,0:T(8,128)(2,1)S(1)}, u32[]{:S(2)}, u32[]{:S(2)}) %collective-permute-start.29) | collective-permute-done | bytes 65568 | tf_op jit(solution)/shard_map/ppermute | solution.py:297
  (86 shorter events, 9.5 us)
Async XLA Ops:
  0.0 62.7 %copy-start = (s32[32,20,8]{0,2,1:T(8,128)S(1)}, s32[32,20,8]{0,2,1:T(8,128)}, u32[]{:S(2)}) copy-start(s32[32,20,8]{0,2,1:T(8,128)} %param.10) | copy-start | bytes 61444
  2.3 8.5 %collective-permute-start.20 = (bf16[256,256]{1,0:T(8,128)(2,1)S(1)}, bf16[256,256]{1,0:T(8,128)(2,1)S(1)}, u32[]{:S(2)}, u32[]{:S(2)}) collective-permute-start(bf16[256,256]{1,0:T(8,128)(2,1)S(1)} %get-tuple-element.42), channel_id=1, source_target_pairs={{0,4},{1,5},{2,6},{3,7},{4,0},{5,1},{6,2},{7,3},{8,12},{9,13},{10,... | collective-permute-start | bytes 393224 | tf_op jit(solution)/shard_map/ppermute | solution.py:297
  5.4 8.8 %collective-permute-start.21 = (bf16[256,256]{1,0:T(8,128)(2,1)S(1)}, bf16[256,256]{1,0:T(8,128)(2,1)S(1)}, u32[]{:S(2)}, u32[]{:S(2)}) collective-permute-start(bf16[256,256]{1,0:T(8,128)(2,1)S(1)} %get-tuple-element.43), channel_id=1, source_target_pairs={{0,8},{1,9},{2,10},{3,11},{4,12},{5,13},{6,14},{7,15},{8,0},{9,1},... | collective-permute-start | bytes 393224 | tf_op jit(solution)/shard_map/ppermute | solution.py:297
  8.0 54.2 %collective-permute-start.3 = (bf16[256,640]{1,0:T(8,128)(2,1)S(1)}, bf16[256,640]{1,0:T(8,128)(2,1)S(1)}, u32[]{:S(2)}, u32[]{:S(2)}) collective-permute-start(bf16[256,640]{1,0:T(8,128)(2,1)S(1)} %get-tuple-element.31.refs_4_), channel_id=1, source_target_pairs={{0,2},{1,3},{2,0},{3,1},{4,6},{5,7},{6,4},{7,5},{8,10},{9,11},{10,... | collective-permute-start | bytes 983048 | tf_op jit(solution)/shard_map/ppermute | solution.py:300
  9.5 52.8 %collective-permute-start.4 = (bf16[256,640]{1,0:T(8,128)(2,1)S(1)}, bf16[256,640]{1,0:T(8,128)(2,1)S(1)}, u32[]{:S(2)}, u32[]{:S(2)}) collective-permute-start(bf16[256,640]{1,0:T(8,128)(2,1)S(1)} %get-tuple-element.31.refs_4_), channel_id=1, source_target_pairs={{0,1},{1,0},{2,3},{3,2},{4,5},{5,4},{6,7},{7,6},{8,9},{9,8},{10,11... | collective-permute-start | bytes 983048 | tf_op jit(solution)/shard_map/ppermute | solution.py:300
  9.5 8.3 %collective-permute-start.22 = (bf16[256,256]{1,0:T(8,128)(2,1)S(1)}, bf16[256,256]{1,0:T(8,128)(2,1)S(1)}, u32[]{:S(2)}, u32[]{:S(2)}) collective-permute-start(bf16[256,256]{1,0:T(8,128)(2,1)S(1)} %get-tuple-element.44), channel_id=1, source_target_pairs={{0,12},{1,13},{2,14},{3,15},{4,8},{5,9},{6,10},{7,11},{8,4},{9,5},... | collective-permute-start | bytes 393224 | tf_op jit(solution)/shard_map/ppermute | solution.py:297
  10.8 41.1 %collective-permute-start.17 = (bf16[136,256]{1,0:T(8,128)(2,1)S(1)}, bf16[136,256]{1,0:T(8,128)(2,1)S(1)}, u32[]{:S(2)}, u32[]{:S(2)}) collective-permute-start(bf16[136,256]{1,0:T(8,128)(2,1)S(1)} %get-tuple-element.39), channel_id=1, source_target_pairs={{0,4},{1,5},{2,6},{3,7},{4,0},{5,1},{6,2},{7,3},{8,12},{9,13},{10,... | collective-permute-start | bytes 208904 | tf_op jit(solution)/shard_map/ppermute | solution.py:297
  14.3 10.5 %collective-permute-start.6 = (bf16[256,384]{1,0:T(8,128)(2,1)S(1)}, bf16[256,384]{1,0:T(8,128)(2,1)S(1)}, u32[]{:S(2)}, u32[]{:S(2)}) collective-permute-start(bf16[256,384]{1,0:T(8,128)(2,1)S(1)} %get-tuple-element.32), channel_id=1, source_target_pairs={{0,4},{1,5},{2,6},{3,7},{4,0},{5,1},{6,2},{7,3},{8,12},{9,13},{10,... | collective-permute-start | bytes 589832 | tf_op jit(solution)/shard_map/ppermute | solution.py:297
  17.8 17.7 %collective-permute-start.7 = (bf16[256,384]{1,0:T(8,128)(2,1)S(1)}, bf16[256,384]{1,0:T(8,128)(2,1)S(1)}, u32[]{:S(2)}, u32[]{:S(2)}) collective-permute-start(bf16[256,384]{1,0:T(8,128)(2,1)S(1)} %get-tuple-element.33), channel_id=1, source_target_pairs={{0,8},{1,9},{2,10},{3,11},{4,12},{5,13},{6,14},{7,15},{8,0},{9,1},... | collective-permute-start | bytes 589832 | tf_op jit(solution)/shard_map/ppermute | solution.py:297
  24.8 12.3 %collective-permute-start.8 = (bf16[256,384]{1,0:T(8,128)(2,1)S(1)}, bf16[256,384]{1,0:T(8,128)(2,1)S(1)}, u32[]{:S(2)}, u32[]{:S(2)}) collective-permute-start(bf16[256,384]{1,0:T(8,128)(2,1)S(1)} %get-tuple-element.34), channel_id=1, source_target_pairs={{0,12},{1,13},{2,14},{3,15},{4,8},{5,9},{6,10},{7,11},{8,4},{9,5},... | collective-permute-start | bytes 589832 | tf_op jit(solution)/shard_map/ppermute | solution.py:297
  35.5 6.4 %collective-permute-start.23 = (bf16[256,256]{1,0:T(8,128)(2,1)S(1)}, bf16[256,256]{1,0:T(8,128)(2,1)S(1)}, u32[]{:S(2)}, u32[]{:S(2)}) collective-permute-start(bf16[256,256]{1,0:T(8,128)(2,1)S(1)} %collective-permute-done.20), channel_id=1, source_target_pairs={{0,2},{1,3},{2,0},{3,1},{4,6},{5,7},{6,4},{7,5},{8,10},{9,11},{10,... | collective-permute-start | bytes 393224 | tf_op jit(solution)/shard_map/ppermute | solution.py:300
  37.1 7.6 %collective-permute-start.24 = (bf16[256,256]{1,0:T(8,128)(2,1)S(1)}, bf16[256,256]{1,0:T(8,128)(2,1)S(1)}, u32[]{:S(2)}, u32[]{:S(2)}) collective-permute-start(bf16[256,256]{1,0:T(8,128)(2,1)S(1)} %collective-permute-done.21), channel_id=1, source_target_pairs={{0,2},{1,3},{2,0},{3,1},{4,6},{5,7},{6,4},{7,5},{8,10},{9,11},{10,... | collective-permute-start | bytes 393224 | tf_op jit(solution)/shard_map/ppermute | solution.py:300
  41.9 6.6 %collective-permute-start.9 = (bf16[256,384]{1,0:T(8,128)(2,1)S(1)}, bf16[256,384]{1,0:T(8,128)(2,1)S(1)}, u32[]{:S(2)}, u32[]{:S(2)}) collective-permute-start(bf16[256,384]{1,0:T(8,128)(2,1)S(1)} %collective-permute-done.6), channel_id=1, source_target_pairs={{0,2},{1,3},{2,0},{3,1},{4,6},{5,7},{6,4},{7,5},{8,10},{9,11},{10,... | collective-permute-start | bytes 589832 | tf_op jit(solution)/shard_map/ppermute | solution.py:300
  44.7 5.9 %collective-permute-start.10 = (bf16[256,384]{1,0:T(8,128)(2,1)S(1)}, bf16[256,384]{1,0:T(8,128)(2,1)S(1)}, u32[]{:S(2)}, u32[]{:S(2)}) collective-permute-start(bf16[256,384]{1,0:T(8,128)(2,1)S(1)} %collective-permute-done.7), channel_id=1, source_target_pairs={{0,2},{1,3},{2,0},{3,1},{4,6},{5,7},{6,4},{7,5},{8,10},{9,11},{10,... | collective-permute-start | bytes 589832 | tf_op jit(solution)/shard_map/ppermute | solution.py:300
  48.5 7.0 %collective-permute-start.11 = (bf16[256,384]{1,0:T(8,128)(2,1)S(1)}, bf16[256,384]{1,0:T(8,128)(2,1)S(1)}, u32[]{:S(2)}, u32[]{:S(2)}) collective-permute-start(bf16[256,384]{1,0:T(8,128)(2,1)S(1)} %collective-permute-done.8), channel_id=1, source_target_pairs={{0,2},{1,3},{2,0},{3,1},{4,6},{5,7},{6,4},{7,5},{8,10},{9,11},{10,... | collective-permute-start | bytes 589832 | tf_op jit(solution)/shard_map/ppermute | solution.py:300
  50.6 11.0 %collective-permute-start.25 = (bf16[256,256]{1,0:T(8,128)(2,1)S(1)}, bf16[256,256]{1,0:T(8,128)(2,1)S(1)}, u32[]{:S(2)}, u32[]{:S(2)}) collective-permute-start(bf16[256,256]{1,0:T(8,128)(2,1)S(1)} %collective-permute-done.22), channel_id=1, source_target_pairs={{0,2},{1,3},{2,0},{3,1},{4,6},{5,7},{6,4},{7,5},{8,10},{9,11},{10,... | collective-permute-start | bytes 393224 | tf_op jit(solution)/shard_map/ppermute | solution.py:300
  51.9 5.9 %collective-permute-start.18 = (bf16[136,256]{1,0:T(8,128)(2,1)S(1)}, bf16[136,256]{1,0:T(8,128)(2,1)S(1)}, u32[]{:S(2)}, u32[]{:S(2)}) collective-permute-start(bf16[136,256]{1,0:T(8,128)(2,1)S(1)} %get-tuple-element.40), channel_id=1, source_target_pairs={{0,8},{1,9},{2,10},{3,11},{4,12},{5,13},{6,14},{7,15},{8,0},{9,1},... | collective-permute-start | bytes 208904 | tf_op jit(solution)/shard_map/ppermute | solution.py:297
  55.5 6.1 %collective-permute-start.19 = (bf16[136,256]{1,0:T(8,128)(2,1)S(1)}, bf16[136,256]{1,0:T(8,128)(2,1)S(1)}, u32[]{:S(2)}, u32[]{:S(2)}) collective-permute-start(bf16[136,256]{1,0:T(8,128)(2,1)S(1)} %get-tuple-element.41), channel_id=1, source_target_pairs={{0,12},{1,13},{2,14},{3,15},{4,8},{5,9},{6,10},{7,11},{8,4},{9,5},... | collective-permute-start | bytes 208904 | tf_op jit(solution)/shard_map/ppermute | solution.py:297
  57.8 5.7 %collective-permute-start.26 = (bf16[768,256]{1,0:T(8,128)(2,1)S(1)}, bf16[768,256]{1,0:T(8,128)(2,1)}, u32[]{:S(2)}, u32[]{:S(2)}) collective-permute-start(bf16[768,256]{1,0:T(8,128)(2,1)S(1)} %constant_dynamic-update-slice_fusion.6.refs_8_), channel_id=1, source_target_pairs={{0,1},{1,0},{2,3},{3,2},{4,5},{5,4},{6,7},{7,6},{8,9},{9,8},{10,11... | collective-permute-start | bytes 1179656 | tf_op jit(solution)/shard_map/ppermute | solution.py:300
  61.6 16.9 %collective-permute-start.12 = (bf16[768,384]{1,0:T(8,128)(2,1)S(1)}, bf16[768,384]{1,0:T(8,128)(2,1)}, u32[]{:S(2)}, u32[]{:S(2)}) collective-permute-start(bf16[768,384]{1,0:T(8,128)(2,1)S(1)} %constant_dynamic-update-slice_fusion.refs_8_), channel_id=1, source_target_pairs={{0,1},{1,0},{2,3},{3,2},{4,5},{5,4},{6,7},{7,6},{8,9},{9,8},{10,11... | collective-permute-start | bytes 1769480 | tf_op jit(solution)/shard_map/ppermute | solution.py:300
  61.6 16.9 %collective-permute-start.13 = (bf16[768,384]{1,0:T(8,128)(2,1)S(1)}, bf16[768,384]{1,0:T(8,128)(2,1)}, u32[]{:S(2)}, u32[]{:S(2)}) collective-permute-start(bf16[768,384]{1,0:T(8,128)(2,1)S(1)} %constant_dynamic-update-slice_fusion.3.refs_9_), channel_id=1, source_target_pairs={{0,1},{1,0},{2,3},{3,2},{4,5},{5,4},{6,7},{7,6},{8,9},{9,8},{10,11... | collective-permute-start | bytes 1769480 | tf_op jit(solution)/shard_map/ppermute | solution.py:300
  62.2 2.9 %collective-permute-start.27 = (bf16[768,256]{1,0:T(8,128)(2,1)S(1)}, bf16[768,256]{1,0:T(8,128)(2,1)}, u32[]{:S(2)}, u32[]{:S(2)}) collective-permute-start(bf16[768,256]{1,0:T(8,128)(2,1)S(1)} %constant_dynamic-update-slice_fusion.9.refs_9_), channel_id=1, source_target_pairs={{0,1},{1,0},{2,3},{3,2},{4,5},{5,4},{6,7},{7,6},{8,9},{9,8},{10,11... | collective-permute-start | bytes 1179656 | tf_op jit(solution)/shard_map/ppermute | solution.py:300
  62.3 4.0 %collective-permute-start.5 = (bf16[256,640]{1,0:T(8,128)(2,1)S(1)}, bf16[256,640]{1,0:T(8,128)(2,1)S(1)}, u32[]{:S(2)}, u32[]{:S(2)}) collective-permute-start(bf16[256,640]{1,0:T(8,128)(2,1)S(1)} %collective-permute-done.3.refs_5_), channel_id=1, source_target_pairs={{0,1},{1,0},{2,3},{3,2},{4,5},{5,4},{6,7},{7,6},{8,9},{9,8},{10,11... | collective-permute-start | bytes 983048 | tf_op jit(solution)/shard_map/ppermute | solution.py:300
  63.4 12.8 %collective-permute-start = (bf16[136,384]{1,0:T(8,128)(2,1)}, bf16[136,384]{1,0:T(8,128)(2,1)}, u32[]{:S(2)}, u32[]{:S(2)}) collective-permute-start(bf16[136,384]{1,0:T(8,128)(2,1)} %copy-done.12), channel_id=1, source_target_pairs={{0,4},{1,5},{2,6},{3,7},{4,0},{5,1},{6,2},{7,3},{8,12},{9,13},{10,... | collective-permute-start | bytes 313352 | tf_op jit(solution)/shard_map/ppermute | solution.py:297
  65.2 13.4 %collective-permute-start.1 = (bf16[136,384]{1,0:T(8,128)(2,1)}, bf16[136,384]{1,0:T(8,128)(2,1)}, u32[]{:S(2)}, u32[]{:S(2)}) collective-permute-start(bf16[136,384]{1,0:T(8,128)(2,1)} %copy-done.11), channel_id=1, source_target_pairs={{0,8},{1,9},{2,10},{3,11},{4,12},{5,13},{6,14},{7,15},{8,0},{9,1},... | collective-permute-start | bytes 313352 | tf_op jit(solution)/shard_map/ppermute | solution.py:297
  66.3 12.2 %collective-permute-start.2 = (bf16[136,384]{1,0:T(8,128)(2,1)}, bf16[136,384]{1,0:T(8,128)(2,1)}, u32[]{:S(2)}, u32[]{:S(2)}) collective-permute-start(bf16[136,384]{1,0:T(8,128)(2,1)} %copy-done.10), channel_id=1, source_target_pairs={{0,12},{1,13},{2,14},{3,15},{4,8},{5,9},{6,10},{7,11},{8,4},{9,5},... | collective-permute-start | bytes 313352 | tf_op jit(solution)/shard_map/ppermute | solution.py:297
  76.2 14.5 %collective-permute-start.28 = (bf16[128,256]{1,0:T(8,128)(2,1)S(1)}, bf16[128,256]{1,0:T(8,128)(2,1)S(1)}, u32[]{:S(2)}, u32[]{:S(2)}) collective-permute-start(bf16[128,256]{1,0:T(8,128)(2,1)S(1)} %get-tuple-element.46), channel_id=1, source_target_pairs={{0,12},{1,13},{2,14},{3,15},{4,8},{5,9},{6,10},{7,11},{8,4},{9,5},... | collective-permute-start | bytes 196616 | tf_op jit(solution)/shard_map/ppermute | solution.py:297
  86.2 13.1 %collective-permute-start.14 = (bf16[128,384]{1,0:T(8,128)(2,1)S(1)}, bf16[128,384]{1,0:T(8,128)(2,1)S(1)}, u32[]{:S(2)}, u32[]{:S(2)}) collective-permute-start(bf16[128,384]{1,0:T(8,128)(2,1)S(1)} %get-tuple-element.36), channel_id=1, source_target_pairs={{0,12},{1,13},{2,14},{3,15},{4,8},{5,9},{6,10},{7,11},{8,4},{9,5},... | collective-permute-start | bytes 294920 | tf_op jit(solution)/shard_map/ppermute | solution.py:297
  87.8 11.4 %collective-permute-start.15 = (bf16[128,384]{1,0:T(8,128)(2,1)S(1)}, bf16[128,384]{1,0:T(8,128)(2,1)S(1)}, u32[]{:S(2)}, u32[]{:S(2)}) collective-permute-start(bf16[128,384]{1,0:T(8,128)(2,1)S(1)} %get-tuple-element.37), channel_id=1, source_target_pairs={{0,8},{1,9},{2,10},{3,11},{4,12},{5,13},{6,14},{7,15},{8,0},{9,1},... | collective-permute-start | bytes 294920 | tf_op jit(solution)/shard_map/ppermute | solution.py:297
  87.8 11.4 %collective-permute-start.16 = (bf16[128,384]{1,0:T(8,128)(2,1)S(1)}, bf16[128,384]{1,0:T(8,128)(2,1)S(1)}, u32[]{:S(2)}, u32[]{:S(2)}) collective-permute-start(bf16[128,384]{1,0:T(8,128)(2,1)S(1)} %get-tuple-element.38), channel_id=1, source_target_pairs={{0,4},{1,5},{2,6},{3,7},{4,0},{5,1},{6,2},{7,3},{8,12},{9,13},{10,... | collective-permute-start | bytes 294920 | tf_op jit(solution)/shard_map/ppermute | solution.py:297
  90.6 8.7 %collective-permute-start.29 = (bf16[128,256]{1,0:T(8,128)(2,1)S(1)}, bf16[128,256]{1,0:T(8,128)(2,1)S(1)}, u32[]{:S(2)}, u32[]{:S(2)}) collective-permute-start(bf16[128,256]{1,0:T(8,128)(2,1)S(1)} %get-tuple-element.47), channel_id=1, source_target_pairs={{0,8},{1,9},{2,10},{3,11},{4,12},{5,13},{6,14},{7,15},{8,0},{9,1},... | collective-permute-start | bytes 196616 | tf_op jit(solution)/shard_map/ppermute | solution.py:297
  90.8 8.5 %collective-permute-start.30 = (bf16[128,256]{1,0:T(8,128)(2,1)S(1)}, bf16[128,256]{1,0:T(8,128)(2,1)S(1)}, u32[]{:S(2)}, u32[]{:S(2)}) collective-permute-start(bf16[128,256]{1,0:T(8,128)(2,1)S(1)} %get-tuple-element.48), channel_id=1, source_target_pairs={{0,4},{1,5},{2,6},{3,7},{4,0},{5,1},{6,2},{7,3},{8,12},{9,13},{10,... | collective-permute-start | bytes 196616 | tf_op jit(solution)/shard_map/ppermute | solution.py:297
  (15 other events, 39.9 us)

commit v4 on v3

--- a/solution.py
+++ b/solution.py
@@ -11,7 +11,7 @@
 
 CUBE = 64
 GATE_ROWS = 8
-CHUNKS = (3, 2)
+CHUNKS = ((2, 1), (2,))
 POOL_ROWS = 1024
 HELD_BYTES = 8 << 20
 SMALL_VMEM = 12 << 20
@@ -20,12 +20,14 @@
 VMEM = pl.BlockSpec(memory_space=pltpu.VMEM)
 SMEM = pl.BlockSpec(memory_space=pltpu.SMEM)
 ANY = pl.BlockSpec(memory_space=pl.ANY)
+HBM = pl.BlockSpec(memory_space=pltpu.MemorySpace.HBM)
 TRANSPOSED = (((1,), (1,)), ((), ()))
 
 
 def pack_kernel(jobs, width, index_ref, *refs):
-    sources = refs[: 1 + max(max(rows) for rows, _ in jobs)]
+    sources, refs, sems = refs[: 1 + max(max(rows) for rows, _ in jobs)], refs[:-1], refs[-1]
     outputs = iter(refs[len(sources) :])
+    copies = []
     for numbers, spans in jobs:
         for relative, begin, size in spans:
             head_group = index_ref[0] ^ relative
@@ -33,8 +35,12 @@
             out, row = next(outputs), 0
             for number in numbers:
                 rows = sources[number].shape[0]
-                out[row : row + rows, :] = sources[number][:, columns]
+                source, target = sources[number].at[:, columns], out.at[pl.ds(row, rows), :]
+                copies.append(pltpu.make_async_copy(source, target, sems.at[len(copies)]))
+                copies[-1].start()
                 row += rows
+    for copy in copies:
+        copy.wait()
 
 
 def pack(index, jobs, width):
@@ -52,8 +58,9 @@
     return pl.pallas_call(
         functools.partial(pack_kernel, tuple(numbered), width),
         out_shape=shapes,
-        in_specs=[SMEM] + [VMEM] * len(operands),
+        in_specs=[SMEM] + [HBM] * len(operands),
         out_specs=[VMEM] * len(shapes),
+        scratch_shapes=[pltpu.SemaphoreType.DMA((sum(len(n) * len(p) for n, p in numbered),))],
         compiler_params=pltpu.CompilerParams(vmem_limit_bytes=SMALL_VMEM),
         name="pack",
     )(index, *operands)
@@ -288,7 +295,8 @@
     home = self_index // ring
     place = self_index % ring
 
-    counts = CHUNKS if sum(CHUNKS) == heads else (heads,)
+    chunks = CHUNKS if sum(map(sum, CHUNKS)) == heads else ((heads,),)
+    counts = [sum(parts) for parts in chunks]
     firsts = [sum(counts[:i]) for i in range(len(counts))]
     spans = [(first * head_size, count * head_size) for first, count in zip(firsts, counts)]
 
@@ -354,14 +362,20 @@
         if len(steps) > 2:
             stores = [jnp.concatenate(stores, axis=0)]
         stores = gather(stores, 1)
-        outs = attend(
-            tables,
-            [queries_sent[0]] + [queries[r] for r in range(1, groups)],
-            [begin] + [0] * (groups - 1),
-            own_stores + stores,
-            [begin] * len(own_stores) + [0] * len(stores),
-            (local, cubes, heads, firsts[c], counts[c], picks, head_size),
-        )
+        parts, offset = [], 0
+        for count in chunks[c]:
+            columns = offset * head_size
+            outs = attend(
+                tables,
+                [queries_sent[0]] + [queries[r] for r in range(1, groups)],
+                [begin + columns] + [columns] * (groups - 1),
+                own_stores + stores,
+                [begin + columns] * len(own_stores) + [columns] * len(stores),
+                (local, cubes, heads, firsts[c] + offset, count, picks, head_size),
+            )
+            parts.append(outs)
+            offset += count
+        outs = [jnp.concatenate(part, axis=1) if len(part) > 1 else part[0] for part in zip(*parts)]
         pieces.append(outs[0])
         for r in order:
             pieces.append(over_groups(outs[r], r))

time: 101 us -> 104 us (1.030)
  waiting for transfers between devices: 36.1 us -> 30.6 us
  local copies, waits for them, and re-layouts: 6.61 us -> 11.8 us
  Pallas kernels: 14.1 us -> 17.4 us
    ppermute x18, waiting for transfers between devices: 25.4 us -> 21.7 us  [over_groups(): return lax.ppermute(value, 'cubes', pairs)]
    unnamed x40 -> x38, local copies, waits for them, and re-layouts: 5.75 us -> 8.33 us
    pallas_call x2 -> x3, Pallas kernels: 13.1 us -> 15.3 us  [attend(): pl.pallas_call(functools.partial(attend_kernel, shape), out_shape=[out] *...]
    ppermute x13, waiting for transfers between devices: 10.7 us -> 8.88 us  [over_ring(): return lax.ppermute(value, 'cubes', [(i, i ^ step) for i in range(devices)])]
    concatenate x4, local copies, waits for them, and re-layouts: 0.08 us -> 1.38 us  [body(): jnp.concatenate([part[r] for r in range(1, groups)], axis=0)]
    concatenate x1, local copies, waits for them, and re-layouts: 0.08 us -> 1.37 us  [body(): jnp.concatenate((row_of_cube, chosen.reshape(-1), index, place.reshape(1)))]
    pallas_call x2, Pallas kernels: 0.17 us -> 1.27 us  [pack(): pl.pallas_call(functools.partial(pack_kernel, tuple(numbered), width), ou...]
  transfers between devices with their start and end apart: 31 -> 31, of which waited for: 12 -> 11; matrix products, arithmetic and copies ran while one was open for 1% -> 6% of each run, Pallas kernels for 13% -> 16%
where the time goes in v4:
time: 104 us
  starting transfers between devices  43.5 us (42%)
  waiting for transfers between devices  30.6 us (29%)
  Pallas kernels  17.4 us (17%)
  local copies, waits for them, and re-layouts  11.8 us (11%)
    ppermute x18, starting transfers between devices, over_groups(): return lax.ppermute(value, 'cubes', pairs)  34 us
    ppermute x18, waiting for transfers between devices, over_groups(): return lax.ppermute(value, 'cubes', pairs)  21.7 us
    pallas_call x3, Pallas kernels, attend(): pl.pallas_call(functools.partial(attend_kernel, shape), out_shape=[out] *...  15.3 us
    ppermute x13, starting transfers between devices, over_ring(): return lax.ppermute(value, 'cubes', [(i, i ^ step) for i in range(devices)])  9.45 us
    ppermute x13, waiting for transfers between devices, over_ring(): return lax.ppermute(value, 'cubes', [(i, i ^ step) for i in range(devices)])  8.88 us
    unnamed x38, local copies, waits for them, and re-layouts  8.33 us
  transfers between devices with their start and end apart: 31, of which 11 were waited for; matrix products, arithmetic and copies ran while one was open for 6% of the time, Pallas kernels for 16%

profile of v4, /device:TPU:0, one launch (start us, length us, event | category | flops | bytes accessed | tf_op | source)
XLA Modules:
  0.0 103.7 jit_solution(13355635205960614321)
XLA Ops:
  0.0 1.1 %copy-done.1 = bf16[128,2560]{1,0:T(8,128)(2,1)S(1)} copy-done((bf16[128,2560]{1,0:T(8,128)(2,1)S(1)}, bf16[128,2560]{1,0:T(8,128)(2,1)}, u32[]{:S(2)}) %copy-start.1) | copy-done | bytes 655384
  1.1 1.1 %copy-done.2 = bf16[128,2560]{1,0:T(8,128)(2,1)S(1)} copy-done((bf16[128,2560]{1,0:T(8,128)(2,1)S(1)}, bf16[128,2560]{1,0:T(8,128)(2,1)}, u32[]{:S(2)}) %copy-start.2) | copy-done | bytes 655384
  2.5 3.1 %collective-permute-start.20 = (bf16[256,256]{1,0:T(8,128)(2,1)S(1)}, bf16[256,256]{1,0:T(8,128)(2,1)S(1)}, u32[]{:S(2)}, u32[]{:S(2)}) collective-permute-start(bf16[256,256]{1,0:T(8,128)(2,1)S(1)} %get-tuple-element.50), channel_id=1, source_target_pairs={{0,4},{1,5},{2,6},{3,7},{4,0},{5,1},{6,2},{7,3},{8,12},{9,13},{10,... | collective-permute-start | bytes 393224 | tf_op jit(solution)/shard_map/ppermute | solution.py:305
  5.7 2.6 %collective-permute-start.21 = (bf16[256,256]{1,0:T(8,128)(2,1)S(1)}, bf16[256,256]{1,0:T(8,128)(2,1)S(1)}, u32[]{:S(2)}, u32[]{:S(2)}) collective-permute-start(bf16[256,256]{1,0:T(8,128)(2,1)S(1)} %get-tuple-element.51), channel_id=1, source_target_pairs={{0,8},{1,9},{2,10},{3,11},{4,12},{5,13},{6,14},{7,15},{8,0},{9,1},... | collective-permute-start | bytes 393224 | tf_op jit(solution)/shard_map/ppermute | solution.py:305
  8.3 1.5 %collective-permute-start.3 = (bf16[256,640]{1,0:T(8,128)(2,1)S(1)}, bf16[256,640]{1,0:T(8,128)(2,1)S(1)}, u32[]{:S(2)}, u32[]{:S(2)}) collective-permute-start(bf16[256,640]{1,0:T(8,128)(2,1)S(1)} %get-tuple-element.35.refs_4_), channel_id=1, source_target_pairs={{0,2},{1,3},{2,0},{3,1},{4,6},{5,7},{6,4},{7,5},{8,10},{9,11},{10,... | collective-permute-start | bytes 983048 | tf_op jit(solution)/shard_map/ppermute | solution.py:308
  12.4 2.1 %collective-permute-done.21 = bf16[256,256]{1,0:T(8,128)(2,1)S(1)} collective-permute-done((bf16[256,256]{1,0:T(8,128)(2,1)S(1)}, bf16[256,256]{1,0:T(8,128)(2,1)S(1)}, u32[]{:S(2)}, u32[]{:S(2)}) %collective-permute-start.21) | collective-permute-done | bytes 131104 | tf_op jit(solution)/shard_map/ppermute | solution.py:305
  14.5 3.5 %collective-permute-start.6 = (bf16[256,384]{1,0:T(8,128)(2,1)S(1)}, bf16[256,384]{1,0:T(8,128)(2,1)S(1)}, u32[]{:S(2)}, u32[]{:S(2)}) collective-permute-start(bf16[256,384]{1,0:T(8,128)(2,1)S(1)} %get-tuple-element.36), channel_id=1, source_target_pairs={{0,4},{1,5},{2,6},{3,7},{4,0},{5,1},{6,2},{7,3},{8,12},{9,13},{10,... | collective-permute-start | bytes 589832 | tf_op jit(solution)/shard_map/ppermute | solution.py:305
  18.7 3.4 %collective-permute-start.7 = (bf16[256,384]{1,0:T(8,128)(2,1)S(1)}, bf16[256,384]{1,0:T(8,128)(2,1)S(1)}, u32[]{:S(2)}, u32[]{:S(2)}) collective-permute-start(bf16[256,384]{1,0:T(8,128)(2,1)S(1)} %get-tuple-element.37), channel_id=1, source_target_pairs={{0,8},{1,9},{2,10},{3,11},{4,12},{5,13},{6,14},{7,15},{8,0},{9,1},... | collective-permute-start | bytes 589832 | tf_op jit(solution)/shard_map/ppermute | solution.py:305
  22.7 2.3 %collective-permute-done.6 = bf16[256,384]{1,0:T(8,128)(2,1)S(1)} collective-permute-done((bf16[256,384]{1,0:T(8,128)(2,1)S(1)}, bf16[256,384]{1,0:T(8,128)(2,1)S(1)}, u32[]{:S(2)}, u32[]{:S(2)}) %collective-permute-start.6) | collective-permute-done | bytes 196640 | tf_op jit(solution)/shard_map/ppermute | solution.py:305
  25.0 2.6 %collective-permute-start.8 = (bf16[256,384]{1,0:T(8,128)(2,1)S(1)}, bf16[256,384]{1,0:T(8,128)(2,1)S(1)}, u32[]{:S(2)}, u32[]{:S(2)}) collective-permute-start(bf16[256,384]{1,0:T(8,128)(2,1)S(1)} %get-tuple-element.38), channel_id=1, source_target_pairs={{0,12},{1,13},{2,14},{3,15},{4,8},{5,9},{6,10},{7,11},{8,4},{9,5},... | collective-permute-start | bytes 589832 | tf_op jit(solution)/shard_map/ppermute | solution.py:305
  27.7 8.5 %collective-permute-done.7 = bf16[256,384]{1,0:T(8,128)(2,1)S(1)} collective-permute-done((bf16[256,384]{1,0:T(8,128)(2,1)S(1)}, bf16[256,384]{1,0:T(8,128)(2,1)S(1)}, u32[]{:S(2)}, u32[]{:S(2)}) %collective-permute-start.7) | collective-permute-done | bytes 196640 | tf_op jit(solution)/shard_map/ppermute | solution.py:305
  36.2 1.3 %collective-permute-start.23 = (bf16[256,256]{1,0:T(8,128)(2,1)S(1)}, bf16[256,256]{1,0:T(8,128)(2,1)S(1)}, u32[]{:S(2)}, u32[]{:S(2)}) collective-permute-start(bf16[256,256]{1,0:T(8,128)(2,1)S(1)} %collective-permute-done.20), channel_id=1, source_target_pairs={{0,2},{1,3},{2,0},{3,1},{4,6},{5,7},{6,4},{7,5},{8,10},{9,11},{10,... | collective-permute-start | bytes 393224 | tf_op jit(solution)/shard_map/ppermute | solution.py:308
  38.3 4.2 %collective-permute-done.23 = bf16[256,256]{1,0:T(8,128)(2,1)S(1)} collective-permute-done((bf16[256,256]{1,0:T(8,128)(2,1)S(1)}, bf16[256,256]{1,0:T(8,128)(2,1)S(1)}, u32[]{:S(2)}, u32[]{:S(2)}) %collective-permute-start.23) | collective-permute-done | bytes 131104 | tf_op jit(solution)/shard_map/ppermute | solution.py:308
  42.5 1.3 %collective-permute-start.9 = (bf16[256,384]{1,0:T(8,128)(2,1)S(1)}, bf16[256,384]{1,0:T(8,128)(2,1)S(1)}, u32[]{:S(2)}, u32[]{:S(2)}) collective-permute-start(bf16[256,384]{1,0:T(8,128)(2,1)S(1)} %collective-permute-done.6), channel_id=1, source_target_pairs={{0,2},{1,3},{2,0},{3,1},{4,6},{5,7},{6,4},{7,5},{8,10},{9,11},{10,... | collective-permute-start | bytes 589832 | tf_op jit(solution)/shard_map/ppermute | solution.py:308
  45.3 1.3 %collective-permute-start.10 = (bf16[256,384]{1,0:T(8,128)(2,1)S(1)}, bf16[256,384]{1,0:T(8,128)(2,1)S(1)}, u32[]{:S(2)}, u32[]{:S(2)}) collective-permute-start(bf16[256,384]{1,0:T(8,128)(2,1)S(1)} %collective-permute-done.7), channel_id=1, source_target_pairs={{0,2},{1,3},{2,0},{3,1},{4,6},{5,7},{6,4},{7,5},{8,10},{9,11},{10,... | collective-permute-start | bytes 589832 | tf_op jit(solution)/shard_map/ppermute | solution.py:308
  47.3 1.3 %collective-permute-done.9 = bf16[256,384]{1,0:T(8,128)(2,1)S(1)} collective-permute-done((bf16[256,384]{1,0:T(8,128)(2,1)S(1)}, bf16[256,384]{1,0:T(8,128)(2,1)S(1)}, u32[]{:S(2)}, u32[]{:S(2)}) %collective-permute-start.9) | collective-permute-done | bytes 196640 | tf_op jit(solution)/shard_map/ppermute | solution.py:308
  49.5 1.5 %collective-permute-done.10 = bf16[256,384]{1,0:T(8,128)(2,1)S(1)} collective-permute-done((bf16[256,384]{1,0:T(8,128)(2,1)S(1)}, bf16[256,384]{1,0:T(8,128)(2,1)S(1)}, u32[]{:S(2)}, u32[]{:S(2)}) %collective-permute-start.10) | collective-permute-done | bytes 196640 | tf_op jit(solution)/shard_map/ppermute | solution.py:308
  51.0 1.3 %collective-permute-start.25 = (bf16[256,256]{1,0:T(8,128)(2,1)S(1)}, bf16[256,256]{1,0:T(8,128)(2,1)S(1)}, u32[]{:S(2)}, u32[]{:S(2)}) collective-permute-start(bf16[256,256]{1,0:T(8,128)(2,1)S(1)} %collective-permute-done.22), channel_id=1, source_target_pairs={{0,2},{1,3},{2,0},{3,1},{4,6},{5,7},{6,4},{7,5},{8,10},{9,11},{10,... | collective-permute-start | bytes 393224 | tf_op jit(solution)/shard_map/ppermute | solution.py:308
  52.4 3.4 %collective-permute-start.18 = (bf16[136,256]{1,0:T(8,128)(2,1)S(1)}, bf16[136,256]{1,0:T(8,128)(2,1)S(1)}, u32[]{:S(2)}, u32[]{:S(2)}) collective-permute-start(bf16[136,256]{1,0:T(8,128)(2,1)S(1)} %get-tuple-element.48), channel_id=1, source_target_pairs={{0,8},{1,9},{2,10},{3,11},{4,12},{5,13},{6,14},{7,15},{8,0},{9,1},... | collective-permute-start | bytes 208904 | tf_op jit(solution)/shard_map/ppermute | solution.py:305
  55.7 2.0 %collective-permute-start.19 = (bf16[136,256]{1,0:T(8,128)(2,1)S(1)}, bf16[136,256]{1,0:T(8,128)(2,1)S(1)}, u32[]{:S(2)}, u32[]{:S(2)}) collective-permute-start(bf16[136,256]{1,0:T(8,128)(2,1)S(1)} %get-tuple-element.49), channel_id=1, source_target_pairs={{0,12},{1,13},{2,14},{3,15},{4,8},{5,9},{6,10},{7,11},{8,4},{9,5},... | collective-permute-start | bytes 208904 | tf_op jit(solution)/shard_map/ppermute | solution.py:305
  58.0 3.8 %collective-permute-done.19.refs_3_ = bf16[136,256]{1,0:T(8,128)(2,1)S(1)} collective-permute-done((bf16[136,256]{1,0:T(8,128)(2,1)S(1)}, bf16[136,256]{1,0:T(8,128)(2,1)S(1)}, u32[]{:S(2)}, u32[]{:S(2)}) %collective-permute-start.19) | collective-permute-done | bytes 69664 | tf_op jit(solution)/shard_map/ppermute | solution.py:305
  65.4 1.6 %collective-permute-start.1 = (bf16[136,384]{1,0:T(8,128)(2,1)}, bf16[136,384]{1,0:T(8,128)(2,1)S(1)}, u32[]{:S(2)}, u32[]{:S(2)}) collective-permute-start(bf16[136,384]{1,0:T(8,128)(2,1)} %copy-done.12), channel_id=1, source_target_pairs={{0,8},{1,9},{2,10},{3,11},{4,12},{5,13},{6,14},{7,15},{8,0},{9,1},... | collective-permute-start | bytes 313352 | tf_op jit(solution)/shard_map/ppermute | solution.py:305
  67.0 1.8 %collective-permute-start.2 = (bf16[136,384]{1,0:T(8,128)(2,1)}, bf16[136,384]{1,0:T(8,128)(2,1)}, u32[]{:S(2)}, u32[]{:S(2)}) collective-permute-start(bf16[136,384]{1,0:T(8,128)(2,1)} %copy-done.11), channel_id=1, source_target_pairs={{0,12},{1,13},{2,14},{3,15},{4,8},{5,9},{6,10},{7,11},{8,4},{9,5},... | collective-permute-start | bytes 313352 | tf_op jit(solution)/shard_map/ppermute | solution.py:305
  68.9 1.4 %concatenate.27.tables_ref = s32[1314]{0:T(1024)} concatenate(s32[32]{0:T(128)S(1)} %select_reduce_fusion, s32[1280]{0:T(1024)} %reshape.78, s32[1]{0:T(128)} %bitcast.index_ref, s32[1]{0:T(128)} %bitcast.2), dimensions={0} | concatenate | bytes 10512 | tf_op jit(solution)/shard_map/concatenate | solution.py:345
  73.6 5.6 %attend.5 = (bf16[128,256]{1,0:T(8,128)(2,1)S(1)}, bf16[128,256]{1,0:T(8,128)(2,1)S(1)}, bf16[128,256]{1,0:T(8,128)(2,1)S(1)}, bf16[128,256]{1,0:T(8,128)(2,1)S(1)}) custom-call(s32[1314]{0:T(1024)S(1)} %copy-done.4, bf16[136,640]{1,0:T(8,128)(2,1)S(1)} %get-tuple-element.31.refs_0_, bf16[136,256]{1,0:T(8,128)(2,1)S(1)} %copy-done.6, ...), custom_call_target="tpu_custom_call" | custom-call | flops 268435456 | bytes 2097152 | tf_op jit(solution)/shard_map/attend/pallas_call | solution.py:249
  79.2 2.1 %collective-permute-start.28 = (bf16[128,256]{1,0:T(8,128)(2,1)S(1)}, bf16[128,256]{1,0:T(8,128)(2,1)S(1)}, u32[]{:S(2)}, u32[]{:S(2)}) collective-permute-start(bf16[128,256]{1,0:T(8,128)(2,1)S(1)} %get-tuple-element.54), channel_id=1, source_target_pairs={{0,12},{1,13},{2,14},{3,15},{4,8},{5,9},{6,10},{7,11},{8,4},{9,5},... | collective-permute-start | bytes 196616 | tf_op jit(solution)/shard_map/ppermute | solution.py:305
  81.3 2.3 %collective-permute-start.30 = (bf16[128,256]{1,0:T(8,128)(2,1)S(1)}, bf16[128,256]{1,0:T(8,128)(2,1)S(1)}, u32[]{:S(2)}, u32[]{:S(2)}) collective-permute-start(bf16[128,256]{1,0:T(8,128)(2,1)S(1)} %get-tuple-element.56), channel_id=1, source_target_pairs={{0,4},{1,5},{2,6},{3,7},{4,0},{5,1},{6,2},{7,3},{8,12},{9,13},{10,... | collective-permute-start | bytes 196616 | tf_op jit(solution)/shard_map/ppermute | solution.py:305
  83.7 5.7 %attend.3 = (bf16[128,256]{1,0:T(8,128)(2,1)S(1)}, bf16[128,256]{1,0:T(8,128)(2,1)S(1)}, bf16[128,256]{1,0:T(8,128)(2,1)S(1)}, bf16[128,256]{1,0:T(8,128)(2,1)S(1)}) custom-call(s32[1314]{0:T(1024)S(1)} %copy-done.4, bf16[136,640]{1,0:T(8,128)(2,1)S(1)} %get-tuple-element.31.refs_0_, bf16[136,384]{1,0:T(8,128)(2,1)S(1)} %collective-permute-done.refs_1_, ...), custom_call_target="tpu_custom_call" | custom-call | flops 268435456 | bytes 2097152 | tf_op jit(solution)/shard_map/attend/pallas_call | solution.py:249
  89.3 4.0 %attend.4 = (bf16[128,128]{1,0:T(8,128)(2,1)S(1)}, bf16[128,128]{1,0:T(8,128)(2,1)S(1)}, bf16[128,128]{1,0:T(8,128)(2,1)S(1)}, bf16[128,128]{1,0:T(8,128)(2,1)S(1)}) custom-call(s32[1314]{0:T(1024)S(1)} %copy-done.4, bf16[136,640]{1,0:T(8,128)(2,1)S(1)} %get-tuple-element.31.refs_0_, bf16[136,384]{1,0:T(8,128)(2,1)S(1)} %collective-permute-done.refs_1_, ...), custom_call_target="tpu_custom_call" | custom-call | flops 134217728 | bytes 1048576 | tf_op jit(solution)/shard_map/attend/pallas_call | solution.py:249
  93.5 2.6 %collective-permute-start.15 = (bf16[128,384]{1,0:T(8,128)(2,1)S(1)}, bf16[128,384]{1,0:T(8,128)(2,1)S(1)}, u32[]{:S(2)}, u32[]{:S(2)}) collective-permute-start(bf16[128,384]{1,0:T(8,128)(2,1)S(1)} %pad_maximum_fusion.2), channel_id=1, source_target_pairs={{0,8},{1,9},{2,10},{3,11},{4,12},{5,13},{6,14},{7,15},{8,0},{9,1},... | collective-permute-start | bytes 294920 | tf_op jit(solution)/shard_map/ppermute | solution.py:305
  96.1 1.8 %collective-permute-start.14 = (bf16[128,384]{1,0:T(8,128)(2,1)S(1)}, bf16[128,384]{1,0:T(8,128)(2,1)S(1)}, u32[]{:S(2)}, u32[]{:S(2)}) collective-permute-start(bf16[128,384]{1,0:T(8,128)(2,1)S(1)} %pad_maximum_fusion.1), channel_id=1, source_target_pairs={{0,12},{1,13},{2,14},{3,15},{4,8},{5,9},{6,10},{7,11},{8,4},{9,5},... | collective-permute-start | bytes 294920 | tf_op jit(solution)/shard_map/ppermute | solution.py:305
  98.1 4.7 %collective-permute-done.15.refs_2_ = bf16[128,384]{1,0:T(8,128)(2,1)S(1)} collective-permute-done((bf16[128,384]{1,0:T(8,128)(2,1)S(1)}, bf16[128,384]{1,0:T(8,128)(2,1)S(1)}, u32[]{:S(2)}, u32[]{:S(2)}) %collective-permute-start.15) | collective-permute-done | bytes 98336 | tf_op jit(solution)/shard_map/ppermute | solution.py:305
  (89 shorter events, 16.6 us)
Async XLA Ops:
  0.0 63.6 %copy-start = (s32[32,20,8]{0,2,1:T(8,128)S(1)}, s32[32,20,8]{0,2,1:T(8,128)}, u32[]{:S(2)}) copy-start(s32[32,20,8]{0,2,1:T(8,128)} %param.10) | copy-start | bytes 61444
  2.5 8.5 %collective-permute-start.20 = (bf16[256,256]{1,0:T(8,128)(2,1)S(1)}, bf16[256,256]{1,0:T(8,128)(2,1)S(1)}, u32[]{:S(2)}, u32[]{:S(2)}) collective-permute-start(bf16[256,256]{1,0:T(8,128)(2,1)S(1)} %get-tuple-element.50), channel_id=1, source_target_pairs={{0,4},{1,5},{2,6},{3,7},{4,0},{5,1},{6,2},{7,3},{8,12},{9,13},{10,... | collective-permute-start | bytes 393224 | tf_op jit(solution)/shard_map/ppermute | solution.py:305
  5.7 8.8 %collective-permute-start.21 = (bf16[256,256]{1,0:T(8,128)(2,1)S(1)}, bf16[256,256]{1,0:T(8,128)(2,1)S(1)}, u32[]{:S(2)}, u32[]{:S(2)}) collective-permute-start(bf16[256,256]{1,0:T(8,128)(2,1)S(1)} %get-tuple-element.51), channel_id=1, source_target_pairs={{0,8},{1,9},{2,10},{3,11},{4,12},{5,13},{6,14},{7,15},{8,0},{9,1},... | collective-permute-start | bytes 393224 | tf_op jit(solution)/shard_map/ppermute | solution.py:305
  8.3 54.8 %collective-permute-start.3 = (bf16[256,640]{1,0:T(8,128)(2,1)S(1)}, bf16[256,640]{1,0:T(8,128)(2,1)S(1)}, u32[]{:S(2)}, u32[]{:S(2)}) collective-permute-start(bf16[256,640]{1,0:T(8,128)(2,1)S(1)} %get-tuple-element.35.refs_4_), channel_id=1, source_target_pairs={{0,2},{1,3},{2,0},{3,1},{4,6},{5,7},{6,4},{7,5},{8,10},{9,11},{10,... | collective-permute-start | bytes 983048 | tf_op jit(solution)/shard_map/ppermute | solution.py:308
  9.7 53.4 %collective-permute-start.4 = (bf16[256,640]{1,0:T(8,128)(2,1)S(1)}, bf16[256,640]{1,0:T(8,128)(2,1)S(1)}, u32[]{:S(2)}, u32[]{:S(2)}) collective-permute-start(bf16[256,640]{1,0:T(8,128)(2,1)S(1)} %get-tuple-element.35.refs_4_), channel_id=1, source_target_pairs={{0,1},{1,0},{2,3},{3,2},{4,5},{5,4},{6,7},{7,6},{8,9},{9,8},{10,11... | collective-permute-start | bytes 983048 | tf_op jit(solution)/shard_map/ppermute | solution.py:308
  9.8 8.9 %collective-permute-start.22 = (bf16[256,256]{1,0:T(8,128)(2,1)S(1)}, bf16[256,256]{1,0:T(8,128)(2,1)S(1)}, u32[]{:S(2)}, u32[]{:S(2)}) collective-permute-start(bf16[256,256]{1,0:T(8,128)(2,1)S(1)} %get-tuple-element.52), channel_id=1, source_target_pairs={{0,12},{1,13},{2,14},{3,15},{4,8},{5,9},{6,10},{7,11},{8,4},{9,5},... | collective-permute-start | bytes 393224 | tf_op jit(solution)/shard_map/ppermute | solution.py:305
  11.0 41.3 %collective-permute-start.17 = (bf16[136,256]{1,0:T(8,128)(2,1)S(1)}, bf16[136,256]{1,0:T(8,128)(2,1)S(1)}, u32[]{:S(2)}, u32[]{:S(2)}) collective-permute-start(bf16[136,256]{1,0:T(8,128)(2,1)S(1)} %get-tuple-element.47), channel_id=1, source_target_pairs={{0,4},{1,5},{2,6},{3,7},{4,0},{5,1},{6,2},{7,3},{8,12},{9,13},{10,... | collective-permute-start | bytes 208904 | tf_op jit(solution)/shard_map/ppermute | solution.py:305
  14.5 10.5 %collective-permute-start.6 = (bf16[256,384]{1,0:T(8,128)(2,1)S(1)}, bf16[256,384]{1,0:T(8,128)(2,1)S(1)}, u32[]{:S(2)}, u32[]{:S(2)}) collective-permute-start(bf16[256,384]{1,0:T(8,128)(2,1)S(1)} %get-tuple-element.36), channel_id=1, source_target_pairs={{0,4},{1,5},{2,6},{3,7},{4,0},{5,1},{6,2},{7,3},{8,12},{9,13},{10,... | collective-permute-start | bytes 589832 | tf_op jit(solution)/shard_map/ppermute | solution.py:305
  18.7 17.5 %collective-permute-start.7 = (bf16[256,384]{1,0:T(8,128)(2,1)S(1)}, bf16[256,384]{1,0:T(8,128)(2,1)S(1)}, u32[]{:S(2)}, u32[]{:S(2)}) collective-permute-start(bf16[256,384]{1,0:T(8,128)(2,1)S(1)} %get-tuple-element.37), channel_id=1, source_target_pairs={{0,8},{1,9},{2,10},{3,11},{4,12},{5,13},{6,14},{7,15},{8,0},{9,1},... | collective-permute-start | bytes 589832 | tf_op jit(solution)/shard_map/ppermute | solution.py:305
  25.0 12.5 %collective-permute-start.8 = (bf16[256,384]{1,0:T(8,128)(2,1)S(1)}, bf16[256,384]{1,0:T(8,128)(2,1)S(1)}, u32[]{:S(2)}, u32[]{:S(2)}) collective-permute-start(bf16[256,384]{1,0:T(8,128)(2,1)S(1)} %get-tuple-element.38), channel_id=1, source_target_pairs={{0,12},{1,13},{2,14},{3,15},{4,8},{5,9},{6,10},{7,11},{8,4},{9,5},... | collective-permute-start | bytes 589832 | tf_op jit(solution)/shard_map/ppermute | solution.py:305
  36.2 6.4 %collective-permute-start.23 = (bf16[256,256]{1,0:T(8,128)(2,1)S(1)}, bf16[256,256]{1,0:T(8,128)(2,1)S(1)}, u32[]{:S(2)}, u32[]{:S(2)}) collective-permute-start(bf16[256,256]{1,0:T(8,128)(2,1)S(1)} %collective-permute-done.20), channel_id=1, source_target_pairs={{0,2},{1,3},{2,0},{3,1},{4,6},{5,7},{6,4},{7,5},{8,10},{9,11},{10,... | collective-permute-start | bytes 393224 | tf_op jit(solution)/shard_map/ppermute | solution.py:308
  37.5 7.8 %collective-permute-start.24 = (bf16[256,256]{1,0:T(8,128)(2,1)S(1)}, bf16[256,256]{1,0:T(8,128)(2,1)S(1)}, u32[]{:S(2)}, u32[]{:S(2)}) collective-permute-start(bf16[256,256]{1,0:T(8,128)(2,1)S(1)} %collective-permute-done.21), channel_id=1, source_target_pairs={{0,2},{1,3},{2,0},{3,1},{4,6},{5,7},{6,4},{7,5},{8,10},{9,11},{10,... | collective-permute-start | bytes 393224 | tf_op jit(solution)/shard_map/ppermute | solution.py:308
  42.5 6.1 %collective-permute-start.9 = (bf16[256,384]{1,0:T(8,128)(2,1)S(1)}, bf16[256,384]{1,0:T(8,128)(2,1)S(1)}, u32[]{:S(2)}, u32[]{:S(2)}) collective-permute-start(bf16[256,384]{1,0:T(8,128)(2,1)S(1)} %collective-permute-done.6), channel_id=1, source_target_pairs={{0,2},{1,3},{2,0},{3,1},{4,6},{5,7},{6,4},{7,5},{8,10},{9,11},{10,... | collective-permute-start | bytes 589832 | tf_op jit(solution)/shard_map/ppermute | solution.py:308
  45.3 5.7 %collective-permute-start.10 = (bf16[256,384]{1,0:T(8,128)(2,1)S(1)}, bf16[256,384]{1,0:T(8,128)(2,1)S(1)}, u32[]{:S(2)}, u32[]{:S(2)}) collective-permute-start(bf16[256,384]{1,0:T(8,128)(2,1)S(1)} %collective-permute-done.7), channel_id=1, source_target_pairs={{0,2},{1,3},{2,0},{3,1},{4,6},{5,7},{6,4},{7,5},{8,10},{9,11},{10,... | collective-permute-start | bytes 589832 | tf_op jit(solution)/shard_map/ppermute | solution.py:308
  48.6 7.1 %collective-permute-start.11 = (bf16[256,384]{1,0:T(8,128)(2,1)S(1)}, bf16[256,384]{1,0:T(8,128)(2,1)S(1)}, u32[]{:S(2)}, u32[]{:S(2)}) collective-permute-start(bf16[256,384]{1,0:T(8,128)(2,1)S(1)} %collective-permute-done.8), channel_id=1, source_target_pairs={{0,2},{1,3},{2,0},{3,1},{4,6},{5,7},{6,4},{7,5},{8,10},{9,11},{10,... | collective-permute-start | bytes 589832 | tf_op jit(solution)/shard_map/ppermute | solution.py:308
  51.0 10.8 %collective-permute-start.25 = (bf16[256,256]{1,0:T(8,128)(2,1)S(1)}, bf16[256,256]{1,0:T(8,128)(2,1)S(1)}, u32[]{:S(2)}, u32[]{:S(2)}) collective-permute-start(bf16[256,256]{1,0:T(8,128)(2,1)S(1)} %collective-permute-done.22), channel_id=1, source_target_pairs={{0,2},{1,3},{2,0},{3,1},{4,6},{5,7},{6,4},{7,5},{8,10},{9,11},{10,... | collective-permute-start | bytes 393224 | tf_op jit(solution)/shard_map/ppermute | solution.py:308
  52.4 5.6 %collective-permute-start.18 = (bf16[136,256]{1,0:T(8,128)(2,1)S(1)}, bf16[136,256]{1,0:T(8,128)(2,1)S(1)}, u32[]{:S(2)}, u32[]{:S(2)}) collective-permute-start(bf16[136,256]{1,0:T(8,128)(2,1)S(1)} %get-tuple-element.48), channel_id=1, source_target_pairs={{0,8},{1,9},{2,10},{3,11},{4,12},{5,13},{6,14},{7,15},{8,0},{9,1},... | collective-permute-start | bytes 208904 | tf_op jit(solution)/shard_map/ppermute | solution.py:305
  55.7 6.1 %collective-permute-start.19 = (bf16[136,256]{1,0:T(8,128)(2,1)S(1)}, bf16[136,256]{1,0:T(8,128)(2,1)S(1)}, u32[]{:S(2)}, u32[]{:S(2)}) collective-permute-start(bf16[136,256]{1,0:T(8,128)(2,1)S(1)} %get-tuple-element.49), channel_id=1, source_target_pairs={{0,12},{1,13},{2,14},{3,15},{4,8},{5,9},{6,10},{7,11},{8,4},{9,5},... | collective-permute-start | bytes 208904 | tf_op jit(solution)/shard_map/ppermute | solution.py:305
  58.0 6.3 %collective-permute-start.26 = (bf16[768,256]{1,0:T(8,128)(2,1)}, bf16[768,256]{1,0:T(8,128)(2,1)}, u32[]{:S(2)}, u32[]{:S(2)}) collective-permute-start(bf16[768,256]{1,0:T(8,128)(2,1)} %constant_dynamic-update-slice_fusion.6.refs_8_), channel_id=1, source_target_pairs={{0,1},{1,0},{2,3},{3,2},{4,5},{5,4},{6,7},{7,6},{8,9},{9,8},{10,11... | collective-permute-start | bytes 1179656 | tf_op jit(solution)/shard_map/ppermute | solution.py:308
  61.8 21.8 %collective-permute-start.12 = (bf16[768,384]{1,0:T(8,128)(2,1)S(1)}, bf16[768,384]{1,0:T(8,128)(2,1)S(1)}, u32[]{:S(2)}, u32[]{:S(2)}) collective-permute-start(bf16[768,384]{1,0:T(8,128)(2,1)S(1)} %constant_dynamic-update-slice_fusion.refs_8_), channel_id=1, source_target_pairs={{0,1},{1,0},{2,3},{3,2},{4,5},{5,4},{6,7},{7,6},{8,9},{9,8},{10,11... | collective-permute-start | bytes 1769480 | tf_op jit(solution)/shard_map/ppermute | solution.py:308
  61.8 21.8 %collective-permute-start.13 = (bf16[768,384]{1,0:T(8,128)(2,1)S(1)}, bf16[768,384]{1,0:T(8,128)(2,1)}, u32[]{:S(2)}, u32[]{:S(2)}) collective-permute-start(bf16[768,384]{1,0:T(8,128)(2,1)S(1)} %constant_dynamic-update-slice_fusion.3.refs_9_), channel_id=1, source_target_pairs={{0,1},{1,0},{2,3},{3,2},{4,5},{5,4},{6,7},{7,6},{8,9},{9,8},{10,11... | collective-permute-start | bytes 1769480 | tf_op jit(solution)/shard_map/ppermute | solution.py:308
  63.0 2.4 %collective-permute-start.27 = (bf16[768,256]{1,0:T(8,128)(2,1)}, bf16[768,256]{1,0:T(8,128)(2,1)}, u32[]{:S(2)}, u32[]{:S(2)}) collective-permute-start(bf16[768,256]{1,0:T(8,128)(2,1)} %constant_dynamic-update-slice_fusion.9.refs_9_), channel_id=1, source_target_pairs={{0,1},{1,0},{2,3},{3,2},{4,5},{5,4},{6,7},{7,6},{8,9},{9,8},{10,11... | collective-permute-start | bytes 1179656 | tf_op jit(solution)/shard_map/ppermute | solution.py:308
  63.1 3.8 %collective-permute-start.5 = (bf16[256,640]{1,0:T(8,128)(2,1)S(1)}, bf16[256,640]{1,0:T(8,128)(2,1)S(1)}, u32[]{:S(2)}, u32[]{:S(2)}) collective-permute-start(bf16[256,640]{1,0:T(8,128)(2,1)S(1)} %collective-permute-done.3.refs_5_), channel_id=1, source_target_pairs={{0,1},{1,0},{2,3},{3,2},{4,5},{5,4},{6,7},{7,6},{8,9},{9,8},{10,11... | collective-permute-start | bytes 983048 | tf_op jit(solution)/shard_map/ppermute | solution.py:308
  64.3 14.9 %collective-permute-start = (bf16[136,384]{1,0:T(8,128)(2,1)}, bf16[136,384]{1,0:T(8,128)(2,1)S(1)}, u32[]{:S(2)}, u32[]{:S(2)}) collective-permute-start(bf16[136,384]{1,0:T(8,128)(2,1)} %get-tuple-element.32), channel_id=1, source_target_pairs={{0,4},{1,5},{2,6},{3,7},{4,0},{5,1},{6,2},{7,3},{8,12},{9,13},{10,... | collective-permute-start | bytes 313352 | tf_op jit(solution)/shard_map/ppermute | solution.py:305
  65.4 15.9 %collective-permute-start.1 = (bf16[136,384]{1,0:T(8,128)(2,1)}, bf16[136,384]{1,0:T(8,128)(2,1)S(1)}, u32[]{:S(2)}, u32[]{:S(2)}) collective-permute-start(bf16[136,384]{1,0:T(8,128)(2,1)} %copy-done.12), channel_id=1, source_target_pairs={{0,8},{1,9},{2,10},{3,11},{4,12},{5,13},{6,14},{7,15},{8,0},{9,1},... | collective-permute-start | bytes 313352 | tf_op jit(solution)/shard_map/ppermute | solution.py:305
  67.0 14.3 %collective-permute-start.2 = (bf16[136,384]{1,0:T(8,128)(2,1)}, bf16[136,384]{1,0:T(8,128)(2,1)}, u32[]{:S(2)}, u32[]{:S(2)}) collective-permute-start(bf16[136,384]{1,0:T(8,128)(2,1)} %copy-done.11), channel_id=1, source_target_pairs={{0,12},{1,13},{2,14},{3,15},{4,8},{5,9},{6,10},{7,11},{8,4},{9,5},... | collective-permute-start | bytes 313352 | tf_op jit(solution)/shard_map/ppermute | solution.py:305
  79.2 16.9 %collective-permute-start.28 = (bf16[128,256]{1,0:T(8,128)(2,1)S(1)}, bf16[128,256]{1,0:T(8,128)(2,1)S(1)}, u32[]{:S(2)}, u32[]{:S(2)}) collective-permute-start(bf16[128,256]{1,0:T(8,128)(2,1)S(1)} %get-tuple-element.54), channel_id=1, source_target_pairs={{0,12},{1,13},{2,14},{3,15},{4,8},{5,9},{6,10},{7,11},{8,4},{9,5},... | collective-permute-start | bytes 196616 | tf_op jit(solution)/shard_map/ppermute | solution.py:305
  81.3 16.7 %collective-permute-start.29 = (bf16[128,256]{1,0:T(8,128)(2,1)S(1)}, bf16[128,256]{1,0:T(8,128)(2,1)S(1)}, u32[]{:S(2)}, u32[]{:S(2)}) collective-permute-start(bf16[128,256]{1,0:T(8,128)(2,1)S(1)} %get-tuple-element.55), channel_id=1, source_target_pairs={{0,8},{1,9},{2,10},{3,11},{4,12},{5,13},{6,14},{7,15},{8,0},{9,1},... | collective-permute-start | bytes 196616 | tf_op jit(solution)/shard_map/ppermute | solution.py:305
  81.3 16.7 %collective-permute-start.30 = (bf16[128,256]{1,0:T(8,128)(2,1)S(1)}, bf16[128,256]{1,0:T(8,128)(2,1)S(1)}, u32[]{:S(2)}, u32[]{:S(2)}) collective-permute-start(bf16[128,256]{1,0:T(8,128)(2,1)S(1)} %get-tuple-element.56), channel_id=1, source_target_pairs={{0,4},{1,5},{2,6},{3,7},{4,0},{5,1},{6,2},{7,3},{8,12},{9,13},{10,... | collective-permute-start | bytes 196616 | tf_op jit(solution)/shard_map/ppermute | solution.py:305
  93.4 4.7 %collective-permute-start.16 = (bf16[128,384]{1,0:T(8,128)(2,1)S(1)}, bf16[128,384]{1,0:T(8,128)(2,1)S(1)}, u32[]{:S(2)}, u32[]{:S(2)}) collective-permute-start(bf16[128,384]{1,0:T(8,128)(2,1)S(1)} %pad_maximum_fusion.3), channel_id=1, source_target_pairs={{0,4},{1,5},{2,6},{3,7},{4,0},{5,1},{6,2},{7,3},{8,12},{9,13},{10,... | collective-permute-start | bytes 294920 | tf_op jit(solution)/shard_map/ppermute | solution.py:305
  93.5 9.3 %collective-permute-start.15 = (bf16[128,384]{1,0:T(8,128)(2,1)S(1)}, bf16[128,384]{1,0:T(8,128)(2,1)S(1)}, u32[]{:S(2)}, u32[]{:S(2)}) collective-permute-start(bf16[128,384]{1,0:T(8,128)(2,1)S(1)} %pad_maximum_fusion.2), channel_id=1, source_target_pairs={{0,8},{1,9},{2,10},{3,11},{4,12},{5,13},{6,14},{7,15},{8,0},{9,1},... | collective-permute-start | bytes 294920 | tf_op jit(solution)/shard_map/ppermute | solution.py:305
  96.1 6.7 %collective-permute-start.14 = (bf16[128,384]{1,0:T(8,128)(2,1)S(1)}, bf16[128,384]{1,0:T(8,128)(2,1)S(1)}, u32[]{:S(2)}, u32[]{:S(2)}) collective-permute-start(bf16[128,384]{1,0:T(8,128)(2,1)S(1)} %pad_maximum_fusion.1), channel_id=1, source_target_pairs={{0,12},{1,13},{2,14},{3,15},{4,8},{5,9},{6,10},{7,11},{8,4},{9,5},... | collective-permute-start | bytes 294920 | tf_op jit(solution)/shard_map/ppermute | solution.py:305
  (14 other events, 39.0 us)

commit v5 on v4

--- a/solution.py
+++ b/solution.py
@@ -13,6 +13,7 @@
 GATE_ROWS = 8
 CHUNKS = ((2, 1), (2,))
 POOL_ROWS = 1024
+COARSE_ROWS = 512
 HELD_BYTES = 8 << 20
 SMALL_VMEM = 12 << 20
 LOG2E = 1.4426950408889634
@@ -165,8 +166,8 @@
         pooled_values[:, head_size:] = ones[:cubes] if cubes <= picks * CUBE else jnp.ones(
             (cubes, head_size), jnp.bfloat16
         )
-        for group in range(groups):
-            rows = slice(group * tokens, (group + 1) * tokens)
+        for row in range(0, groups * tokens, COARSE_ROWS):
+            rows = slice(row, min(row + COARSE_ROWS, groups * tokens))
             scores = lax.dot_general(
                 query_all[rows, columns],
                 pooled_keys[...],

time: 104 us -> 103 us (level)
  Pallas kernels: 17.4 us -> 16 us
    pallas_call x3, Pallas kernels: 15.3 us -> 13.8 us  [attend(): pl.pallas_call(functools.partial(attend_kernel, shape), out_shape=[out] *...]
  transfers between devices with their start and end apart: 31 -> 31, of which waited for: 11 -> 11; matrix products, arithmetic and copies ran while one was open for 6% -> 6% of each run, Pallas kernels for 16% -> 14%
where the time goes in v5:
time: 103 us; the launch traced here: 102 us
  starting transfers between devices  43.5 us (42%)
  waiting for transfers between devices  30.6 us (30%)
  Pallas kernels  16 us (16%)
  local copies, waits for them, and re-layouts  11.8 us (11%)
    ppermute x18, starting transfers between devices, over_groups(): return lax.ppermute(value, 'cubes', pairs)  34 us
    ppermute x18, waiting for transfers between devices, over_groups(): return lax.ppermute(value, 'cubes', pairs)  21.7 us
    pallas_call x3, Pallas kernels, attend(): pl.pallas_call(functools.partial(attend_kernel, shape), out_shape=[out] *...  13.8 us
    ppermute x13, starting transfers between devices, over_ring(): return lax.ppermute(value, 'cubes', [(i, i ^ step) for i in range(devices)])  9.45 us
    ppermute x13, waiting for transfers between devices, over_ring(): return lax.ppermute(value, 'cubes', [(i, i ^ step) for i in range(devices)])  8.88 us
    unnamed x38, local copies, waits for them, and re-layouts  8.33 us
  transfers between devices with their start and end apart: 31, of which 11 were waited for; matrix products, arithmetic and copies ran while one was open for 6% of the time, Pallas kernels for 14%

profile of v5, /device:TPU:0, one launch (start us, length us, event | category | flops | bytes accessed | tf_op | source)
XLA Modules:
  0.0 102.3 jit_solution(12406387138126138894)
XLA Ops:
  0.0 1.1 %copy-done.1 = bf16[128,2560]{1,0:T(8,128)(2,1)S(1)} copy-done((bf16[128,2560]{1,0:T(8,128)(2,1)S(1)}, bf16[128,2560]{1,0:T(8,128)(2,1)}, u32[]{:S(2)}) %copy-start.1) | copy-done | bytes 655384
  1.1 1.1 %copy-done.2 = bf16[128,2560]{1,0:T(8,128)(2,1)S(1)} copy-done((bf16[128,2560]{1,0:T(8,128)(2,1)S(1)}, bf16[128,2560]{1,0:T(8,128)(2,1)}, u32[]{:S(2)}) %copy-start.2) | copy-done | bytes 655384
  2.5 3.1 %collective-permute-start.20 = (bf16[256,256]{1,0:T(8,128)(2,1)S(1)}, bf16[256,256]{1,0:T(8,128)(2,1)S(1)}, u32[]{:S(2)}, u32[]{:S(2)}) collective-permute-start(bf16[256,256]{1,0:T(8,128)(2,1)S(1)} %get-tuple-element.50), channel_id=1, source_target_pairs={{0,4},{1,5},{2,6},{3,7},{4,0},{5,1},{6,2},{7,3},{8,12},{9,13},{10,... | collective-permute-start | bytes 393224 | tf_op jit(solution)/shard_map/ppermute | solution.py:306
  5.7 2.6 %collective-permute-start.21 = (bf16[256,256]{1,0:T(8,128)(2,1)S(1)}, bf16[256,256]{1,0:T(8,128)(2,1)S(1)}, u32[]{:S(2)}, u32[]{:S(2)}) collective-permute-start(bf16[256,256]{1,0:T(8,128)(2,1)S(1)} %get-tuple-element.51), channel_id=1, source_target_pairs={{0,8},{1,9},{2,10},{3,11},{4,12},{5,13},{6,14},{7,15},{8,0},{9,1},... | collective-permute-start | bytes 393224 | tf_op jit(solution)/shard_map/ppermute | solution.py:306
  8.3 1.5 %collective-permute-start.3 = (bf16[256,640]{1,0:T(8,128)(2,1)S(1)}, bf16[256,640]{1,0:T(8,128)(2,1)S(1)}, u32[]{:S(2)}, u32[]{:S(2)}) collective-permute-start(bf16[256,640]{1,0:T(8,128)(2,1)S(1)} %get-tuple-element.35.refs_4_), channel_id=1, source_target_pairs={{0,2},{1,3},{2,0},{3,1},{4,6},{5,7},{6,4},{7,5},{8,10},{9,11},{10,... | collective-permute-start | bytes 983048 | tf_op jit(solution)/shard_map/ppermute | solution.py:309
  12.4 2.1 %collective-permute-done.21 = bf16[256,256]{1,0:T(8,128)(2,1)S(1)} collective-permute-done((bf16[256,256]{1,0:T(8,128)(2,1)S(1)}, bf16[256,256]{1,0:T(8,128)(2,1)S(1)}, u32[]{:S(2)}, u32[]{:S(2)}) %collective-permute-start.21) | collective-permute-done | bytes 131104 | tf_op jit(solution)/shard_map/ppermute | solution.py:306
  14.5 3.5 %collective-permute-start.6 = (bf16[256,384]{1,0:T(8,128)(2,1)S(1)}, bf16[256,384]{1,0:T(8,128)(2,1)S(1)}, u32[]{:S(2)}, u32[]{:S(2)}) collective-permute-start(bf16[256,384]{1,0:T(8,128)(2,1)S(1)} %get-tuple-element.36), channel_id=1, source_target_pairs={{0,4},{1,5},{2,6},{3,7},{4,0},{5,1},{6,2},{7,3},{8,12},{9,13},{10,... | collective-permute-start | bytes 589832 | tf_op jit(solution)/shard_map/ppermute | solution.py:306
  18.7 3.4 %collective-permute-start.7 = (bf16[256,384]{1,0:T(8,128)(2,1)S(1)}, bf16[256,384]{1,0:T(8,128)(2,1)S(1)}, u32[]{:S(2)}, u32[]{:S(2)}) collective-permute-start(bf16[256,384]{1,0:T(8,128)(2,1)S(1)} %get-tuple-element.37), channel_id=1, source_target_pairs={{0,8},{1,9},{2,10},{3,11},{4,12},{5,13},{6,14},{7,15},{8,0},{9,1},... | collective-permute-start | bytes 589832 | tf_op jit(solution)/shard_map/ppermute | solution.py:306
  22.7 2.3 %collective-permute-done.6 = bf16[256,384]{1,0:T(8,128)(2,1)S(1)} collective-permute-done((bf16[256,384]{1,0:T(8,128)(2,1)S(1)}, bf16[256,384]{1,0:T(8,128)(2,1)S(1)}, u32[]{:S(2)}, u32[]{:S(2)}) %collective-permute-start.6) | collective-permute-done | bytes 196640 | tf_op jit(solution)/shard_map/ppermute | solution.py:306
  25.0 2.6 %collective-permute-start.8 = (bf16[256,384]{1,0:T(8,128)(2,1)S(1)}, bf16[256,384]{1,0:T(8,128)(2,1)S(1)}, u32[]{:S(2)}, u32[]{:S(2)}) collective-permute-start(bf16[256,384]{1,0:T(8,128)(2,1)S(1)} %get-tuple-element.38), channel_id=1, source_target_pairs={{0,12},{1,13},{2,14},{3,15},{4,8},{5,9},{6,10},{7,11},{8,4},{9,5},... | collective-permute-start | bytes 589832 | tf_op jit(solution)/shard_map/ppermute | solution.py:306
  27.7 8.5 %collective-permute-done.7 = bf16[256,384]{1,0:T(8,128)(2,1)S(1)} collective-permute-done((bf16[256,384]{1,0:T(8,128)(2,1)S(1)}, bf16[256,384]{1,0:T(8,128)(2,1)S(1)}, u32[]{:S(2)}, u32[]{:S(2)}) %collective-permute-start.7) | collective-permute-done | bytes 196640 | tf_op jit(solution)/shard_map/ppermute | solution.py:306
  36.2 1.3 %collective-permute-start.23 = (bf16[256,256]{1,0:T(8,128)(2,1)S(1)}, bf16[256,256]{1,0:T(8,128)(2,1)S(1)}, u32[]{:S(2)}, u32[]{:S(2)}) collective-permute-start(bf16[256,256]{1,0:T(8,128)(2,1)S(1)} %collective-permute-done.20), channel_id=1, source_target_pairs={{0,2},{1,3},{2,0},{3,1},{4,6},{5,7},{6,4},{7,5},{8,10},{9,11},{10,... | collective-permute-start | bytes 393224 | tf_op jit(solution)/shard_map/ppermute | solution.py:309
  38.3 4.2 %collective-permute-done.23 = bf16[256,256]{1,0:T(8,128)(2,1)S(1)} collective-permute-done((bf16[256,256]{1,0:T(8,128)(2,1)S(1)}, bf16[256,256]{1,0:T(8,128)(2,1)S(1)}, u32[]{:S(2)}, u32[]{:S(2)}) %collective-permute-start.23) | collective-permute-done | bytes 131104 | tf_op jit(solution)/shard_map/ppermute | solution.py:309
  42.5 1.3 %collective-permute-start.9 = (bf16[256,384]{1,0:T(8,128)(2,1)S(1)}, bf16[256,384]{1,0:T(8,128)(2,1)S(1)}, u32[]{:S(2)}, u32[]{:S(2)}) collective-permute-start(bf16[256,384]{1,0:T(8,128)(2,1)S(1)} %collective-permute-done.6), channel_id=1, source_target_pairs={{0,2},{1,3},{2,0},{3,1},{4,6},{5,7},{6,4},{7,5},{8,10},{9,11},{10,... | collective-permute-start | bytes 589832 | tf_op jit(solution)/shard_map/ppermute | solution.py:309
  45.3 1.3 %collective-permute-start.10 = (bf16[256,384]{1,0:T(8,128)(2,1)S(1)}, bf16[256,384]{1,0:T(8,128)(2,1)S(1)}, u32[]{:S(2)}, u32[]{:S(2)}) collective-permute-start(bf16[256,384]{1,0:T(8,128)(2,1)S(1)} %collective-permute-done.7), channel_id=1, source_target_pairs={{0,2},{1,3},{2,0},{3,1},{4,6},{5,7},{6,4},{7,5},{8,10},{9,11},{10,... | collective-permute-start | bytes 589832 | tf_op jit(solution)/shard_map/ppermute | solution.py:309
  47.3 1.3 %collective-permute-done.9 = bf16[256,384]{1,0:T(8,128)(2,1)S(1)} collective-permute-done((bf16[256,384]{1,0:T(8,128)(2,1)S(1)}, bf16[256,384]{1,0:T(8,128)(2,1)S(1)}, u32[]{:S(2)}, u32[]{:S(2)}) %collective-permute-start.9) | collective-permute-done | bytes 196640 | tf_op jit(solution)/shard_map/ppermute | solution.py:309
  49.5 1.5 %collective-permute-done.10 = bf16[256,384]{1,0:T(8,128)(2,1)S(1)} collective-permute-done((bf16[256,384]{1,0:T(8,128)(2,1)S(1)}, bf16[256,384]{1,0:T(8,128)(2,1)S(1)}, u32[]{:S(2)}, u32[]{:S(2)}) %collective-permute-start.10) | collective-permute-done | bytes 196640 | tf_op jit(solution)/shard_map/ppermute | solution.py:309
  51.0 1.3 %collective-permute-start.25 = (bf16[256,256]{1,0:T(8,128)(2,1)S(1)}, bf16[256,256]{1,0:T(8,128)(2,1)S(1)}, u32[]{:S(2)}, u32[]{:S(2)}) collective-permute-start(bf16[256,256]{1,0:T(8,128)(2,1)S(1)} %collective-permute-done.22), channel_id=1, source_target_pairs={{0,2},{1,3},{2,0},{3,1},{4,6},{5,7},{6,4},{7,5},{8,10},{9,11},{10,... | collective-permute-start | bytes 393224 | tf_op jit(solution)/shard_map/ppermute | solution.py:309
  52.4 3.4 %collective-permute-start.18 = (bf16[136,256]{1,0:T(8,128)(2,1)S(1)}, bf16[136,256]{1,0:T(8,128)(2,1)S(1)}, u32[]{:S(2)}, u32[]{:S(2)}) collective-permute-start(bf16[136,256]{1,0:T(8,128)(2,1)S(1)} %get-tuple-element.48), channel_id=1, source_target_pairs={{0,8},{1,9},{2,10},{3,11},{4,12},{5,13},{6,14},{7,15},{8,0},{9,1},... | collective-permute-start | bytes 208904 | tf_op jit(solution)/shard_map/ppermute | solution.py:306
  55.7 2.0 %collective-permute-start.19 = (bf16[136,256]{1,0:T(8,128)(2,1)S(1)}, bf16[136,256]{1,0:T(8,128)(2,1)S(1)}, u32[]{:S(2)}, u32[]{:S(2)}) collective-permute-start(bf16[136,256]{1,0:T(8,128)(2,1)S(1)} %get-tuple-element.49), channel_id=1, source_target_pairs={{0,12},{1,13},{2,14},{3,15},{4,8},{5,9},{6,10},{7,11},{8,4},{9,5},... | collective-permute-start | bytes 208904 | tf_op jit(solution)/shard_map/ppermute | solution.py:306
  58.0 3.8 %collective-permute-done.19.refs_3_ = bf16[136,256]{1,0:T(8,128)(2,1)S(1)} collective-permute-done((bf16[136,256]{1,0:T(8,128)(2,1)S(1)}, bf16[136,256]{1,0:T(8,128)(2,1)S(1)}, u32[]{:S(2)}, u32[]{:S(2)}) %collective-permute-start.19) | collective-permute-done | bytes 69664 | tf_op jit(solution)/shard_map/ppermute | solution.py:306
  65.4 1.6 %collective-permute-start.1 = (bf16[136,384]{1,0:T(8,128)(2,1)}, bf16[136,384]{1,0:T(8,128)(2,1)S(1)}, u32[]{:S(2)}, u32[]{:S(2)}) collective-permute-start(bf16[136,384]{1,0:T(8,128)(2,1)} %copy-done.12), channel_id=1, source_target_pairs={{0,8},{1,9},{2,10},{3,11},{4,12},{5,13},{6,14},{7,15},{8,0},{9,1},... | collective-permute-start | bytes 313352 | tf_op jit(solution)/shard_map/ppermute | solution.py:306
  67.0 1.8 %collective-permute-start.2 = (bf16[136,384]{1,0:T(8,128)(2,1)}, bf16[136,384]{1,0:T(8,128)(2,1)}, u32[]{:S(2)}, u32[]{:S(2)}) collective-permute-start(bf16[136,384]{1,0:T(8,128)(2,1)} %copy-done.11), channel_id=1, source_target_pairs={{0,12},{1,13},{2,14},{3,15},{4,8},{5,9},{6,10},{7,11},{8,4},{9,5},... | collective-permute-start | bytes 313352 | tf_op jit(solution)/shard_map/ppermute | solution.py:306
  68.9 1.4 %concatenate.27.tables_ref = s32[1314]{0:T(1024)} concatenate(s32[32]{0:T(128)S(1)} %select_reduce_fusion, s32[1280]{0:T(1024)} %reshape.78, s32[1]{0:T(128)} %bitcast.index_ref, s32[1]{0:T(128)} %bitcast.2), dimensions={0} | concatenate | bytes 10512 | tf_op jit(solution)/shard_map/concatenate | solution.py:346
  73.6 5.1 %attend.5 = (bf16[128,256]{1,0:T(8,128)(2,1)S(1)}, bf16[128,256]{1,0:T(8,128)(2,1)S(1)}, bf16[128,256]{1,0:T(8,128)(2,1)S(1)}, bf16[128,256]{1,0:T(8,128)(2,1)S(1)}) custom-call(s32[1314]{0:T(1024)S(1)} %copy-done.4, bf16[136,640]{1,0:T(8,128)(2,1)S(1)} %get-tuple-element.31.refs_0_, bf16[136,256]{1,0:T(8,128)(2,1)S(1)} %copy-done.6, ...), custom_call_target="tpu_custom_call" | custom-call | flops 268435456 | bytes 2097152 | tf_op jit(solution)/shard_map/attend/pallas_call | solution.py:250
  78.7 2.1 %collective-permute-start.28 = (bf16[128,256]{1,0:T(8,128)(2,1)S(1)}, bf16[128,256]{1,0:T(8,128)(2,1)S(1)}, u32[]{:S(2)}, u32[]{:S(2)}) collective-permute-start(bf16[128,256]{1,0:T(8,128)(2,1)S(1)} %get-tuple-element.54), channel_id=1, source_target_pairs={{0,12},{1,13},{2,14},{3,15},{4,8},{5,9},{6,10},{7,11},{8,4},{9,5},... | collective-permute-start | bytes 196616 | tf_op jit(solution)/shard_map/ppermute | solution.py:306
  80.8 2.3 %collective-permute-start.30 = (bf16[128,256]{1,0:T(8,128)(2,1)S(1)}, bf16[128,256]{1,0:T(8,128)(2,1)S(1)}, u32[]{:S(2)}, u32[]{:S(2)}) collective-permute-start(bf16[128,256]{1,0:T(8,128)(2,1)S(1)} %get-tuple-element.56), channel_id=1, source_target_pairs={{0,4},{1,5},{2,6},{3,7},{4,0},{5,1},{6,2},{7,3},{8,12},{9,13},{10,... | collective-permute-start | bytes 196616 | tf_op jit(solution)/shard_map/ppermute | solution.py:306
  83.1 5.2 %attend.3 = (bf16[128,256]{1,0:T(8,128)(2,1)S(1)}, bf16[128,256]{1,0:T(8,128)(2,1)S(1)}, bf16[128,256]{1,0:T(8,128)(2,1)S(1)}, bf16[128,256]{1,0:T(8,128)(2,1)S(1)}) custom-call(s32[1314]{0:T(1024)S(1)} %copy-done.4, bf16[136,640]{1,0:T(8,128)(2,1)S(1)} %get-tuple-element.31.refs_0_, bf16[136,384]{1,0:T(8,128)(2,1)S(1)} %collective-permute-done.refs_1_, ...), custom_call_target="tpu_custom_call" | custom-call | flops 268435456 | bytes 2097152 | tf_op jit(solution)/shard_map/attend/pallas_call | solution.py:250
  88.3 3.6 %attend.4 = (bf16[128,128]{1,0:T(8,128)(2,1)S(1)}, bf16[128,128]{1,0:T(8,128)(2,1)S(1)}, bf16[128,128]{1,0:T(8,128)(2,1)S(1)}, bf16[128,128]{1,0:T(8,128)(2,1)S(1)}) custom-call(s32[1314]{0:T(1024)S(1)} %copy-done.4, bf16[136,640]{1,0:T(8,128)(2,1)S(1)} %get-tuple-element.31.refs_0_, bf16[136,384]{1,0:T(8,128)(2,1)S(1)} %collective-permute-done.refs_1_, ...), custom_call_target="tpu_custom_call" | custom-call | flops 134217728 | bytes 1048576 | tf_op jit(solution)/shard_map/attend/pallas_call | solution.py:250
  92.0 2.7 %collective-permute-start.15 = (bf16[128,384]{1,0:T(8,128)(2,1)S(1)}, bf16[128,384]{1,0:T(8,128)(2,1)S(1)}, u32[]{:S(2)}, u32[]{:S(2)}) collective-permute-start(bf16[128,384]{1,0:T(8,128)(2,1)S(1)} %pad_maximum_fusion.2), channel_id=1, source_target_pairs={{0,8},{1,9},{2,10},{3,11},{4,12},{5,13},{6,14},{7,15},{8,0},{9,1},... | collective-permute-start | bytes 294920 | tf_op jit(solution)/shard_map/ppermute | solution.py:306
  94.7 1.8 %collective-permute-start.14 = (bf16[128,384]{1,0:T(8,128)(2,1)S(1)}, bf16[128,384]{1,0:T(8,128)(2,1)S(1)}, u32[]{:S(2)}, u32[]{:S(2)}) collective-permute-start(bf16[128,384]{1,0:T(8,128)(2,1)S(1)} %pad_maximum_fusion.1), channel_id=1, source_target_pairs={{0,12},{1,13},{2,14},{3,15},{4,8},{5,9},{6,10},{7,11},{8,4},{9,5},... | collective-permute-start | bytes 294920 | tf_op jit(solution)/shard_map/ppermute | solution.py:306
  96.6 4.7 %collective-permute-done.15.refs_2_ = bf16[128,384]{1,0:T(8,128)(2,1)S(1)} collective-permute-done((bf16[128,384]{1,0:T(8,128)(2,1)S(1)}, bf16[128,384]{1,0:T(8,128)(2,1)S(1)}, u32[]{:S(2)}, u32[]{:S(2)}) %collective-permute-start.15) | collective-permute-done | bytes 98336 | tf_op jit(solution)/shard_map/ppermute | solution.py:306
  (89 shorter events, 16.6 us)
Async XLA Ops:
  0.0 63.6 %copy-start = (s32[32,20,8]{0,2,1:T(8,128)S(1)}, s32[32,20,8]{0,2,1:T(8,128)}, u32[]{:S(2)}) copy-start(s32[32,20,8]{0,2,1:T(8,128)} %param.10) | copy-start | bytes 61444
  2.5 8.5 %collective-permute-start.20 = (bf16[256,256]{1,0:T(8,128)(2,1)S(1)}, bf16[256,256]{1,0:T(8,128)(2,1)S(1)}, u32[]{:S(2)}, u32[]{:S(2)}) collective-permute-start(bf16[256,256]{1,0:T(8,128)(2,1)S(1)} %get-tuple-element.50), channel_id=1, source_target_pairs={{0,4},{1,5},{2,6},{3,7},{4,0},{5,1},{6,2},{7,3},{8,12},{9,13},{10,... | collective-permute-start | bytes 393224 | tf_op jit(solution)/shard_map/ppermute | solution.py:306
  5.7 8.8 %collective-permute-start.21 = (bf16[256,256]{1,0:T(8,128)(2,1)S(1)}, bf16[256,256]{1,0:T(8,128)(2,1)S(1)}, u32[]{:S(2)}, u32[]{:S(2)}) collective-permute-start(bf16[256,256]{1,0:T(8,128)(2,1)S(1)} %get-tuple-element.51), channel_id=1, source_target_pairs={{0,8},{1,9},{2,10},{3,11},{4,12},{5,13},{6,14},{7,15},{8,0},{9,1},... | collective-permute-start | bytes 393224 | tf_op jit(solution)/shard_map/ppermute | solution.py:306
  8.3 54.8 %collective-permute-start.3 = (bf16[256,640]{1,0:T(8,128)(2,1)S(1)}, bf16[256,640]{1,0:T(8,128)(2,1)S(1)}, u32[]{:S(2)}, u32[]{:S(2)}) collective-permute-start(bf16[256,640]{1,0:T(8,128)(2,1)S(1)} %get-tuple-element.35.refs_4_), channel_id=1, source_target_pairs={{0,2},{1,3},{2,0},{3,1},{4,6},{5,7},{6,4},{7,5},{8,10},{9,11},{10,... | collective-permute-start | bytes 983048 | tf_op jit(solution)/shard_map/ppermute | solution.py:309
  9.7 53.4 %collective-permute-start.4 = (bf16[256,640]{1,0:T(8,128)(2,1)S(1)}, bf16[256,640]{1,0:T(8,128)(2,1)S(1)}, u32[]{:S(2)}, u32[]{:S(2)}) collective-permute-start(bf16[256,640]{1,0:T(8,128)(2,1)S(1)} %get-tuple-element.35.refs_4_), channel_id=1, source_target_pairs={{0,1},{1,0},{2,3},{3,2},{4,5},{5,4},{6,7},{7,6},{8,9},{9,8},{10,11... | collective-permute-start | bytes 983048 | tf_op jit(solution)/shard_map/ppermute | solution.py:309
  9.8 8.9 %collective-permute-start.22 = (bf16[256,256]{1,0:T(8,128)(2,1)S(1)}, bf16[256,256]{1,0:T(8,128)(2,1)S(1)}, u32[]{:S(2)}, u32[]{:S(2)}) collective-permute-start(bf16[256,256]{1,0:T(8,128)(2,1)S(1)} %get-tuple-element.52), channel_id=1, source_target_pairs={{0,12},{1,13},{2,14},{3,15},{4,8},{5,9},{6,10},{7,11},{8,4},{9,5},... | collective-permute-start | bytes 393224 | tf_op jit(solution)/shard_map/ppermute | solution.py:306
  11.0 41.3 %collective-permute-start.17 = (bf16[136,256]{1,0:T(8,128)(2,1)S(1)}, bf16[136,256]{1,0:T(8,128)(2,1)S(1)}, u32[]{:S(2)}, u32[]{:S(2)}) collective-permute-start(bf16[136,256]{1,0:T(8,128)(2,1)S(1)} %get-tuple-element.47), channel_id=1, source_target_pairs={{0,4},{1,5},{2,6},{3,7},{4,0},{5,1},{6,2},{7,3},{8,12},{9,13},{10,... | collective-permute-start | bytes 208904 | tf_op jit(solution)/shard_map/ppermute | solution.py:306
  14.5 10.5 %collective-permute-start.6 = (bf16[256,384]{1,0:T(8,128)(2,1)S(1)}, bf16[256,384]{1,0:T(8,128)(2,1)S(1)}, u32[]{:S(2)}, u32[]{:S(2)}) collective-permute-start(bf16[256,384]{1,0:T(8,128)(2,1)S(1)} %get-tuple-element.36), channel_id=1, source_target_pairs={{0,4},{1,5},{2,6},{3,7},{4,0},{5,1},{6,2},{7,3},{8,12},{9,13},{10,... | collective-permute-start | bytes 589832 | tf_op jit(solution)/shard_map/ppermute | solution.py:306
  18.7 17.5 %collective-permute-start.7 = (bf16[256,384]{1,0:T(8,128)(2,1)S(1)}, bf16[256,384]{1,0:T(8,128)(2,1)S(1)}, u32[]{:S(2)}, u32[]{:S(2)}) collective-permute-start(bf16[256,384]{1,0:T(8,128)(2,1)S(1)} %get-tuple-element.37), channel_id=1, source_target_pairs={{0,8},{1,9},{2,10},{3,11},{4,12},{5,13},{6,14},{7,15},{8,0},{9,1},... | collective-permute-start | bytes 589832 | tf_op jit(solution)/shard_map/ppermute | solution.py:306
  25.0 12.5 %collective-permute-start.8 = (bf16[256,384]{1,0:T(8,128)(2,1)S(1)}, bf16[256,384]{1,0:T(8,128)(2,1)S(1)}, u32[]{:S(2)}, u32[]{:S(2)}) collective-permute-start(bf16[256,384]{1,0:T(8,128)(2,1)S(1)} %get-tuple-element.38), channel_id=1, source_target_pairs={{0,12},{1,13},{2,14},{3,15},{4,8},{5,9},{6,10},{7,11},{8,4},{9,5},... | collective-permute-start | bytes 589832 | tf_op jit(solution)/shard_map/ppermute | solution.py:306
  36.2 6.4 %collective-permute-start.23 = (bf16[256,256]{1,0:T(8,128)(2,1)S(1)}, bf16[256,256]{1,0:T(8,128)(2,1)S(1)}, u32[]{:S(2)}, u32[]{:S(2)}) collective-permute-start(bf16[256,256]{1,0:T(8,128)(2,1)S(1)} %collective-permute-done.20), channel_id=1, source_target_pairs={{0,2},{1,3},{2,0},{3,1},{4,6},{5,7},{6,4},{7,5},{8,10},{9,11},{10,... | collective-permute-start | bytes 393224 | tf_op jit(solution)/shard_map/ppermute | solution.py:309
  37.5 7.8 %collective-permute-start.24 = (bf16[256,256]{1,0:T(8,128)(2,1)S(1)}, bf16[256,256]{1,0:T(8,128)(2,1)S(1)}, u32[]{:S(2)}, u32[]{:S(2)}) collective-permute-start(bf16[256,256]{1,0:T(8,128)(2,1)S(1)} %collective-permute-done.21), channel_id=1, source_target_pairs={{0,2},{1,3},{2,0},{3,1},{4,6},{5,7},{6,4},{7,5},{8,10},{9,11},{10,... | collective-permute-start | bytes 393224 | tf_op jit(solution)/shard_map/ppermute | solution.py:309
  42.5 6.1 %collective-permute-start.9 = (bf16[256,384]{1,0:T(8,128)(2,1)S(1)}, bf16[256,384]{1,0:T(8,128)(2,1)S(1)}, u32[]{:S(2)}, u32[]{:S(2)}) collective-permute-start(bf16[256,384]{1,0:T(8,128)(2,1)S(1)} %collective-permute-done.6), channel_id=1, source_target_pairs={{0,2},{1,3},{2,0},{3,1},{4,6},{5,7},{6,4},{7,5},{8,10},{9,11},{10,... | collective-permute-start | bytes 589832 | tf_op jit(solution)/shard_map/ppermute | solution.py:309
  45.3 5.7 %collective-permute-start.10 = (bf16[256,384]{1,0:T(8,128)(2,1)S(1)}, bf16[256,384]{1,0:T(8,128)(2,1)S(1)}, u32[]{:S(2)}, u32[]{:S(2)}) collective-permute-start(bf16[256,384]{1,0:T(8,128)(2,1)S(1)} %collective-permute-done.7), channel_id=1, source_target_pairs={{0,2},{1,3},{2,0},{3,1},{4,6},{5,7},{6,4},{7,5},{8,10},{9,11},{10,... | collective-permute-start | bytes 589832 | tf_op jit(solution)/shard_map/ppermute | solution.py:309
  48.6 7.1 %collective-permute-start.11 = (bf16[256,384]{1,0:T(8,128)(2,1)S(1)}, bf16[256,384]{1,0:T(8,128)(2,1)S(1)}, u32[]{:S(2)}, u32[]{:S(2)}) collective-permute-start(bf16[256,384]{1,0:T(8,128)(2,1)S(1)} %collective-permute-done.8), channel_id=1, source_target_pairs={{0,2},{1,3},{2,0},{3,1},{4,6},{5,7},{6,4},{7,5},{8,10},{9,11},{10,... | collective-permute-start | bytes 589832 | tf_op jit(solution)/shard_map/ppermute | solution.py:309
  51.0 10.8 %collective-permute-start.25 = (bf16[256,256]{1,0:T(8,128)(2,1)S(1)}, bf16[256,256]{1,0:T(8,128)(2,1)S(1)}, u32[]{:S(2)}, u32[]{:S(2)}) collective-permute-start(bf16[256,256]{1,0:T(8,128)(2,1)S(1)} %collective-permute-done.22), channel_id=1, source_target_pairs={{0,2},{1,3},{2,0},{3,1},{4,6},{5,7},{6,4},{7,5},{8,10},{9,11},{10,... | collective-permute-start | bytes 393224 | tf_op jit(solution)/shard_map/ppermute | solution.py:309
  52.4 5.6 %collective-permute-start.18 = (bf16[136,256]{1,0:T(8,128)(2,1)S(1)}, bf16[136,256]{1,0:T(8,128)(2,1)S(1)}, u32[]{:S(2)}, u32[]{:S(2)}) collective-permute-start(bf16[136,256]{1,0:T(8,128)(2,1)S(1)} %get-tuple-element.48), channel_id=1, source_target_pairs={{0,8},{1,9},{2,10},{3,11},{4,12},{5,13},{6,14},{7,15},{8,0},{9,1},... | collective-permute-start | bytes 208904 | tf_op jit(solution)/shard_map/ppermute | solution.py:306
  55.7 6.1 %collective-permute-start.19 = (bf16[136,256]{1,0:T(8,128)(2,1)S(1)}, bf16[136,256]{1,0:T(8,128)(2,1)S(1)}, u32[]{:S(2)}, u32[]{:S(2)}) collective-permute-start(bf16[136,256]{1,0:T(8,128)(2,1)S(1)} %get-tuple-element.49), channel_id=1, source_target_pairs={{0,12},{1,13},{2,14},{3,15},{4,8},{5,9},{6,10},{7,11},{8,4},{9,5},... | collective-permute-start | bytes 208904 | tf_op jit(solution)/shard_map/ppermute | solution.py:306
  58.0 6.3 %collective-permute-start.26 = (bf16[768,256]{1,0:T(8,128)(2,1)}, bf16[768,256]{1,0:T(8,128)(2,1)}, u32[]{:S(2)}, u32[]{:S(2)}) collective-permute-start(bf16[768,256]{1,0:T(8,128)(2,1)} %constant_dynamic-update-slice_fusion.6.refs_8_), channel_id=1, source_target_pairs={{0,1},{1,0},{2,3},{3,2},{4,5},{5,4},{6,7},{7,6},{8,9},{9,8},{10,11... | collective-permute-start | bytes 1179656 | tf_op jit(solution)/shard_map/ppermute | solution.py:309
  61.8 21.3 %collective-permute-start.12 = (bf16[768,384]{1,0:T(8,128)(2,1)S(1)}, bf16[768,384]{1,0:T(8,128)(2,1)S(1)}, u32[]{:S(2)}, u32[]{:S(2)}) collective-permute-start(bf16[768,384]{1,0:T(8,128)(2,1)S(1)} %constant_dynamic-update-slice_fusion.refs_8_), channel_id=1, source_target_pairs={{0,1},{1,0},{2,3},{3,2},{4,5},{5,4},{6,7},{7,6},{8,9},{9,8},{10,11... | collective-permute-start | bytes 1769480 | tf_op jit(solution)/shard_map/ppermute | solution.py:309
  61.8 21.3 %collective-permute-start.13 = (bf16[768,384]{1,0:T(8,128)(2,1)S(1)}, bf16[768,384]{1,0:T(8,128)(2,1)}, u32[]{:S(2)}, u32[]{:S(2)}) collective-permute-start(bf16[768,384]{1,0:T(8,128)(2,1)S(1)} %constant_dynamic-update-slice_fusion.3.refs_9_), channel_id=1, source_target_pairs={{0,1},{1,0},{2,3},{3,2},{4,5},{5,4},{6,7},{7,6},{8,9},{9,8},{10,11... | collective-permute-start | bytes 1769480 | tf_op jit(solution)/shard_map/ppermute | solution.py:309
  63.0 2.4 %collective-permute-start.27 = (bf16[768,256]{1,0:T(8,128)(2,1)}, bf16[768,256]{1,0:T(8,128)(2,1)}, u32[]{:S(2)}, u32[]{:S(2)}) collective-permute-start(bf16[768,256]{1,0:T(8,128)(2,1)} %constant_dynamic-update-slice_fusion.9.refs_9_), channel_id=1, source_target_pairs={{0,1},{1,0},{2,3},{3,2},{4,5},{5,4},{6,7},{7,6},{8,9},{9,8},{10,11... | collective-permute-start | bytes 1179656 | tf_op jit(solution)/shard_map/ppermute | solution.py:309
  63.1 3.8 %collective-permute-start.5 = (bf16[256,640]{1,0:T(8,128)(2,1)S(1)}, bf16[256,640]{1,0:T(8,128)(2,1)S(1)}, u32[]{:S(2)}, u32[]{:S(2)}) collective-permute-start(bf16[256,640]{1,0:T(8,128)(2,1)S(1)} %collective-permute-done.3.refs_5_), channel_id=1, source_target_pairs={{0,1},{1,0},{2,3},{3,2},{4,5},{5,4},{6,7},{7,6},{8,9},{9,8},{10,11... | collective-permute-start | bytes 983048 | tf_op jit(solution)/shard_map/ppermute | solution.py:309
  64.3 14.4 %collective-permute-start = (bf16[136,384]{1,0:T(8,128)(2,1)}, bf16[136,384]{1,0:T(8,128)(2,1)S(1)}, u32[]{:S(2)}, u32[]{:S(2)}) collective-permute-start(bf16[136,384]{1,0:T(8,128)(2,1)} %get-tuple-element.32), channel_id=1, source_target_pairs={{0,4},{1,5},{2,6},{3,7},{4,0},{5,1},{6,2},{7,3},{8,12},{9,13},{10,... | collective-permute-start | bytes 313352 | tf_op jit(solution)/shard_map/ppermute | solution.py:306
  65.4 15.4 %collective-permute-start.1 = (bf16[136,384]{1,0:T(8,128)(2,1)}, bf16[136,384]{1,0:T(8,128)(2,1)S(1)}, u32[]{:S(2)}, u32[]{:S(2)}) collective-permute-start(bf16[136,384]{1,0:T(8,128)(2,1)} %copy-done.12), channel_id=1, source_target_pairs={{0,8},{1,9},{2,10},{3,11},{4,12},{5,13},{6,14},{7,15},{8,0},{9,1},... | collective-permute-start | bytes 313352 | tf_op jit(solution)/shard_map/ppermute | solution.py:306
  67.0 13.8 %collective-permute-start.2 = (bf16[136,384]{1,0:T(8,128)(2,1)}, bf16[136,384]{1,0:T(8,128)(2,1)}, u32[]{:S(2)}, u32[]{:S(2)}) collective-permute-start(bf16[136,384]{1,0:T(8,128)(2,1)} %copy-done.11), channel_id=1, source_target_pairs={{0,12},{1,13},{2,14},{3,15},{4,8},{5,9},{6,10},{7,11},{8,4},{9,5},... | collective-permute-start | bytes 313352 | tf_op jit(solution)/shard_map/ppermute | solution.py:306
  78.7 16.1 %collective-permute-start.28 = (bf16[128,256]{1,0:T(8,128)(2,1)S(1)}, bf16[128,256]{1,0:T(8,128)(2,1)S(1)}, u32[]{:S(2)}, u32[]{:S(2)}) collective-permute-start(bf16[128,256]{1,0:T(8,128)(2,1)S(1)} %get-tuple-element.54), channel_id=1, source_target_pairs={{0,12},{1,13},{2,14},{3,15},{4,8},{5,9},{6,10},{7,11},{8,4},{9,5},... | collective-permute-start | bytes 196616 | tf_op jit(solution)/shard_map/ppermute | solution.py:306
  80.8 15.8 %collective-permute-start.29 = (bf16[128,256]{1,0:T(8,128)(2,1)S(1)}, bf16[128,256]{1,0:T(8,128)(2,1)S(1)}, u32[]{:S(2)}, u32[]{:S(2)}) collective-permute-start(bf16[128,256]{1,0:T(8,128)(2,1)S(1)} %get-tuple-element.55), channel_id=1, source_target_pairs={{0,8},{1,9},{2,10},{3,11},{4,12},{5,13},{6,14},{7,15},{8,0},{9,1},... | collective-permute-start | bytes 196616 | tf_op jit(solution)/shard_map/ppermute | solution.py:306
  80.8 15.8 %collective-permute-start.30 = (bf16[128,256]{1,0:T(8,128)(2,1)S(1)}, bf16[128,256]{1,0:T(8,128)(2,1)S(1)}, u32[]{:S(2)}, u32[]{:S(2)}) collective-permute-start(bf16[128,256]{1,0:T(8,128)(2,1)S(1)} %get-tuple-element.56), channel_id=1, source_target_pairs={{0,4},{1,5},{2,6},{3,7},{4,0},{5,1},{6,2},{7,3},{8,12},{9,13},{10,... | collective-permute-start | bytes 196616 | tf_op jit(solution)/shard_map/ppermute | solution.py:306
  91.9 4.7 %collective-permute-start.16 = (bf16[128,384]{1,0:T(8,128)(2,1)S(1)}, bf16[128,384]{1,0:T(8,128)(2,1)S(1)}, u32[]{:S(2)}, u32[]{:S(2)}) collective-permute-start(bf16[128,384]{1,0:T(8,128)(2,1)S(1)} %pad_maximum_fusion.3), channel_id=1, source_target_pairs={{0,4},{1,5},{2,6},{3,7},{4,0},{5,1},{6,2},{7,3},{8,12},{9,13},{10,... | collective-permute-start | bytes 294920 | tf_op jit(solution)/shard_map/ppermute | solution.py:306
  92.0 9.3 %collective-permute-start.15 = (bf16[128,384]{1,0:T(8,128)(2,1)S(1)}, bf16[128,384]{1,0:T(8,128)(2,1)S(1)}, u32[]{:S(2)}, u32[]{:S(2)}) collective-permute-start(bf16[128,384]{1,0:T(8,128)(2,1)S(1)} %pad_maximum_fusion.2), channel_id=1, source_target_pairs={{0,8},{1,9},{2,10},{3,11},{4,12},{5,13},{6,14},{7,15},{8,0},{9,1},... | collective-permute-start | bytes 294920 | tf_op jit(solution)/shard_map/ppermute | solution.py:306
  94.7 6.7 %collective-permute-start.14 = (bf16[128,384]{1,0:T(8,128)(2,1)S(1)}, bf16[128,384]{1,0:T(8,128)(2,1)S(1)}, u32[]{:S(2)}, u32[]{:S(2)}) collective-permute-start(bf16[128,384]{1,0:T(8,128)(2,1)S(1)} %pad_maximum_fusion.1), channel_id=1, source_target_pairs={{0,12},{1,13},{2,14},{3,15},{4,8},{5,9},{6,10},{7,11},{8,4},{9,5},... | collective-permute-start | bytes 294920 | tf_op jit(solution)/shard_map/ppermute | solution.py:306
  (14 other events, 39.0 us)
